TPU v7x, 32 devices: a whole 2x2x4 slice. The times are simulated.
32 devices in a mesh: dp: 8 (over z, x), seq: 4 (over y, core).
Axes of the slice: x: 2, y: 2, z: 4, core: 2. Of those that a mesh axis runs over, the one named last changes fastest.
Arguments:
- layer_in: bfloat16 [8192, 2048], P(('dp', 'seq')), may hold values from -6 to 6
- out_grad: bfloat16 [8192, 2048], P(('dp', 'seq')), may hold values from -6 to 6
- seq_start: int32 [8, 4], P('dp'), may hold values from 0 to 1, as said below
- norm1_gain: bfloat16 [2048], P(('dp', 'seq')), may hold values from 0.25 to 1.75
- norm1_shift: bfloat16 [2048], P(('dp', 'seq')), may hold values from -3 to 3
- proj_in: bfloat16 [2048, 12288], P(('dp', 'seq')), may hold values from -0.125 to 0.125
- proj_out: bfloat16 [4096, 2048], P(('dp', 'seq')), may hold values from -0.125 to 0.125
- norm2_gain: bfloat16 [2048], P(('dp', 'seq')), may hold values from 0.25 to 1.75
- norm2_shift: bfloat16 [2048], P(('dp', 'seq')), may hold values from -3 to 3
- ffn_up: bfloat16 [2048, 4096], P(('dp', 'seq')), may hold values from -0.125 to 0.125
- ffn_down: bfloat16 [4096, 2048], P(('dp', 'seq')), may hold values from -0.125 to 0.125
Outputs:
- layer_out: bfloat16 [8192, 2048], P(('dp', 'seq'))
- in_grad: bfloat16 [8192, 2048], P(('dp', 'seq'))
- norm1_gain_grad: float32 [2048], P(('dp', 'seq'))
- norm1_shift_grad: float32 [2048], P(('dp', 'seq'))
- proj_in_grad: float32 [2048, 12288], P(('dp', 'seq'))
- proj_out_grad: float32 [4096, 2048], P(('dp', 'seq'))
- norm2_gain_grad: float32 [2048], P(('dp', 'seq'))
- norm2_shift_grad: float32 [2048], P(('dp', 'seq'))
- ffn_up_grad: float32 [2048, 4096], P(('dp', 'seq'))
- ffn_down_grad: float32 [4096, 2048], P(('dp', 'seq'))
Inputs may be any that keep to these rules, and one draw needn't show every extreme that they name: `seq_start`: each group's first block is 1, and a 1 stands only at even block indices, so every sequence covers an even number of blocks of 256 tokens.
All inputs are finite; a program needn't handle non-finite values.
Results may differ from a plain program's by a relative error of at most 0.014.
The roundings to bfloat16 on the way count: a program that leaves them out, or rounds other values in their place, can miss the bound.
Values may be sent and summed in bfloat16 or wider, within the bound.
No kernel may reach another device: no remote copies, remote signals or barrier semaphores. Data moves between devices by JAX's collectives and lax.ppermute only.
A program may use at most 336 MiB of HBM per device.

v0:
```python
import jax
import jax.numpy as jnp
from jax import lax
from jax.sharding import PartitionSpec as P

D = 2048
HEADS = 8
VD = 4096
DK = 256
DV = 512


def carried_in(x, axis, combine, identity):
    count, place = (lax.axis_size(axis), lax.axis_index(axis))
    everything = jax.tree.map(lambda part: lax.all_gather(part, axis), x)
    start = jax.tree.map(
        lambda part, zero: jnp.broadcast_to(jnp.asarray(zero, part.dtype), part.shape), x, identity
    )

    def hop(k, before):
        reached = k < place
        new = combine(before, jax.tree.map(lambda part: part[k], everything))
        return jax.tree.map(lambda a, b: jnp.where(reached, a, b), new, before)

    return lax.fori_loop(0, count, hop, start)


def carried_in_2(x, axis, join, neutral):
    count = lax.axis_size(axis)
    place = lax.axis_index(axis)
    ahead = count - 1 - place
    gathered = jax.tree.map(
        lambda a, kind: lax.all_gather(a.astype(kind), axis), x, (jnp.bfloat16, jnp.bfloat16)
    )
    state = jax.tree.map(lambda a, e: jnp.zeros_like(a) + jnp.asarray(e, a.dtype), x, neutral)

    def one(hop, state):
        source = count - 1 - hop
        return join(
            state,
            jax.tree.map(
                lambda a, own: lax.dynamic_index_in_dim(a, source, 0, False).astype(own.dtype),
                gathered,
                x,
            ),
        )

    return lax.fori_loop(0, ahead, one, state)


def layer_norm(rows, row_gain, row_shift):
    average = jnp.mean(rows, axis=-1, keepdims=True)
    centred = rows - average
    spread = jnp.mean(centred * centred, axis=-1, keepdims=True)
    return centred * lax.rsqrt(spread + 1e-05) * row_gain + row_shift


def gate_norm(gate_pre, retained):
    average = jnp.mean(retained, axis=-1, keepdims=True)
    centred = retained - average
    spread = jnp.maximum(jnp.mean(centred * centred, axis=-1, keepdims=True), 0.25)
    normed = centred * lax.rsqrt(spread + 1e-05)
    swish = gate_pre * jax.nn.sigmoid(gate_pre)
    return swish * normed.reshape(gate_pre.shape)


def gelu_exact(values):
    return jax.nn.gelu(values, approximate=False)


def rotate(heads_in, cosine, sine):
    half_width = heads_in.shape[-1] // 2
    first = heads_in[..., :half_width]
    second = heads_in[..., half_width:]
    return jnp.concatenate(
        [first * cosine - second * sine, first * sine + second * cosine], axis=-1
    )


def rotary_tables(positions, head_width):
    half_width = head_width // 2
    factor = jnp.power(10000.0, -jnp.arange(half_width, dtype=jnp.float32) / (half_width - 1))
    angles = positions.astype(jnp.float32)[:, None] * factor[None, :]
    return (jnp.cos(angles)[:, None, :], jnp.sin(angles)[:, None, :])


def decay_logs(count):
    return jnp.log(1.0 - jnp.exp2(-5.0 - jnp.arange(count, dtype=jnp.float32)))


def causal_decay(steps_here, log_decay):
    distance = steps_here[:, None] - steps_here[None, :]
    lower = distance[None] >= 0.0
    safe_distance = jnp.where(lower, distance[None], 0.0)
    return jnp.where(lower, jnp.exp(safe_distance * log_decay[:, None, None]), 0.0)


def compose(earlier, later):
    return (later[0] * earlier[0], later[0][:, None, None] * earlier[1] + later[1])


def local(
    layer_in,
    out_grad,
    seq_start,
    norm1_gain,
    norm1_shift,
    proj_in,
    proj_out,
    norm2_gain,
    norm2_shift,
    ffn_up,
    ffn_down,
):
    f32 = jnp.float32
    bf16 = jnp.bfloat16
    tok_rows = layer_in.shape[0]
    attn_parts = (
        lax.all_gather(norm1_gain, ("dp", "seq"), axis=0, tiled=True),
        lax.all_gather(norm1_shift, ("dp", "seq"), axis=0, tiled=True),
        lax.all_gather(proj_in, ("dp", "seq"), axis=0, tiled=True),
        lax.all_gather(proj_out, ("dp", "seq"), axis=0, tiled=True),
    )
    rows_full = layer_in.astype(f32)
    normed_one, norm1_back = jax.vjp(
        layer_norm, rows_full, attn_parts[0].astype(f32), attn_parts[1].astype(f32)
    )
    hidden_one = normed_one.astype(bf16)
    projected = jnp.dot(hidden_one, attn_parts[2], preferred_element_type=f32)
    query_pre = projected[:, :D].reshape(tok_rows, HEADS, DK)
    key_pre = projected[:, D : 2 * D].reshape(tok_rows, HEADS, DK)
    value_all = projected[:, 2 * D : 2 * D + VD].astype(bf16).reshape(tok_rows, HEADS, DV)
    gate_pre = projected[:, 2 * D + VD :]
    block_index = lax.axis_index("seq")
    positions = block_index * tok_rows + jnp.arange(tok_rows, dtype=jnp.int32)
    cosine, sine = rotary_tables(positions, DK)
    key_scale = DK ** (-0.5)
    query_rot, query_back = jax.vjp(lambda heads_in: rotate(heads_in, cosine, sine), query_pre)
    key_rot, key_back = jax.vjp(
        lambda heads_in: rotate(heads_in, cosine, sine) * key_scale, key_pre
    )
    queries = query_rot.astype(bf16)
    keys = key_rot.astype(bf16)
    log_decay = decay_logs(HEADS)
    steps_here = jnp.arange(tok_rows, dtype=f32)
    decay_query = jnp.exp((steps_here + 1.0)[:, None] * log_decay[None, :])
    decay_key = jnp.exp((tok_rows - 1.0 - steps_here)[:, None] * log_decay[None, :])
    decay_mask = causal_decay(steps_here, log_decay)
    query_decay = (queries.astype(f32) * decay_query[:, :, None]).astype(bf16)
    key_decay = (keys.astype(f32) * decay_key[:, :, None]).astype(bf16)
    raw_scores = jnp.einsum("ihd,jhd->hij", queries, keys, preferred_element_type=f32)
    scores = (raw_scores * decay_mask).astype(bf16)
    intra = jnp.einsum("hij,jhe->ihe", scores, value_all, preferred_element_type=f32)
    local_state = jnp.einsum("jhd,jhe->hde", key_decay, value_all, preferred_element_type=f32)
    block_ids = jnp.arange(seq_start.shape[1], dtype=jnp.int32)
    start_here = jnp.sum(jnp.where(block_ids == block_index, seq_start[0], 0)).astype(f32)
    keep_state = 1.0 - start_here
    block_decay = jnp.exp(tok_rows * log_decay) * keep_state
    identity = (jnp.ones((HEADS,), f32), jnp.zeros((HEADS, DK, DV), f32))
    prefix = carried_in((block_decay, local_state), "seq", compose, identity)
    state_in = (keep_state * prefix[1]).astype(bf16)
    inter = jnp.einsum("ihd,hde->ihe", query_decay, state_in, preferred_element_type=f32)
    retained = intra + inter
    gated, gate_back = jax.vjp(gate_norm, gate_pre, retained)
    mixed = gated.astype(bf16)
    middle = rows_full + jnp.dot(mixed, attn_parts[3], preferred_element_type=f32)
    ffn_parts = (
        lax.all_gather(norm2_gain, ("dp", "seq"), axis=0, tiled=True),
        lax.all_gather(norm2_shift, ("dp", "seq"), axis=0, tiled=True),
        lax.all_gather(ffn_up, ("dp", "seq"), axis=0, tiled=True),
        lax.all_gather(ffn_down, ("dp", "seq"), axis=0, tiled=True),
    )
    normed_two, norm2_back = jax.vjp(
        layer_norm, middle, ffn_parts[0].astype(f32), ffn_parts[1].astype(f32)
    )
    hidden_two = normed_two.astype(bf16)
    up_pre = jnp.dot(hidden_two, ffn_parts[2], preferred_element_type=f32)
    active_full, gelu_back = jax.vjp(gelu_exact, up_pre)
    active = active_full.astype(bf16)
    layer_out = (middle + jnp.dot(active, ffn_parts[3], preferred_element_type=f32)).astype(bf16)
    ffn_mats = (
        lax.all_gather(ffn_up, ("dp", "seq"), axis=0, tiled=True),
        lax.all_gather(ffn_down, ("dp", "seq"), axis=0, tiled=True),
    )
    down_term = jnp.einsum("tf,td->fd", active, out_grad, preferred_element_type=f32)
    grad_active = jnp.einsum("td,fd->tf", out_grad, ffn_mats[1], preferred_element_type=f32)
    grad_up = gelu_back(grad_active)[0].astype(bf16)
    up_term = jnp.einsum("tc,tf->cf", hidden_two, grad_up, preferred_element_type=f32)
    grad_hidden_two = jnp.einsum("tf,cf->tc", grad_up, ffn_mats[0], preferred_element_type=f32)
    grad_mid_part, gain_two_grad, shift_two_grad = norm2_back(grad_hidden_two)
    grad_middle = out_grad.astype(f32) + grad_mid_part
    ffn_sums = (
        lax.psum_scatter(gain_two_grad, ("dp", "seq"), scatter_dimension=0, tiled=True),
        lax.psum_scatter(shift_two_grad, ("dp", "seq"), scatter_dimension=0, tiled=True),
        lax.psum_scatter(up_term, ("dp", "seq"), scatter_dimension=0, tiled=True),
        lax.psum_scatter(down_term, ("dp", "seq"), scatter_dimension=0, tiled=True),
    )
    attn_mats = (
        lax.all_gather(proj_in, ("dp", "seq"), axis=0, tiled=True),
        lax.all_gather(proj_out, ("dp", "seq"), axis=0, tiled=True),
    )
    grad_attn = grad_middle.astype(bf16)
    out_term = jnp.einsum("tv,td->vd", mixed, grad_attn, preferred_element_type=f32)
    grad_mixed = jnp.einsum("td,vd->tv", grad_attn, attn_mats[1], preferred_element_type=f32)
    grad_gate_full, grad_ret_full = gate_back(grad_mixed)
    grad_gate = grad_gate_full.astype(bf16)
    grad_ret = grad_ret_full.astype(bf16)
    grad_qdecay = jnp.einsum("ihe,hde->ihd", grad_ret, state_in, preferred_element_type=f32)
    state_grad_here = jnp.einsum("ihd,ihe->hde", query_decay, grad_ret, preferred_element_type=f32)
    grad_value = jnp.einsum("hij,ihe->jhe", scores, grad_ret, preferred_element_type=f32)
    grad_scores = jnp.einsum("ihe,jhe->hij", grad_ret, value_all, preferred_element_type=f32)
    grad_raw = (grad_scores * decay_mask).astype(bf16)
    grad_query = (
        jnp.einsum("hij,jhd->ihd", grad_raw, keys, preferred_element_type=f32)
        + grad_qdecay * decay_query[:, :, None]
    )
    grad_key = jnp.einsum("hij,ihd->jhd", grad_raw, queries, preferred_element_type=f32)
    later = carried_in_2((block_decay, keep_state * state_grad_here), "seq", compose, identity)
    grad_local = later[1].astype(bf16)
    grad_kdecay = jnp.einsum("jhe,hde->jhd", value_all, grad_local, preferred_element_type=f32)
    grad_value = grad_value + jnp.einsum(
        "jhd,hde->jhe", key_decay, grad_local, preferred_element_type=f32
    )
    grad_key = grad_key + grad_kdecay * decay_key[:, :, None]
    grad_qpre = query_back(grad_query)[0].astype(bf16).reshape(tok_rows, D)
    grad_kpre = key_back(grad_key)[0].astype(bf16).reshape(tok_rows, D)
    grad_vpre = grad_value.astype(bf16).reshape(tok_rows, VD)
    grad_projected = jnp.concatenate([grad_qpre, grad_kpre, grad_vpre, grad_gate], axis=1)
    in_term = jnp.einsum("tc,tp->cp", hidden_one, grad_projected, preferred_element_type=f32)
    grad_hidden_one = jnp.einsum(
        "tp,cp->tc", grad_projected, attn_mats[0], preferred_element_type=f32
    )
    grad_in_part, gain_one_grad, shift_one_grad = norm1_back(grad_hidden_one)
    attn_sums = (
        lax.psum_scatter(gain_one_grad, ("dp", "seq"), scatter_dimension=0, tiled=True),
        lax.psum_scatter(shift_one_grad, ("dp", "seq"), scatter_dimension=0, tiled=True),
        lax.psum_scatter(in_term, ("dp", "seq"), scatter_dimension=0, tiled=True),
        lax.psum_scatter(out_term, ("dp", "seq"), scatter_dimension=0, tiled=True),
    )
    in_grad = (grad_middle + grad_in_part).astype(bf16)
    return (
        layer_out,
        in_grad,
        attn_sums[0],
        attn_sums[1],
        attn_sums[2],
        attn_sums[3],
        ffn_sums[0],
        ffn_sums[1],
        ffn_sums[2],
        ffn_sums[3],
    )


def solution(mesh):
    in_specs = (
        P(("dp", "seq"), None),
        P(("dp", "seq"), None),
        P("dp", None),
        P(("dp", "seq")),
        P(("dp", "seq")),
        P(("dp", "seq"), None),
        P(("dp", "seq"), None),
        P(("dp", "seq")),
        P(("dp", "seq")),
        P(("dp", "seq"), None),
        P(("dp", "seq"), None),
    )
    out_specs = (
        P(("dp", "seq"), None),
        P(("dp", "seq"), None),
        P(("dp", "seq")),
        P(("dp", "seq")),
        P(("dp", "seq"), None),
        P(("dp", "seq"), None),
        P(("dp", "seq")),
        P(("dp", "seq")),
        P(("dp", "seq"), None),
        P(("dp", "seq"), None),
    )
    return jax.shard_map(local, mesh=mesh, in_specs=in_specs, out_specs=out_specs, check_vma=False)
```

profile of v0, /device:TPU:0, one launch (start us, length us, event | category | flops | bytes accessed | tf_op | source)
XLA Modules:
  0.0 2830.8 jit_solution(17019214859224508175)
XLA Ops:
  11.4 45.0 %all-reduce.13 = (bf16[2048]{0:T(1024)(128)(2,1)S(1)}, bf16[2048]{0:T(1024)(128)(2,1)S(1)}, bf16[2048]{0:T(1024)(128)(2,1)S(1)}, bf16[2048]{0:T(1024)(128)(2,1)S(1)}) all-reduce(bf16[2048]{0:T(1024)(128)(2,1)S(1)} %dynamic-update-slice.1, bf16[2048]{0:T(1024)(128)(2,1)S(1)} %dynamic-update-slice, ...), channel_id=1, replica_groups=mesh['dp'=8,'seq'=4] {'dp','seq'}, use_global_device_ids=true, to_apply=%add.5 | all-reduce | flops 8192 | bytes 32768
  60.8 229.3 %all-gather.11.cloned.1.call-done = bf16[2048,12288]{1,0:T(8,128)(2,1)} async-done(((bf16[64,12288]{1,0:T(8,128)(2,1)}), bf16[2048,12288]{1,0:T(8,128)(2,1)}) %all-gather.11.cloned.1.call-update) | async-done | bytes 50331664 | tf_op jit(solution)/shard_map/all_gather | solution.py:121
  290.1 26.4 fusion.65
  325.5 3.1 fusion.30
  331.9 5.3 all-gather.2
  341.2 2.9 fusion.24
  344.1 88.8 %all-gather.19.cloned.1.call-done = f32[32,256,512]{2,1,0:T(8,128)} async-done(((f32[8,256,512]{2,1,0:T(8,128)}), f32[32,256,512]{2,1,0:T(8,128)}) %all-gather.19.cloned.1.call-update) | async-done | bytes 16777232 | tf_op jit(solution)/shard_map/all_gather | solution.py:15
  432.9 25.2 while.29
  432.9 5.4 fusion.109
  438.3 6.6 fusion.109
  444.8 6.7 fusion.109
  451.5 6.6 fusion.109
  458.1 4.7 bitcast_reduce_fusion
  463.3 3.0 fusion.11
  466.2 5.6 copy.115
  471.8 6.1 multiply_convert_fusion.2
  477.9 72.7 %all-gather.13.cloned.1.call-done = bf16[4096,2048]{1,0:T(8,128)(2,1)} async-done(((bf16[128,2048]{1,0:T(8,128)(2,1)}), bf16[4096,2048]{1,0:T(8,128)(2,1)}) %all-gather.13.cloned.1.call-update) | async-done | bytes 16777232 | tf_op jit(solution)/shard_map/all_gather | solution.py:122
  550.6 8.8 fusion.76
  559.9 106.6 %all-gather.15.cloned.1.call-done = bf16[2048,4096]{1,0:T(8,128)(2,1)} async-done(((bf16[64,4096]{1,0:T(8,128)(2,1)}), bf16[2048,4096]{1,0:T(8,128)(2,1)}) %all-gather.15.cloned.1.call-update) | async-done | bytes 16777232 | tf_op jit(solution)/shard_map/all_gather | solution.py:170
  666.4 10.4 fusion.69
  676.8 105.4 %all-gather.17.cloned.1.call-done = bf16[4096,2048]{1,0:T(8,128)(2,1)} async-done(((bf16[128,2048]{1,0:T(8,128)(2,1)}), bf16[4096,2048]{1,0:T(8,128)(2,1)}) %all-gather.17.cloned.1.call-update) | async-done | bytes 16777232 | tf_op jit(solution)/shard_map/all_gather | solution.py:171
  782.2 20.1 add_convert_fusion.2
  802.4 13.3 multiply_reduce_fusion.2
  820.8 12.2 fusion.53
  833.0 5.8 copy.117
  838.8 4.2 multiply_reduce_fusion
  850.7 17.2 fusion.78
  868.0 15.1 fusion.68
  883.1 4.3 multiply_convert_fusion.1
  888.9 13.3 fusion.79
  902.3 5.6 all-gather.3
  907.9 2.8 multiply_convert_fusion.4
  920.9 17.5 while.28
  920.9 5.8 convert_add_fusion.3
  926.7 5.9 convert_add_fusion.3
  932.6 5.8 convert_add_fusion.3
  938.4 6.1 add_convert_fusion
  944.5 4.1 copy.116
  948.6 3.9 fusion.34
  955.7 38.0 %fusion.45 = f32[2048,12288]{1,0:T(8,128)} fusion(bf16[256,4096]{1,0:T(8,128)(2,1)} %get-tuple-element.248, bf16[256,4096]{1,0:T(8,128)(2,1)S(1)} %copy-done.21, bf16[256,2048]{1,0:T(8,128)(2,1)} %bitcast.133, bf16[256,2048]{1,0:T(8,128)(2,1)} %bitcast.135, bf16[256,2048]{1,0:T(8,128)(2,1)S(1)} %copy-done.7, f32[2048]{0:T(1024)S(1)} %copy-done.39, ...), kind=kOutput, calls=%fused_computation.93 | convolution fusion | flops 12913213440 | bytes 108021760 | tf_op jit(solution)/shard_map/tc,tp->cp/dot_general | solution.py:229
  995.3 12.1 fusion.16
  1007.4 24.5 fusion.70
  1034.6 43.3 %all-reduce.12 = (f32[2048]{0:T(1024)S(1)}, f32[2048]{0:T(1024)S(1)}, f32[2048]{0:T(1024)S(1)}, f32[2048]{0:T(1024)S(1)}) all-reduce(f32[2048]{0:T(1024)S(1)} %get-tuple-element.210, f32[2048]{0:T(1024)S(1)} %get-tuple-element.213, f32[2048]{0:T(1024)S(1)} %copy-done.54, ...), channel_id=4, replica_groups=mesh['dp'=8,'seq'=4] {'dp','seq'}, use_global_device_ids=true, to_apply=%region_18.19.clone | all-reduce | flops 8192 | bytes 65536
  1080.2 3.8 add_convert_fusion.3
  1084.0 181.5 %reduce-scatter.7.cloned.1.call-done = f32[128,2048]{1,0:T(8,128)} async-done(((f32[4096,2048]{1,0:T(8,128)}), f32[128,2048]{1,0:T(8,128)}) %reduce-scatter.7.cloned.1.call-update) | async-done | bytes 1048592 | tf_op jit(solution)/shard_map/reduce_scatter | solution.py:238
  1265.6 360.5 %reduce-scatter.9.cloned.1.call-done = f32[64,4096]{1,0:T(8,128)} async-done(((f32[2048,4096]{1,0:T(8,128)}), f32[64,4096]{1,0:T(8,128)}) %reduce-scatter.9.cloned.1.call-update) | async-done | bytes 1048592 | tf_op jit(solution)/shard_map/reduce_scatter | solution.py:195
  1626.1 360.5 %reduce-scatter.11.cloned.1.call-done = f32[128,2048]{1,0:T(8,128)} async-done(((f32[4096,2048]{1,0:T(8,128)}), f32[128,2048]{1,0:T(8,128)}) %reduce-scatter.11.cloned.1.call-update) | async-done | bytes 1048592 | tf_op jit(solution)/shard_map/reduce_scatter | solution.py:196
  1986.6 837.2 %reduce-scatter.5.cloned.1.call-done = f32[64,12288]{1,0:T(8,128)} async-done(((f32[2048,12288]{1,0:T(8,128)}), f32[64,12288]{1,0:T(8,128)}) %reduce-scatter.5.cloned.1.call-update) | async-done | bytes 3145744 | tf_op jit(solution)/shard_map/reduce_scatter | solution.py:237
  (215 shorter events, 58.9 us)
Async XLA Ops:
  7.2 283.0 %all-gather.11.cloned.1.call-start = ((), (), s32[]{:S(2)}) async-start(), calls=%async_computation.4 | async-start | bytes 51904512 | tf_op jit(solution)/shard_map/all_gather | solution.py:121
  7.9 425.0 %all-gather.19.cloned.1.call-start = ((), (), s32[]{:S(2)}) async-start(), calls=%async_computation.12 | async-start | bytes 20971520 | tf_op jit(solution)/shard_map/all_gather | solution.py:15
  56.4 260.1 %copy-start.38 = (f32[2048]{0:T(1024)}, f32[2048]{0:T(1024)S(1)}, u32[]{:S(2)}) copy-start(f32[2048]{0:T(1024)S(1)} %convert_element_type.138) | copy-start | bytes 24580
  56.4 260.1 %copy-start.36 = (f32[2048]{0:T(1024)}, f32[2048]{0:T(1024)S(1)}, u32[]{:S(2)}) copy-start(f32[2048]{0:T(1024)S(1)} %convert_element_type.137) | copy-start | bytes 24580
  56.5 280.9 %copy-start.56 = (f32[8]{0:T(128)}, f32[8]{0:T(128)S(1)}, u32[]{:S(2)}) copy-start(f32[8]{0:T(128)S(1)} %subtract_log_fusion) | copy-start | bytes 100
  57.9 258.6 %copy-start.40 = (f32[256]{0:T(256)}, f32[256]{0:T(256)S(1)}, u32[]{:S(2)}) copy-start(f32[256]{0:T(256)S(1)} %broadcast_multiply_fusion.2) | copy-start | bytes 3076
  59.6 256.9 %copy-start.42 = (f32[256]{0:T(256)}, f32[256]{0:T(256)S(1)}, u32[]{:S(2)}) copy-start(f32[256]{0:T(256)S(1)} %fusion.57) | copy-start | bytes 3076
  60.3 265.2 %copy-start.46 = (f32[256,8]{0,1:T(8,128)}, f32[256,8]{0,1:T(8,128)S(1)}, u32[]{:S(2)}) copy-start(f32[256,8]{0,1:T(8,128)S(1)} %get-tuple-element.269) | copy-start | bytes 24580
  60.8 262.8 %copy-start.32 = (f32[256,128]{1,0:T(8,128)}, f32[256,128]{1,0:T(8,128)S(1)}, u32[]{:S(2)}) copy-start(f32[256,128]{1,0:T(8,128)S(1)} %get-tuple-element.267) | copy-start | bytes 393220
  60.8 262.8 %copy-start.34 = (f32[256,128]{1,0:T(8,128)}, f32[256,128]{1,0:T(8,128)S(1)}, u32[]{:S(2)}) copy-start(f32[256,128]{1,0:T(8,128)S(1)} %get-tuple-element.268) | copy-start | bytes 393220
  321.5 18.7 copy-start.4
  325.5 11.9 copy-start.15
  328.6 222.0 %all-gather.13.cloned.1.call-start = ((), (), s32[]{:S(2)}) async-start(), calls=%async_computation.5 | async-start | bytes 17301504 | tf_op jit(solution)/shard_map/all_gather | solution.py:122
  329.3 337.1 %all-gather.15.cloned.1.call-start = ((), (), s32[]{:S(2)}) async-start(), calls=%async_computation.6 | async-start | bytes 17301504 | tf_op jit(solution)/shard_map/all_gather | solution.py:170
  329.9 452.3 %all-gather.17.cloned.1.call-start = ((), (), s32[]{:S(2)}) async-start(), calls=%async_computation.7 | async-start | bytes 17301504 | tf_op jit(solution)/shard_map/all_gather | solution.py:171
  330.5 588.0 %all-gather.21.cloned.1.call-start = ((), (), s32[]{:S(2)}) async-start(), calls=%async_computation.13 | async-start | bytes 10485760 | tf_op jit(solution)/shard_map/all_gather | solution.py:33
  337.3 6.8 copy-start.48
  432.9 25.2 copy-start.23
  432.9 25.2 copy-start.26
  471.8 78.8 %copy-start.6 = (bf16[256,2048]{1,0:T(8,128)(2,1)S(1)}, bf16[256,2048]{1,0:T(8,128)(2,1)}, u32[]{:S(2)}) copy-start(bf16[256,2048]{1,0:T(8,128)(2,1)} %param.15) | copy-start | bytes 3145732
  559.5 308.5 %copy-start.8 = (f32[256,2048]{1,0:T(8,128)}, f32[256,2048]{1,0:T(8,128)S(1)}, u32[]{:S(2)}) copy-start(f32[256,2048]{1,0:T(8,128)S(1)} %get-tuple-element.274) | copy-start | bytes 6291460
  559.9 222.4 %copy-start.18 = (bf16[256,2048]{1,0:T(8,128)(2,1)S(1)}, bf16[256,2048]{1,0:T(8,128)(2,1)}, u32[]{:S(2)}) copy-start(bf16[256,2048]{1,0:T(8,128)(2,1)} %param.16) | copy-start | bytes 3145732
  815.8 5.0 copy-start.14
  818.1 14.8 copy-start.50
  838.8 4.6 copy-start.2
  838.8 5.9 copy-start.3
  850.6 415.0 %reduce-scatter.7.cloned.1.call-start = ((), (), s32[]{:S(2)}) async-start(), calls=%async_computation.9 | async-start | bytes 34603008 | tf_op jit(solution)/shard_map/reduce_scatter | solution.py:238
  867.9 758.2 %reduce-scatter.9.cloned.1.call-start = ((), (), s32[]{:S(2)}) async-start(), calls=%async_computation.10 | async-start | bytes 34603008 | tf_op jit(solution)/shard_map/reduce_scatter | solution.py:195
  883.0 1103.5 %reduce-scatter.11.cloned.1.call-start = ((), (), s32[]{:S(2)}) async-start(), calls=%async_computation.11 | async-start | bytes 34603008 | tf_op jit(solution)/shard_map/reduce_scatter | solution.py:196
  883.1 5.8 copy-start.20
  902.2 5.7 copy-start.5
  902.2 5.7 copy-start.45
  902.2 5.7 copy-start.49
  902.2 5.7 copy-start.57
  902.2 8.5 copy-start.25
  902.2 8.5 copy-start.28
  902.2 1921.5 %reduce-scatter.5.cloned.1.call-start = ((), (), s32[]{:S(2)}) async-start(), calls=%async_computation.8 | async-start | bytes 103809024 | tf_op jit(solution)/shard_map/reduce_scatter | solution.py:237
  907.9 4.8 copy-start
  907.9 4.8 copy-start.11
  920.9 17.5 copy-start.47
  948.6 3.9 copy-start.22
  948.6 3.9 copy-start.33
  948.6 3.9 copy-start.35
  1007.4 24.5 copy-start.53
  1007.4 27.2 copy-start.54
  1007.4 27.2 copy-start.55
  1007.4 72.8 %copy-start.51 = (f32[256]{0:T(256)S(1)}, f32[256]{0:T(256)}, u32[]{:S(2)}) copy-start(f32[256]{0:T(256)} %copy-done.50) | copy-start | bytes 3076
  1031.9 48.3 %copy-start.13 = (f32[256,2048]{1,0:T(8,128)S(1)}, f32[256,2048]{1,0:T(8,128)}, u32[]{:S(2)}) copy-start(f32[256,2048]{1,0:T(8,128)} %copy-done.12) | copy-start | bytes 6291460
  (21 other events, 41.8 us)
Sparse Core Ops, SparseCore 0:
  10.9 279.1 all-gather.10
  328.7 104.0 all-gather.18
  435.7 114.8 all-gather.12
  553.4 113.0 all-gather.14
  669.2 113.0 all-gather.16
  850.7 56.4 all-gather.20
  910.1 355.4 reduce-scatter.6
  1268.4 357.5 reduce-scatter.8
  1628.9 357.5 reduce-scatter.10
  1993.4 830.2 reduce-scatter.4
where the time goes:
time: 2840 us; the launch traced here: 2830 us
  waiting for transfers between devices  2350 us (83%)
  matrix products  247 us (9%)
  blocking collectives  99.2 us (3%)
  other arithmetic  80.4 us (3%)
  local copies, waits for them, and re-layouts  43 us (2%)
    reduce_scatter x1, waiting for transfers between devices, local(): lax.psum_scatter(in_term, ('dp', 'seq'), scatter_dimension=0, tiled=True)  837 us
    reduce_scatter x1, waiting for transfers between devices, local(): lax.psum_scatter(up_term, ('dp', 'seq'), scatter_dimension=0, tiled=True)  361 us
    reduce_scatter x1, waiting for transfers between devices, local(): lax.psum_scatter(down_term, ('dp', 'seq'), scatter_dimension=0, tiled=True)  360 us
    all_gather x1, waiting for transfers between devices, local(): lax.all_gather(proj_in, ('dp', 'seq'), axis=0, tiled=True)  229 us
    reduce_scatter x1, waiting for transfers between devices, local(): lax.psum_scatter(out_term, ('dp', 'seq'), scatter_dimension=0, tiled=True)  182 us
    all_gather x1, waiting for transfers between devices, local(): lax.all_gather(ffn_up, ('dp', 'seq'), axis=0, tiled=True)  107 us
    all_gather x1, waiting for transfers between devices, local(): lax.all_gather(ffn_down, ('dp', 'seq'), axis=0, tiled=True)  105 us
    all_gather x1, waiting for transfers between devices, carried_in(): everything = jax.tree.map(lambda part: lax.all_gather(part, axis), x)  88.8 us
  transfers between devices with their start and end apart: 10, of which 9 were waited for; matrix products, arithmetic and copies ran while one was open for 9% of the time, Pallas kernels for 0%

commit v1 on v0

v1 whole, which is shorter than its diff:
```python
import jax
import jax.numpy as jnp
from jax import lax
from jax.sharding import PartitionSpec as P

D = 2048
HEADS = 8
VD = 4096
DK = 256
DV = 512
BOTH = ("dp", "seq")
f32 = jnp.float32
bf16 = jnp.bfloat16


def layer_norm(rows, row_gain, row_shift):
    average = jnp.mean(rows, axis=-1, keepdims=True)
    centred = rows - average
    spread = jnp.mean(centred * centred, axis=-1, keepdims=True)
    return centred * lax.rsqrt(spread + 1e-05) * row_gain + row_shift


def gate_norm(gate_pre, retained):
    average = jnp.mean(retained, axis=-1, keepdims=True)
    centred = retained - average
    spread = jnp.maximum(jnp.mean(centred * centred, axis=-1, keepdims=True), 0.25)
    normed = centred * lax.rsqrt(spread + 1e-05)
    swish = gate_pre * jax.nn.sigmoid(gate_pre)
    return swish * normed


def gelu_exact(values):
    return jax.nn.gelu(values, approximate=False)


def rotate(heads_in, cosine, sine):
    half_width = heads_in.shape[-1] // 2
    first = heads_in[..., :half_width]
    second = heads_in[..., half_width:]
    return jnp.concatenate(
        [first * cosine - second * sine, first * sine + second * cosine], axis=-1
    )


def dot(a, b, dims):
    return lax.dot_general(a, b, (dims, ((), ())), preferred_element_type=f32)


def seq_bits(size):
    return [1 << b for b in range(size.bit_length() - 1)]


def swap_seq(x, bit):
    size = lax.axis_size("seq")
    return lax.ppermute(x, "seq", [(i, i ^ bit) for i in range(size)])


def gather_seq(x):
    size, me = lax.axis_size("seq"), lax.axis_index("seq")
    held = x[None]
    for bit in reversed(seq_bits(size)):
        other = swap_seq(held, bit)
        upper = (me & bit) != 0
        held = jnp.where(upper, jnp.stack([other, held]), jnp.stack([held, other]))
        held = held.reshape((-1,) + x.shape) if bit == size // 2 else held
        if bit != size // 2:
            held = jnp.swapaxes(held, 0, 1).reshape((-1,) + x.shape)
    return held


def scatter_seq(x):
    size, me = lax.axis_size("seq"), lax.axis_index("seq")
    held = x
    for bit in seq_bits(size):
        pairs = held.reshape((held.shape[0] // 2, 2) + held.shape[1:])
        mine = jnp.where((me & bit) != 0, 1, 0)
        keep = lax.dynamic_index_in_dim(pairs, mine, 1, False)
        give = lax.dynamic_index_in_dim(pairs, 1 - mine, 1, False)
        held = keep.astype(f32) + swap_seq(give.astype(bf16), bit).astype(f32)
    return held[0]


def exchange_seq(x):
    return lax.all_to_all(x, "seq", 0, 0)


def gather_dp(x):
    return lax.all_gather(x, "dp", axis=0, tiled=True)


def scatter_dp(x):
    return lax.psum_scatter(x.astype(bf16), "dp", scatter_dimension=0, tiled=True)


def local(
    layer_in,
    out_grad,
    seq_start,
    norm1_gain,
    norm1_shift,
    proj_in,
    proj_out,
    norm2_gain,
    norm2_shift,
    ffn_up,
    ffn_down,
):
    S, G = lax.axis_size("seq"), lax.axis_size("dp")
    me = lax.axis_index("seq")
    T = layer_in.shape[0]
    TG = S * T
    H = HEADS // S
    QW, VW = H * DK, H * DV
    FR = ffn_down.shape[0]
    FW = G * FR

    norms = lax.all_gather(
        jnp.stack([norm1_gain, norm1_shift, norm2_gain, norm2_shift]), BOTH, axis=1, tiled=True
    ).astype(f32)
    gain_one, shift_one, gain_two, shift_two = norms

    rows_in = proj_in.shape[0]
    pieces = []
    start = 0
    for width in (QW, QW, VW, VW):
        part = proj_in[:, start : start + S * width]
        pieces.append(part.reshape(rows_in, S, width))
        start += S * width
    w_in = jnp.concatenate(pieces, axis=2).transpose(1, 0, 2)
    w_in = exchange_seq(w_in).reshape(S * rows_in, 2 * QW + 2 * VW)
    w_in = gather_dp(w_in)
    w_out = lax.ppermute(
        proj_out, BOTH, [(j * G + t, t * S + j) for j in range(S) for t in range(G)]
    )
    w_out = gather_dp(w_out)
    rows_up = ffn_up.shape[0]
    w_up = ffn_up.reshape(rows_up, G, S, FR).transpose(2, 0, 1, 3).reshape(S, rows_up, FW)
    w_up = gather_dp(exchange_seq(w_up).reshape(S * rows_up, FW))
    w_down = gather_dp(ffn_down)

    rows_full = layer_in.astype(f32)
    normed_one, norm1_back = jax.vjp(layer_norm, rows_full, gain_one, shift_one)
    hidden_one = gather_seq(normed_one.astype(bf16)).reshape(TG, D)
    cot = gather_seq(out_grad).reshape(TG, D)

    projected = dot(hidden_one, w_in, ((1,), (0,)))
    q_pre = projected[:, :QW].reshape(S, T, H, DK)
    k_pre = projected[:, QW : 2 * QW].reshape(S, T, H, DK)
    values = projected[:, 2 * QW : 2 * QW + VW].astype(bf16).reshape(S, T, H, DV)
    gate_pre = projected[:, 2 * QW + VW :].reshape(S, T, H, DV)

    half = DK // 2
    factor = jnp.power(10000.0, -jnp.arange(half, dtype=f32) / (half - 1))
    angles = jnp.arange(TG, dtype=f32)[:, None] * factor[None, :]
    cosine = jnp.cos(angles).reshape(S, T, 1, half)
    sine = jnp.sin(angles).reshape(S, T, 1, half)
    key_scale = DK ** (-0.5)
    queries = rotate(q_pre, cosine, sine).astype(bf16)
    keys = (rotate(k_pre, cosine, sine) * key_scale).astype(bf16)

    log_all = jnp.log(1.0 - jnp.exp2(-5.0 - jnp.arange(HEADS, dtype=f32)))
    log_decay = lax.dynamic_slice_in_dim(log_all, me * H, H)
    steps = jnp.arange(T, dtype=f32)
    decay_query = jnp.exp((steps + 1.0)[:, None] * log_decay[None, :])
    decay_key = jnp.exp((T - 1.0 - steps)[:, None] * log_decay[None, :])
    distance = steps[:, None] - steps[None, :]
    lower = distance[None] >= 0.0
    safe = jnp.where(lower, distance[None], 0.0)
    mask = jnp.where(lower, jnp.exp(safe * log_decay[:, None, None]), 0.0)
    block_decay = jnp.exp(T * log_decay)[:, None, None]
    keep = 1.0 - seq_start[0].astype(f32)

    query_decay = (queries.astype(f32) * decay_query[None, :, :, None]).astype(bf16)
    key_decay = (keys.astype(f32) * decay_key[None, :, :, None]).astype(bf16)

    def ein(spec, a, b):
        return jnp.einsum(spec, a, b, preferred_element_type=f32)

    raw = ein("bihd,bjhd->bhij", queries, keys)
    scores = (raw * mask[None]).astype(bf16)
    local_state = ein("bjhd,bjhe->bhde", key_decay, values)
    carry = jnp.zeros_like(local_state[0])
    states = []
    for b in range(S):
        state = keep[b] * carry
        states.append(state.astype(bf16))
        carry = block_decay * state + local_state[b]
    state_in = jnp.stack(states)
    retained = ein("bhij,bjhe->bihe", scores, values) + ein("bihd,bhde->bihe", query_decay, state_in)
    gated, gate_back = jax.vjp(gate_norm, gate_pre, retained)
    mixed = gated.astype(bf16).reshape(TG, VW)

    attn = scatter_seq(dot(mixed, w_out, ((1,), (0,))).reshape(S, T, D))
    middle = rows_full + attn
    normed_two, norm2_back = jax.vjp(layer_norm, middle, gain_two, shift_two)
    hidden_two = gather_seq(normed_two.astype(bf16)).reshape(TG, D)
    up_pre = dot(hidden_two, w_up, ((1,), (0,)))
    active_full, gelu_back = jax.vjp(gelu_exact, up_pre)
    active = active_full.astype(bf16)
    down = scatter_seq(dot(active, w_down, ((1,), (0,))).reshape(S, T, D))
    layer_out = (middle + down).astype(bf16)

    down_grad = scatter_dp(dot(active, cot, ((0,), (0,)))).astype(f32)
    grad_active = dot(cot, w_down, ((1,), (1,)))
    grad_up = gelu_back(grad_active)[0].astype(bf16)
    up_grad = scatter_dp(dot(hidden_two, grad_up, ((0,), (0,))))
    up_grad = exchange_seq(up_grad.reshape(S, rows_up, FW)).reshape(S, rows_up, G, FR)
    up_grad = up_grad.transpose(1, 2, 0, 3).reshape(rows_up, G * S * FR).astype(f32)
    grad_hidden_two = scatter_seq(dot(grad_up, w_up, ((1,), (1,))).reshape(S, T, D))
    grad_mid_part, gain_two_grad, shift_two_grad = norm2_back(grad_hidden_two)
    grad_middle = out_grad.astype(f32) + grad_mid_part

    grad_attn = gather_seq(grad_middle.astype(bf16)).reshape(TG, D)
    out_term = scatter_dp(dot(mixed, grad_attn, ((0,), (0,))))
    out_grad_w = lax.ppermute(
        out_term, BOTH, [(t * S + j, j * G + t) for j in range(S) for t in range(G)]
    ).astype(f32)
    grad_mixed = dot(grad_attn, w_out, ((1,), (1,))).reshape(S, T, H, DV)
    grad_gate, grad_ret = gate_back(grad_mixed)
    grad_gate = grad_gate.astype(bf16)
    grad_ret = grad_ret.astype(bf16)
    grad_qdecay = ein("bihe,bhde->bihd", grad_ret, state_in)
    state_grad = ein("bihd,bihe->bhde", query_decay, grad_ret)
    grad_scores = ein("bihe,bjhe->bhij", grad_ret, values)
    grad_raw = (grad_scores * mask[None]).astype(bf16)
    later = jnp.zeros_like(state_grad[0])
    laters = [None] * S
    for b in reversed(range(S)):
        laters[b] = later.astype(bf16)
        later = keep[b] * (state_grad[b] + block_decay * later)
    grad_local = jnp.stack(laters)
    grad_query = (
        ein("bhij,bjhd->bihd", grad_raw, keys) + grad_qdecay * decay_query[None, :, :, None]
    )
    grad_key = (
        ein("bhij,bihd->bjhd", grad_raw, queries)
        + ein("bjhe,bhde->bjhd", values, grad_local) * decay_key[None, :, :, None]
    )
    grad_value = ein("bhij,bihe->bjhe", scores, grad_ret) + ein(
        "bjhd,bhde->bjhe", key_decay, grad_local
    )
    grad_qpre = rotate(grad_query, cosine, -sine).astype(bf16).reshape(TG, QW)
    grad_kpre = rotate(grad_key * key_scale, cosine, -sine).astype(bf16).reshape(TG, QW)
    grad_projected = jnp.concatenate(
        [grad_qpre, grad_kpre, grad_value.astype(bf16).reshape(TG, VW), grad_gate.reshape(TG, VW)],
        axis=1,
    )
    in_term = scatter_dp(dot(hidden_one, grad_projected, ((0,), (0,))))
    in_term = exchange_seq(in_term.reshape(S, rows_in, 2 * QW + 2 * VW))
    cols = []
    start = 0
    for width in (QW, QW, VW, VW):
        part = in_term[:, :, start : start + width]
        cols.append(part.transpose(1, 0, 2).reshape(rows_in, S * width))
        start += width
    in_grad_w = jnp.concatenate(cols, axis=1).astype(f32)
    grad_hidden_one = scatter_seq(dot(grad_projected, w_in, ((1,), (1,))).reshape(S, T, D))
    grad_in_part, gain_one_grad, shift_one_grad = norm1_back(grad_hidden_one)
    in_grad = (grad_middle + grad_in_part).astype(bf16)
    norm_grads = lax.psum_scatter(
        jnp.stack([gain_one_grad, shift_one_grad, gain_two_grad, shift_two_grad]),
        BOTH,
        scatter_dimension=1,
        tiled=True,
    )
    return (
        layer_out,
        in_grad,
        norm_grads[0],
        norm_grads[1],
        in_grad_w,
        out_grad_w,
        norm_grads[2],
        norm_grads[3],
        up_grad,
        down_grad,
    )


def solution(mesh):
    rows, vector = P(BOTH, None), P(BOTH)
    in_specs = (rows, rows, P("dp", None), vector, vector, rows, rows, vector, vector, rows, rows)
    out_specs = (rows, rows, vector, vector, rows, rows, vector, vector, rows, rows)
    return jax.shard_map(local, mesh=mesh, in_specs=in_specs, out_specs=out_specs, check_vma=False)
```

time: 2840 us -> 1140 us (0.40)
  waiting for transfers between devices: 2350 us -> 620 us
  matrix products: 247 us -> 132 us
  local copies, waits for them, and re-layouts: 43 us -> 127 us
  blocking collectives: 99.2 us -> 130 us
    reduce_scatter x4, waiting for transfers between devices: 1740 us -> 216 us  [scatter_dp(): lax.psum_scatter(x.astype(bf16), 'dp', scatter_dimension=0, tiled=True)]
    all_gather x6 -> x4, waiting for transfers between devices: 603 us -> 99.7 us  [gather_dp(): return lax.all_gather(x, 'dp', axis=0, tiled=True)]
    ppermute x0 -> x18, waiting for transfers between devices: none -> 150 us  [the longest x16 150 us: swap_seq(): return lax.ppermute(x, 'seq', [(i, i ^ bit) for i in range(size)])]
    unnamed x10, waiting for transfers between devices: 2.52 us -> 133 us
    dot_general x24, matrix products: 247 us -> 132 us  [the longest x12 120 us: dot(): return lax.dot_general(a, b, (dims, ((), ())), preferred_element_type=f32)]
    all_gather x2 -> x1, blocking collectives: 10.9 us -> 106 us  [local(): lax.all_gather(jnp.stack([norm1_gain, norm1_shift, norm2_gain, norm2_shif...]
    unnamed x2 -> x0, blocking collectives: 88.3 us -> none
  transfers between devices with their start and end apart: 10 -> 30, of which waited for: 9 -> 17; matrix products, arithmetic and copies ran while one was open for 9% -> 24% of each run, Pallas kernels for 0% -> 0%
where the time goes in v1:
time: 1140 us; the launch traced here: 1130 us
  waiting for transfers between devices  620 us (54%)
  matrix products  132 us (12%)
  blocking collectives  130 us (11%)
  local copies, waits for them, and re-layouts  127 us (11%)
  other arithmetic  77.9 us (7%)
  starting transfers between devices  26.8 us (2%)
  between operations  16.2 us (1%)
    reduce_scatter x4, waiting for transfers between devices, scatter_dp(): lax.psum_scatter(x.astype(bf16), 'dp', scatter_dimension=0, tiled=True)  216 us
    ppermute x16, waiting for transfers between devices, swap_seq(): return lax.ppermute(x, 'seq', [(i, i ^ bit) for i in range(size)])  150 us
    unnamed x10, waiting for transfers between devices  133 us
    dot_general x12, matrix products, dot(): return lax.dot_general(a, b, (dims, ((), ())), preferred_element_type=f32)  120 us
    all_gather x1, blocking collectives, local(): lax.all_gather(jnp.stack([norm1_gain, norm1_shift, norm2_gain, norm2_shif...  106 us
    all_gather x4, waiting for transfers between devices, gather_dp(): return lax.all_gather(x, 'dp', axis=0, tiled=True)  99.7 us
    unnamed x166, local copies, waits for them, and re-layouts  45.7 us
    all_to_all x1, blocking collectives, exchange_seq(): return lax.all_to_all(x, 'seq', 0, 0)  24.4 us
  transfers between devices with their start and end apart: 30, of which 17 were waited for; matrix products, arithmetic and copies ran while one was open for 24% of the time, Pallas kernels for 0%

profile of v1, /device:TPU:0, one launch (start us, length us, event | category | flops | bytes accessed | tf_op | source)
XLA Modules:
  0.0 1129.9 jit_solution(7035085313268230148)
XLA Ops:
  12.0 24.4 %all_to_all.20 = bf16[4,64,3072]{2,1,0:T(8,128)(2,1)} all-to-all(bf16[4,64,3072]{2,1,0:T(8,128)(2,1)S(1)} %copy.198), channel_id=1, replica_groups=mesh['dp'=8,'seq'=4] {'seq'}, dimensions={0} | all-to-all | bytes 3145728 | tf_op jit(solution)/shard_map/all_to_all | solution.py:84
  38.0 106.0 %all-gather = bf16[32,64,4]{1,2,0:T(4,128)(2,1)S(1)} all-gather(bf16[1,64,4]{1,2,0:T(4,128)(2,1)S(1)} %maximum_bitcast_fusion.1), channel_id=1, replica_groups=mesh['dp'=8,'seq'=4] {'dp','seq'}, dimensions={0}, use_global_device_ids=true | all-gather | bytes 16896 | tf_op jit(solution)/shard_map/all_gather | solution.py:117
  153.1 4.1 all-to-all-start.1
  157.3 15.8 %collective-permute-done = bf16[1,256,2048]{2,1,0:T(8,128)(2,1)S(1)} collective-permute-done((bf16[1,256,2048]{2,1,0:T(8,128)(2,1)}, bf16[1,256,2048]{2,1,0:T(8,128)(2,1)S(1)}, u32[]{:S(2)}, u32[]{:S(2)}) %collective-permute-start) | collective-permute-done | bytes 1048608 | tf_op jit(solution)/shard_map/ppermute | solution.py:55
  173.1 3.3 maximum_select_fusion.4
  179.5 3.1 fusion.58
  188.8 50.7 %all-gather.6.cloned.1.call-done = bf16[2048,3072]{1,0:T(8,128)(2,1)} async-done(((bf16[256,3072]{1,0:T(8,128)(2,1)}), bf16[2048,3072]{1,0:T(8,128)(2,1)}) %all-gather.6.cloned.1.call-update) | async-done | bytes 12582928 | tf_op jit(solution)/shard_map/all_gather | solution.py:88
  239.5 17.0 %fusion.85 = f32[1024,3072]{1,0:T(8,128)S(1)} fusion(bf16[1024,2048]{1,0:T(8,128)(2,1)} %bitcast.265, bf16[2048,3072]{1,0:T(8,128)(2,1)} %all-gather.6.cloned.1.call-done), kind=kOutput, calls=%fused_computation.220 | convolution fusion | flops 12884901888 | bytes 29360128 | tf_op jit(solution)/shard_map/dot_general | solution.py:46
  262.8 3.3 reshape.733
  266.1 4.3 reshape.734
  270.5 6.7 reshape.732
  277.2 7.2 copy.200
  284.4 3.7 reshape.735
  303.1 10.7 all-gather.8.cloned.1.call-done
  313.8 6.4 fusion.8
  324.2 4.4 collective-permute-done.3
  335.7 23.9 %collective-permute-done.4 = bf16[1,256,2048]{2,1,0:T(8,128)(2,1)} collective-permute-done((bf16[1,256,2048]{2,1,0:T(8,128)(2,1)S(1)}, bf16[1,256,2048]{2,1,0:T(8,128)(2,1)}, u32[]{:S(2)}, u32[]{:S(2)}) %collective-permute-start.4) | collective-permute-done | bytes 1048608 | tf_op jit(solution)/shard_map/ppermute | solution.py:55
  364.4 17.7 %collective-permute-done.9 = bf16[1,256,2048]{2,1,0:T(8,128)(2,1)S(1)} collective-permute-done((bf16[1,256,2048]{2,1,0:T(8,128)(2,1)}, bf16[1,256,2048]{2,1,0:T(8,128)(2,1)S(1)}, u32[]{:S(2)}, u32[]{:S(2)}) %collective-permute-start.9) | collective-permute-done | bytes 1048608 | tf_op jit(solution)/shard_map/ppermute | solution.py:55
  384.1 19.6 %collective-permute-done.5 = bf16[1,256,2048]{2,1,0:T(8,128)(2,1)S(1)} collective-permute-done((bf16[1,256,2048]{2,1,0:T(8,128)(2,1)S(1)}, bf16[1,256,2048]{2,1,0:T(8,128)(2,1)S(1)}, u32[]{:S(2)}, u32[]{:S(2)}) %collective-permute-start.5) | collective-permute-done | bytes 1048608 | tf_op jit(solution)/shard_map/ppermute | solution.py:55
  413.2 9.9 fusion.86
  423.1 38.3 %all-gather.12.cloned.1.call-done = bf16[1024,2048]{1,0:T(8,128)(2,1)} async-done(((bf16[128,2048]{1,0:T(8,128)(2,1)}), bf16[1024,2048]{1,0:T(8,128)(2,1)}) %all-gather.12.cloned.1.call-update) | async-done | bytes 4194320 | tf_op jit(solution)/shard_map/all_gather | solution.py:88
  461.3 16.9 %add_convert_fusion.2 = (bf16[1024,1024]{1,0:T(8,128)(2,1)S(1)}, f32[1024,1024]{1,0:T(8,128)S(1)}) fusion(f32[1024,1024]{1,0:T(8,128)} %fusion.86, bf16[1024,2048]{1,0:T(8,128)(2,1)} %bitcast.269, bf16[1024,2048]{1,0:T(8,128)(2,1)} %all-gather.12.cloned.1.call-done), kind=kOutput, calls=%fused_computation.31 | convolution fusion | flops 4370464768 | bytes 18874368 | tf_op jit(solution)/shard_map/dot_general | solution.py:46
  481.9 6.2 convolution_convert_fusion.2
  488.2 7.6 fusion.88
  497.4 4.5 fusion.87
  510.9 18.6 %collective-permute-done.12 = bf16[1,256,2048]{2,1,0:T(8,128)(2,1)S(1)} collective-permute-done((bf16[1,256,2048]{2,1,0:T(8,128)(2,1)S(1)}, bf16[1,256,2048]{2,1,0:T(8,128)(2,1)S(1)}, u32[]{:S(2)}, u32[]{:S(2)}) %collective-permute-start.12) | collective-permute-done | bytes 1048608 | tf_op jit(solution)/shard_map/ppermute | solution.py:55
  530.2 21.3 %collective-permute-done.8 = bf16[1,256,2048]{2,1,0:T(8,128)(2,1)S(1)} collective-permute-done((bf16[1,256,2048]{2,1,0:T(8,128)(2,1)S(1)}, bf16[1,256,2048]{2,1,0:T(8,128)(2,1)S(1)}, u32[]{:S(2)}, u32[]{:S(2)}) %collective-permute-start.8) | collective-permute-done | bytes 1048608 | tf_op jit(solution)/shard_map/ppermute | solution.py:55
  557.3 23.3 %collective-permute-done.13 = bf16[1,256,2048]{2,1,0:T(8,128)(2,1)S(1)} collective-permute-done((bf16[1,256,2048]{2,1,0:T(8,128)(2,1)S(1)}, bf16[1,256,2048]{2,1,0:T(8,128)(2,1)S(1)}, u32[]{:S(2)}, u32[]{:S(2)}) %collective-permute-start.13) | collective-permute-done | bytes 1048608 | tf_op jit(solution)/shard_map/ppermute | solution.py:55
  582.4 6.4 convolution_convert_fusion.1
  600.4 5.3 multiply_reduce_fusion
  605.7 4.6 fusion.73
  610.3 6.4 copy.235
  616.6 3.7 copy.281
  638.2 6.6 copy.232
  649.2 3.2 copy-done.48
  653.5 16.0 %convolution_convert_fusion = bf16[2048,3072]{1,0:T(8,128)(2,1)} fusion(bf16[1024,2048]{1,0:T(8,128)(2,1)S(1)} %bitcast.266, bf16[1024,3072]{1,0:T(8,128)(2,1)S(1)} %constant_dynamic-update-slice_fusion), kind=kOutput, calls=%fused_computation | convolution fusion | flops 12891193344 | bytes 23068672 | tf_op jit(solution)/shard_map/dot_general | solution.py:46
  669.5 6.2 copy.241
  678.5 6.2 convolution_convert_fusion.3
  684.8 18.0 %fusion.90 = f32[1024,2048]{1,0:T(8,128)S(1)} fusion(bf16[1024,3072]{1,0:T(8,128)(2,1)} %copy-done.48, bf16[2048,3072]{1,0:T(8,128)(2,1)} %all-gather.6.cloned.1.call-done), kind=kOutput, calls=%fused_computation.225 | convolution fusion | flops 12884901888 | bytes 27262976 | tf_op jit(solution)/shard_map/dot_general | solution.py:46
  703.7 3.8 collective-permute-done.15
  713.0 4.1 all-to-all-start.3
  721.4 21.5 %all-to-all-done.3 = bf16[4,64,1024]{2,1,0:T(8,128)(2,1)} async-done(((bf16[4,64,1024]{2,1,0:T(8,128)(2,1)}), bf16[4,64,1024]{2,1,0:T(8,128)(2,1)}, u32[]{:S(2)}, u32[]{:S(2)}) %all-to-all-start.3) | async-done | bytes 524320 | tf_op jit(solution)/shard_map/all_to_all | solution.py:84
  752.7 133.6 %reduce-scatter.8.cloned.1.call-done = bf16[256,3072]{1,0:T(8,128)(2,1)} async-done(((bf16[2048,3072]{1,0:T(8,128)(2,1)}), bf16[256,3072]{1,0:T(8,128)(2,1)}) %reduce-scatter.8.cloned.1.call-update) | async-done | bytes 1572880 | tf_op jit(solution)/shard_map/reduce_scatter | solution.py:92
  886.3 4.4 all-to-all-start.2
  890.7 4.0 fusion.72
  894.7 82.3 %reduce-scatter.10.cloned.1.call-done = bf16[128,2048]{1,0:T(8,128)(2,1)} async-done(((bf16[1024,2048]{1,0:T(8,128)(2,1)}), bf16[128,2048]{1,0:T(8,128)(2,1)}) %reduce-scatter.10.cloned.1.call-update) | async-done | bytes 524304 | tf_op jit(solution)/shard_map/reduce_scatter | solution.py:92
  978.6 3.3 add_convert_fusion.3
  981.9 132.5 %reduce-scatter.16.cloned.1.call-done = f32[64,4]{1,0:T(8,128)} async-done(((f32[2048,4]{1,0:T(8,128)}), f32[64,4]{1,0:T(8,128)}) %reduce-scatter.16.cloned.1.call-update) | async-done | bytes 1040
  (337 shorter events, 163.0 us)
Async XLA Ops:
  7.2 232.3 %all-gather.6.cloned.1.call-start = ((), (), s32[]{:S(2)}) async-start(), calls=%async_computation.9 | async-start | bytes 14155776 | tf_op jit(solution)/shard_map/all_gather | solution.py:88
  11.9 24.5 %copy-start.70 = (bf16[128,2048]{1,0:T(8,128)(2,1)S(1)}, bf16[128,2048]{1,0:T(8,128)(2,1)}, u32[]{:S(2)}) copy-start(bf16[128,2048]{1,0:T(8,128)(2,1)} %param.17) | copy-start | bytes 1572868
  12.0 26.0 %copy-start.64 = (bf16[64]{0:T(256)(128)(2,1)S(1)}, bf16[64]{0:T(256)(128)(2,1)}, u32[]{:S(2)}) copy-start(bf16[64]{0:T(256)(128)(2,1)} %param.19) | copy-start | bytes 388
  12.0 26.0 %copy-start.65 = (bf16[64]{0:T(256)(128)(2,1)S(1)}, bf16[64]{0:T(256)(128)(2,1)}, u32[]{:S(2)}) copy-start(bf16[64]{0:T(256)(128)(2,1)} %param.18) | copy-start | bytes 388
  12.0 26.0 %copy-start.66 = (bf16[64]{0:T(256)(128)(2,1)S(1)}, bf16[64]{0:T(256)(128)(2,1)}, u32[]{:S(2)}) copy-start(bf16[64]{0:T(256)(128)(2,1)} %param.15) | copy-start | bytes 388
  12.0 26.0 %copy-start.67 = (bf16[64]{0:T(256)(128)(2,1)S(1)}, bf16[64]{0:T(256)(128)(2,1)}, u32[]{:S(2)}) copy-start(bf16[64]{0:T(256)(128)(2,1)} %param.14) | copy-start | bytes 388
  12.0 132.2 %copy-start.4 = (bf16[256,2048]{1,0:T(8,128)(2,1)S(1)}, bf16[256,2048]{1,0:T(8,128)(2,1)}, u32[]{:S(2)}) copy-start(bf16[256,2048]{1,0:T(8,128)(2,1)} %param.11) | copy-start | bytes 3145732
  36.4 277.4 %all-gather.8.cloned.1.call-start = ((), (), s32[]{:S(2)}) async-start(), calls=%async_computation.10 | async-start | bytes 4718592 | tf_op jit(solution)/shard_map/all_gather | solution.py:88
  36.5 0.7 collective-permute-start.2
  146.9 10.4 copy-start.71
  146.9 26.2 %collective-permute-start = (bf16[1,256,2048]{2,1,0:T(8,128)(2,1)}, bf16[1,256,2048]{2,1,0:T(8,128)(2,1)S(1)}, u32[]{:S(2)}, u32[]{:S(2)}) collective-permute-start(bf16[1,256,2048]{2,1,0:T(8,128)(2,1)} %get-tuple-element.56), channel_id=1, source_target_pairs={{0,2},{1,3},{2,0},{3,1},{4,6},{5,7},{6,4},{7,5},{8,10},{9,11},{10,... | collective-permute-start | bytes 3145736 | tf_op jit(solution)/shard_map/ppermute | solution.py:55
  153.1 29.6 %all-to-all-start.1 = ((bf16[4,64,1024]{2,1,0:T(8,128)(2,1)}), bf16[4,64,1024]{2,1,0:T(8,128)(2,1)}, u32[]{:S(2)}, u32[]{:S(2)}) async-start(bf16[4,64,1024]{2,1,0:T(8,128)(2,1)} %reshape.737), calls=%async_computation.1 | async-start | bytes 1048576 | tf_op jit(solution)/shard_map/all_to_all | solution.py:84
  157.2 255.9 %all-gather.10.cloned.1.call-start = ((), (), s32[]{:S(2)}) async-start(), calls=%async_computation.11 | async-start | bytes 4718592 | tf_op jit(solution)/shard_map/all_gather | solution.py:88
  176.4 7.2 collective-permute-start.1
  178.4 114.1 %copy-start.61 = (f32[2]{0:T(128)}, f32[2]{0:T(128)S(1)}, u32[]{:S(2)}) copy-start(f32[2]{0:T(128)S(1)} %get-tuple-element.78) | copy-start | bytes 28
  178.5 113.0 %copy-start.59 = (f32[256,2]{0,1:T(2,128)}, f32[256,2]{0,1:T(2,128)S(1)}, u32[]{:S(2)}) copy-start(f32[256,2]{0,1:T(2,128)S(1)} %get-tuple-element.79) | copy-start | bytes 6148
  178.5 118.1 %copy-start.51 = (f32[256,2]{0,1:T(2,128)}, f32[256,2]{0,1:T(2,128)S(1)}, u32[]{:S(2)}) copy-start(f32[256,2]{0,1:T(2,128)S(1)} %get-tuple-element.80) | copy-start | bytes 6148
  179.5 117.1 %copy-start.72 = (bf16[4]{0:T(256)(128)(2,1)}, bf16[4]{0:T(256)(128)(2,1)S(1)}, u32[]{:S(2)}) copy-start(bf16[4]{0:T(256)(128)(2,1)S(1)} %pad.52.clone) | copy-start | bytes 28
  182.7 278.6 %all-gather.12.cloned.1.call-start = ((), (), s32[]{:S(2)}) async-start(), calls=%async_computation.12 | async-start | bytes 4718592 | tf_op jit(solution)/shard_map/all_gather | solution.py:88
  266.1 29.5 %copy-start.10 = (bf16[4,256,2,512]{3,2,1,0:T(2,128)(2,1)}, bf16[4,256,2,512]{3,2,1,0:T(2,128)(2,1)S(1)}, u32[]{:S(2)}) copy-start(bf16[4,256,2,512]{3,2,1,0:T(2,128)(2,1)S(1)} %reshape.733) | copy-start | bytes 6291460
  303.1 17.1 %copy-start.18 = (bf16[4,256,2,512]{1,3,2,0:T(8,128)(2,1)}, bf16[4,256,2,512]{1,3,2,0:T(8,128)(2,1)S(1)}, u32[]{:S(2)}) copy-start(bf16[4,256,2,512]{1,3,2,0:T(8,128)(2,1)S(1)} %multiply_convert_fusion.1) | copy-start | bytes 6291460
  324.2 4.4 collective-permute-start.3
  333.5 26.2 %collective-permute-start.4 = (bf16[1,256,2048]{2,1,0:T(8,128)(2,1)S(1)}, bf16[1,256,2048]{2,1,0:T(8,128)(2,1)}, u32[]{:S(2)}, u32[]{:S(2)}) collective-permute-start(bf16[1,256,2048]{2,1,0:T(8,128)(2,1)S(1)} %dynamic-slice_convert_fusion.4), channel_id=1, source_target_pairs={{0,2},{1,3},{2,0},{3,1},{4,6},{5,7},{6,4},{7,5},{8,10},{9,11},{10,... | collective-permute-start | bytes 3145736 | tf_op jit(solution)/shard_map/ppermute | solution.py:55
  335.1 378.0 %reduce-scatter.12.cloned.1.call-start = ((), (), s32[]{:S(2)}) async-start(), calls=%async_computation.15 | async-start | bytes 4718592 | tf_op jit(solution)/shard_map/reduce_scatter | solution.py:92
  335.1 46.9 %collective-permute-start.9 = (bf16[1,256,2048]{2,1,0:T(8,128)(2,1)}, bf16[1,256,2048]{2,1,0:T(8,128)(2,1)S(1)}, u32[]{:S(2)}, u32[]{:S(2)}) collective-permute-start(bf16[1,256,2048]{2,1,0:T(8,128)(2,1)} %bitcast.42), channel_id=1, source_target_pairs={{0,2},{1,3},{2,0},{3,1},{4,6},{5,7},{6,4},{7,5},{8,10},{9,11},{10,... | collective-permute-start | bytes 3145736 | tf_op jit(solution)/shard_map/ppermute | solution.py:55
  362.9 40.9 %collective-permute-start.5 = (bf16[1,256,2048]{2,1,0:T(8,128)(2,1)S(1)}, bf16[1,256,2048]{2,1,0:T(8,128)(2,1)S(1)}, u32[]{:S(2)}, u32[]{:S(2)}) collective-permute-start(bf16[1,256,2048]{2,1,0:T(8,128)(2,1)S(1)} %fusion.126), channel_id=1, source_target_pairs={{0,2},{1,3},{2,0},{3,1},{4,6},{5,7},{6,4},{7,5},{8,10},{9,11},{10,... | collective-permute-start | bytes 3145736 | tf_op jit(solution)/shard_map/ppermute | solution.py:55
  384.0 22.1 %collective-permute-start.10 = (bf16[2,256,2048]{2,1,0:T(8,128)(2,1)S(1)}, bf16[2,256,2048]{2,1,0:T(8,128)(2,1)S(1)}, u32[]{:S(2)}, u32[]{:S(2)}) collective-permute-start(bf16[2,256,2048]{2,1,0:T(8,128)(2,1)S(1)} %maximum_select_fusion.8), channel_id=1, source_target_pairs={{0,1},{1,0},{2,3},{3,2},{4,5},{5,4},{6,7},{7,6},{8,9},{9,8},{10,11... | collective-permute-start | bytes 6291464 | tf_op jit(solution)/shard_map/ppermute | solution.py:55
  404.1 6.0 collective-permute-start.6
  461.3 16.9 %copy-start.34 = (f32[1024,1024]{1,0:T(8,128)S(1)}, f32[1024,1024]{1,0:T(8,128)}, u32[]{:S(2)}) copy-start(f32[1024,1024]{1,0:T(8,128)} %fusion.86) | copy-start | bytes 12582916
  488.1 231.2 %reduce-scatter.14.cloned.1.call-start = ((), (), s32[]{:S(2)}) async-start(), calls=%async_computation.16 | async-start | bytes 4718592 | tf_op jit(solution)/shard_map/reduce_scatter | solution.py:92
  496.1 6.2 collective-permute-start.11
  502.3 4.4 collective-permute-start.7
  503.2 48.3 %copy-start.9 = (f32[2,256,2048]{2,1,0:T(8,128)}, f32[2,256,2048]{2,1,0:T(8,128)S(1)}, u32[]{:S(2)}) copy-start(f32[2,256,2048]{2,1,0:T(8,128)S(1)} %bitcast_add_fusion.1) | copy-start | bytes 12582916
  503.4 26.0 %collective-permute-start.12 = (bf16[1,256,2048]{2,1,0:T(8,128)(2,1)S(1)}, bf16[1,256,2048]{2,1,0:T(8,128)(2,1)S(1)}, u32[]{:S(2)}, u32[]{:S(2)}) collective-permute-start(bf16[1,256,2048]{2,1,0:T(8,128)(2,1)S(1)} %dynamic-slice_convert_fusion.2), channel_id=1, source_target_pairs={{0,2},{1,3},{2,0},{3,1},{4,6},{5,7},{6,4},{7,5},{8,10},{9,11},{10,... | collective-permute-start | bytes 3145736 | tf_op jit(solution)/shard_map/ppermute | solution.py:55
  509.3 42.2 %collective-permute-start.8 = (bf16[1,256,2048]{2,1,0:T(8,128)(2,1)S(1)}, bf16[1,256,2048]{2,1,0:T(8,128)(2,1)S(1)}, u32[]{:S(2)}, u32[]{:S(2)}) collective-permute-start(bf16[1,256,2048]{2,1,0:T(8,128)(2,1)S(1)} %dynamic-slice_convert_fusion.3), channel_id=1, source_target_pairs={{0,2},{1,3},{2,0},{3,1},{4,6},{5,7},{6,4},{7,5},{8,10},{9,11},{10,... | collective-permute-start | bytes 3145736 | tf_op jit(solution)/shard_map/ppermute | solution.py:55
  529.4 22.1 %copy-start.14 = (bf16[1,256,2048]{2,1,0:T(8,128)(2,1)}, bf16[1,256,2048]{2,1,0:T(8,128)(2,1)S(1)}, u32[]{:S(2)}) copy-start(bf16[1,256,2048]{2,1,0:T(8,128)(2,1)S(1)} %collective-permute-done.12) | copy-start | bytes 3145732
  555.8 26.6 %copy-start.32 = (bf16[2,2,256,2048]{3,2,1,0:T(8,128)(2,1)S(1)}, bf16[2,2,256,2048]{3,2,1,0:T(8,128)(2,1)}, u32[]{:S(2)}) copy-start(bf16[2,2,256,2048]{3,2,1,0:T(8,128)(2,1)} %copy.213) | copy-start | bytes 12582916
  555.8 24.8 %collective-permute-start.13 = (bf16[1,256,2048]{2,1,0:T(8,128)(2,1)S(1)}, bf16[1,256,2048]{2,1,0:T(8,128)(2,1)S(1)}, u32[]{:S(2)}, u32[]{:S(2)}) collective-permute-start(bf16[1,256,2048]{2,1,0:T(8,128)(2,1)S(1)} %fusion.124), channel_id=1, source_target_pairs={{0,2},{1,3},{2,0},{3,1},{4,6},{5,7},{6,4},{7,5},{8,10},{9,11},{10,... | collective-permute-start | bytes 3145736 | tf_op jit(solution)/shard_map/ppermute | solution.py:55
  582.3 10.0 collective-permute-start.14
  588.8 297.5 %reduce-scatter.8.cloned.1.call-start = ((), (), s32[]{:S(2)}) async-start(), calls=%async_computation.13 | async-start | bytes 14155776 | tf_op jit(solution)/shard_map/reduce_scatter | solution.py:92
  595.9 9.8 copy-start.30
  669.5 307.5 %reduce-scatter.10.cloned.1.call-start = ((), (), s32[]{:S(2)}) async-start(), calls=%async_computation.14 | async-start | bytes 4718592 | tf_op jit(solution)/shard_map/reduce_scatter | solution.py:92
  703.1 4.4 collective-permute-start.15
  711.6 34.6 %collective-permute-start.16 = (bf16[1,256,2048]{2,1,0:T(8,128)(2,1)}, bf16[1,256,2048]{2,1,0:T(8,128)(2,1)}, u32[]{:S(2)}, u32[]{:S(2)}) collective-permute-start(bf16[1,256,2048]{2,1,0:T(8,128)(2,1)} %dynamic-slice_convert_fusion.1), channel_id=1, source_target_pairs={{0,2},{1,3},{2,0},{3,1},{4,6},{5,7},{6,4},{7,5},{8,10},{9,11},{10,... | collective-permute-start | bytes 3145736 | tf_op jit(solution)/shard_map/ppermute | solution.py:55
  713.0 29.9 %all-to-all-start.3 = ((bf16[4,64,1024]{2,1,0:T(8,128)(2,1)}), bf16[4,64,1024]{2,1,0:T(8,128)(2,1)}, u32[]{:S(2)}, u32[]{:S(2)}) async-start(bf16[4,64,1024]{2,1,0:T(8,128)(2,1)} %bitcast.289), calls=%async_computation.6 | async-start | bytes 1048576 | tf_op jit(solution)/shard_map/all_to_all | solution.py:84
  717.2 397.2 %reduce-scatter.16.cloned.1.call-start = ((), (), s32[]{:S(2)}) async-start(), calls=%async_computation.17 | async-start | bytes 1081344
  886.3 232.5 %all-to-all-start.2 = ((bf16[4,64,3072]{2,1,0:T(8,128)(2,1)}), bf16[4,64,3072]{2,1,0:T(8,128)(2,1)}, u32[]{:S(2)}, u32[]{:S(2)}) async-start(bf16[4,64,3072]{2,1,0:T(8,128)(2,1)} %bitcast.286), calls=%async_computation.3 | async-start | bytes 3145728 | tf_op jit(solution)/shard_map/all_to_all | solution.py:84
  976.9 140.8 %collective-permute-start.17 = (bf16[128,2048]{1,0:T(8,128)(2,1)}, bf16[128,2048]{1,0:T(8,128)(2,1)S(1)}, u32[]{:S(2)}, u32[]{:S(2)}) collective-permute-start(bf16[128,2048]{1,0:T(8,128)(2,1)} %reduce-scatter.10.cloned.1.call-done), channel_id=1, source_target_pairs={{0,0},{4,1},{8,2},{12,3},{16,4},{20,5},{24,6},{28,7},{1,8},{5,9},{... | collective-permute-start | bytes 1572872 | tf_op jit(solution)/shard_map/ppermute | solution.py:215
  (57 other events, 143.8 us)
Sparse Core Ops, SparseCore 0:
  36.5 202.9 all-gather.5
  242.2 71.5 all-gather.7
  315.9 71.6 all-gather.9
  389.6 71.6 all-gather.11
  488.2 86.1 reduce-scatter.11
  588.9 86.7 reduce-scatter.13
  679.2 207.0 reduce-scatter.7
  889.9 86.9 reduce-scatter.9
  979.9 134.4 reduce-scatter.15

commit v2 on v1

v2 whole, which is shorter than its diff:
```python
import functools

import jax
import jax.numpy as jnp
from jax import lax
from jax.experimental import pallas as pl
from jax.experimental.pallas import tpu as pltpu
from jax.sharding import PartitionSpec as P

D = 2048
HEADS = 8
VD = 4096
DK = 256
DV = 512
HALF = DK // 2
BOTH = ("dp", "seq")
f32 = jnp.float32
bf16 = jnp.bfloat16
ANY = pl.BlockSpec(memory_space=pl.ANY)
VMEM = pl.BlockSpec(memory_space=pltpu.VMEM)
LIMIT = 58 << 20
DEPTH = 4


def dot(a, b, dims):
    return lax.dot_general(a, b, (dims, ((), ())), preferred_element_type=f32)


def call(body, info, ins, outs, scratch=(), grid=(), in_specs=None, out_specs=None, name=None, cost=None, after=()):
    many = isinstance(outs, (list, tuple))
    n_in, n_after = len(ins), len(after)
    ins, after = list(ins), list(after)

    def inner(at, *refs):
        body(at, *refs[:n_in], *refs[n_in + n_after :])

    spec = pltpu.PrefetchScalarGridSpec(
        num_scalar_prefetch=1,
        grid=grid,
        in_specs=list(in_specs or [ANY] * n_in) + [ANY] * n_after,
        out_specs=out_specs or ([ANY] * len(outs) if many else ANY),
        scratch_shapes=list(scratch),
    )
    moved = sum(x.size * x.dtype.itemsize for x in (*ins, *(outs if many else [outs])))
    return pl.pallas_call(
        inner,
        out_shape=outs,
        grid_spec=spec,
        name=name,
        cost_estimate=pl.CostEstimate(
            flops=cost or 0, bytes_accessed=int(moved), transcendentals=0
        ),
        compiler_params=pltpu.CompilerParams(vmem_limit_bytes=LIMIT),
    )(info, *ins, *after)


def tie(x, *after):
    return pl.pallas_call(
        lambda *refs: None,
        out_shape=like(x.shape, x.dtype),
        in_specs=[ANY] * (1 + len(after)),
        out_specs=ANY,
        input_output_aliases={0: 0},
        name="tie",
    )(x, *after)


def like(shape, dtype):
    return jax.ShapeDtypeStruct(shape, dtype)


def seq_gaps(size):
    return [1 << b for b in range(size.bit_length() - 1)]


def swap_seq(x, gap):
    size = lax.axis_size("seq")
    return lax.ppermute(x, "seq", [(i, i ^ gap) for i in range(size)])


class Loads:
    def __init__(self, sems):
        self.sems, self.count, self.groups = sems, 0, {}

    def add(self, group, source, target):
        copy = pltpu.make_async_copy(source, target, self.sems.at[self.count])
        self.groups.setdefault(group, []).append(copy)
        self.count += 1
        copy.start()

    def wait(self, group):
        for copy in self.groups.pop(group, []):
            copy.wait()


def block_row(at, gap, rows):
    return pl.multiple_of((at[0] ^ gap) * rows, rows)


def gather_seq(x, *after):
    held = {0: x}
    for gap in reversed(seq_gaps(lax.axis_size("seq"))):
        new = {g ^ gap: swap_seq(part, gap) for g, part in list(held.items())}
        if after and gap == lax.axis_size("seq") // 2:
            new = {g: tie(part, *after) for g, part in new.items()}
        held.update(new)
    return held


ROWS = 128


def plain(body, ins, outs, grid, in_specs, out_specs, name, after=()):
    n_in = len(ins)

    def inner(*refs):
        body(*refs[:n_in], *refs[n_in + len(after) :])

    return pl.pallas_call(
        inner,
        out_shape=outs,
        grid=grid,
        in_specs=[*in_specs, *[ANY] * len(after)],
        out_specs=out_specs,
        name=name,
        compiler_params=pltpu.CompilerParams(vmem_limit_bytes=LIMIT),
    )(*ins, *after)


def tile_of(rows, cols):
    return pl.BlockSpec((rows, cols), lambda i: (i, 0))


def add_up(parts, dtype, after=()):
    T, C = parts[0].shape

    def body(*refs):
        total = refs[0][...].astype(f32)
        for ref in refs[1:-1]:
            total = total + ref[...].astype(f32)
        refs[-1][...] = total.astype(dtype)

    return plain(
        body,
        parts,
        like((T, C), dtype),
        (T // ROWS,),
        [tile_of(ROWS, C)] * len(parts),
        tile_of(ROWS, C),
        "add_up",
        after,
    )


def swap_odd(parts, got):
    for gap in sorted((gap for gap in parts if gap & 1), reverse=True):
        got.setdefault(gap ^ 1, []).append(swap_seq(parts[gap], 1))


def scatter_seq(parts, got, after=()):
    size = lax.axis_size("seq")
    sent = parts[0]
    bit = 2
    while bit < size:
        for gap in [gap for gap in reversed(range(size)) if gap & bit and gap % bit == 0]:
            sent = add_up([parts[gap], *got[gap]], bf16, after)
            got.setdefault(gap ^ bit, []).append(swap_seq(sent, bit))
        bit *= 2
    return [parts[0], *got[0]], sent


def norm_forward(rows, gain, shift, more=(), after=()):
    T, C = rows.shape
    wide = len(more) > 0

    def body(rows_ref, gain_ref, shift_ref, *refs):
        outs = refs[-2:] if wide else refs[-1:]
        total = rows_ref[...].astype(f32)
        for ref in refs[: len(more)]:
            total = total + ref[...].astype(f32)
        if wide:
            outs[0][...] = total
        centred = total - jnp.mean(total, axis=-1, keepdims=True)
        spread = jnp.mean(centred * centred, axis=-1, keepdims=True)
        normed = centred * lax.rsqrt(spread + 1e-05) * gain_ref[...] + shift_ref[...]
        outs[-1][...] = normed.astype(bf16)

    vector = pl.BlockSpec((1, C), lambda i: (0, 0))
    outs = ([like((T, C), f32)] if wide else []) + [like((T, C), bf16)]
    return plain(
        body,
        [rows, gain, shift, *more],
        outs,
        (T // ROWS,),
        [tile_of(ROWS, C), vector, vector] + [tile_of(ROWS, C)] * len(more),
        [tile_of(ROWS, C)] * len(outs),
        "norm_forward",
        after,
    )


def norm_backward(rows, gain, base, parts, dtypes, after=()):
    T, C = rows.shape
    n = len(parts)

    def body(rows_ref, gain_ref, base_ref, *refs):
        grad = refs[0][...].astype(f32)
        for ref in refs[1:n]:
            grad = grad + ref[...].astype(f32)
        total = rows_ref[...].astype(f32)
        centred = total - jnp.mean(total, axis=-1, keepdims=True)
        inverse = lax.rsqrt(jnp.mean(centred * centred, axis=-1, keepdims=True) + 1e-05)
        normed = centred * inverse
        inner = grad * gain_ref[...]
        pull = inner - jnp.mean(inner, axis=-1, keepdims=True)
        pull = pull - normed * jnp.mean(inner * normed, axis=-1, keepdims=True)
        result = base_ref[...].astype(f32) + inverse * pull
        for out in refs[n:-1]:
            out[...] = result.astype(out.dtype)
        sums = refs[-1]

        @pl.when(pl.program_id(0) == 0)
        def _():
            sums[...] = jnp.zeros_like(sums)

        sums[0:1, :] += jnp.sum(grad * normed, axis=0, keepdims=True)
        sums[1:2, :] += jnp.sum(grad, axis=0, keepdims=True)

    vector = pl.BlockSpec((1, C), lambda i: (0, 0))
    outs = [like((T, C), t) for t in dtypes] + [like((8, C), f32)]
    return plain(
        body,
        [rows, gain, base, *parts],
        outs,
        (T // ROWS,),
        [tile_of(ROWS, C), vector, tile_of(ROWS, C)] + [tile_of(ROWS, C)] * n,
        [tile_of(ROWS, C)] * len(dtypes) + [pl.BlockSpec((8, C), lambda i: (0, 0))],
        "norm_backward",
        after,
    )


def swap_all(x, gap):
    size = lax.axis_size("dp") * lax.axis_size("seq")
    return lax.ppermute(x, BOTH, [(i, i ^ gap) for i in range(size)])


def flat_index():
    return lax.axis_index("dp") * lax.axis_size("seq") + lax.axis_index("seq")


def gather_all(x):
    S, G = lax.axis_size("seq"), lax.axis_size("dp")
    me = flat_index()
    held = x[None, None]
    middle = None
    for gap in [S * g for g in seq_gaps(G)] + seq_gaps(S):
        axis = 0 if gap >= S else 1
        other = swap_all(held, gap)
        held = jnp.where(
            (me & gap) != 0,
            jnp.concatenate([other, held], axis=axis),
            jnp.concatenate([held, other], axis=axis),
        )
        if gap == S * G // 2:
            middle = held
    return held.reshape((G * S,) + x.shape), middle


def scatter_all(x, afters):
    me = flat_index()
    held = x
    for n, gap in enumerate(reversed(seq_gaps(x.shape[0]))):
        half = held.shape[0] // 2
        upper = (me & gap) != 0
        keep = jnp.where(upper, held[half:], held[:half])
        give = jnp.where(upper, held[:half], held[half:])
        got = swap_all(give, gap)
        if n < len(afters):
            got = tie(got, *afters[n])
        held = keep + got
    return held[0]


def cycle(size):
    depth = DEPTH
    width = size // depth
    walk = [(0, x) for x in range(width)]
    for turn, x in enumerate(reversed(range(width))):
        column = [(z, x) for z in range(1, depth)]
        walk += column if turn % 2 == 0 else column[::-1]
    return [z * width + x for z, x in walk]


def ring_moves(size):
    walk = cycle(size)
    ahead = [(walk[i], walk[(i + 1) % size]) for i in range(size)]
    return ahead, [(b, a) for a, b in ahead]


def shard_place(t, size):
    return (t % DEPTH) * (size // DEPTH) + t // DEPTH


def make_info():
    size = lax.axis_size("dp")
    walk = cycle(size)
    table = [[walk[(walk.index(i) - k) % size] for k in range(size)] for i in range(size)]
    shard = {shard_place(t, size): t for t in range(size)}
    table = [row + [shard[i] for i in row] for row in table]
    row = lax.dynamic_index_in_dim(jnp.array(table, jnp.int32), lax.axis_index("dp"), 0, False)
    return jnp.concatenate([lax.axis_index("seq").astype(jnp.int32)[None], row])


class Gather:
    def __init__(self, x):
        self.size = lax.axis_size("dp")
        self.ahead, self.back = ring_moves(self.size)
        self.got = {0: x}
        self.hop = 0

    def step(self):
        size, half = self.size, self.got[0].shape[0] // 2
        self.hop += 1
        k = self.hop
        a, b = self.got[k - 1], self.got[(size - k + 1) % size]
        if k == size // 2:
            a, b = a[:half], b[half:]
        self.sent = (a, b)
        a, b = lax.ppermute(a, "dp", self.ahead), lax.ppermute(b, "dp", self.back)
        if k == size // 2:
            self.halves = (a, b)
        else:
            self.got[k], self.got[size - k] = a, b
        self.last = (a, b)
        return self


def unfold(ref, row, rows, fold, width, start, r0, n):
    views = []
    for c in range(fold):
        lo, hi = max(r0, c * rows), min(r0 + n, (c + 1) * rows)
        if lo < hi:
            views.append((lo - r0, hi - lo, ref.at[pl.ds(row + lo - c * rows, hi - lo), pl.ds(c * width, width)]))
    return views


def piece_views(refs, kinds, places, r0, n, rows):
    out = []
    column = 0
    places = places if isinstance(places, list) else [places] * len(refs)
    for ref, kind, place in zip(refs, kinds, places):
        if kind == 1:
            start = pl.multiple_of(place * rows + r0, n)
            out.append((0, n, column, ref.shape[1], ref.at[pl.ds(start, n)]))
            column += ref.shape[1]
        else:
            width, short = ref.shape[1] // kind, rows // kind
            row = pl.multiple_of(place * short, short)
            for at, count, view in unfold(ref, row, short, kind, width, 0, r0, n):
                out.append((at, count, column, width, view))
            column += width
    return out


class Weight:
    def __init__(self, ring, kind=1, first=0, width=None, shards=False):
        while ring.hop < ring.size // 2:
            ring.step()
        self.kind, self.first, self.shards, self.size = kind, first, shards, ring.size
        self.rows, cols = ring.got[0].shape
        width = width or cols
        half, middle = self.rows // 2, ring.size // 2
        self.parts = [(k, 0, self.rows, x) for k, x in ring.got.items()]
        self.parts += [(middle, 0, half, ring.halves[0]), (middle, half, half, ring.halves[1])]
        self.shape = (self.size * self.rows // kind, width * kind)
        self.arrays = [x for _, _, _, x in self.parts]
        self.copies = len(self.parts) * kind

    def load(self, loads, group, at, refs, target):
        for (k, r0, n, _), ref in zip(self.parts, refs):
            place = at[1 + k + (self.size if self.shards else 0)]
            for row, count, column, width, view in piece_views([target], [self.kind], place, r0, n, self.rows):
                source = ref.at[pl.ds(row, count), pl.ds(self.first + column, width)]
                loads.add(group, source, view)


def tokens_times(info, held, weight, cols, across, name, after=()):
    gaps = list(held)
    S, (T, K) = len(gaps), held[0].shape
    n_w, n_out = len(weight.arrays), len(cols)

    def body(at, *refs):
        pieces, w_refs, outs = refs[:S], refs[S : S + n_w], refs[S + n_w : S + n_w + n_out]
        x, w, *stages, sems = refs[S + n_w + n_out :]
        loads = Loads(sems)
        weight.load(loads, "w", at, w_refs, w)
        for n, piece in enumerate(pieces):
            loads.add(n, piece, x.at[n])
        loads.wait("w")
        for n, gap in enumerate(gaps):
            loads.wait(n)
            for (first, width, dtype), out, stage in zip(cols, outs, stages):
                if across:
                    result = dot(x[n], w[first : first + width, :], ((1,), (1,)))
                else:
                    result = dot(x[n], w[:, first : first + width], ((1,), (0,)))
                stage[n] = result.astype(dtype)
                loads.add("out", stage.at[n], out.at[pl.ds(block_row(at, gap, T), T)])
        loads.wait("out")

    return call(
        body,
        info,
        [*held.values(), *weight.arrays],
        [like((S * T, width), dtype) for _, width, dtype in cols],
        [pltpu.VMEM((S, T, K), bf16), pltpu.VMEM(weight.shape, bf16)]
        + [pltpu.VMEM((S, T, width), dtype) for _, width, dtype in cols]
        + [pltpu.SemaphoreType.DMA((S + weight.copies + S * n_out,))],
        name=name,
        after=after,
        cost=2 * S * T * K * sum(width for _, width, _ in cols),
    )


def partial_rows(info, terms, gaps, name, after=()):
    arrays, picks = [], []
    for x, weight, _ in terms:
        mine = [x[gap] for gap in gaps] if isinstance(x, dict) else [x]
        picks.append((len(arrays), len(mine), isinstance(x, dict)))
        arrays += [*mine, *weight.arrays]
    first = terms[0][0]
    T = first[gaps[0]].shape[0] if isinstance(first, dict) else first.shape[0] // lax.axis_size("seq")
    widths = [weight.shape[1 if across else 0] for _, weight, across in terms]
    n_term, n_gap = len(terms), len(gaps)

    def body(at, *refs):
        ins, outs = refs[: len(arrays)], refs[len(arrays) : len(arrays) + n_gap]
        scratch = refs[len(arrays) + n_gap :]
        xs, ws, stages, sems = scratch[:n_term], scratch[n_term : 2 * n_term], scratch[2 * n_term : -1], scratch[-1]
        loads = Loads(sems)
        for (x, weight, across), (start, count, by_gap), x_ref, w_ref in zip(terms, picks, xs, ws):
            for n, gap in enumerate(gaps):
                if by_gap:
                    source = ins[start + n]
                else:
                    source = ins[start].at[pl.ds(block_row(at, gap, T), T)]
                loads.add("x", source, x_ref.at[n])
            weight.load(loads, "w", at, ins[start + count : start + count + len(weight.arrays)], w_ref)
        loads.wait("x")
        loads.wait("w")
        for n in range(n_gap):
            half = D // 2
            for c in range(2):
                total = None
                for (_, _, across), x_ref, w_ref in zip(terms, xs, ws):
                    cut = slice(c * half, (c + 1) * half)
                    if across:
                        part = dot(x_ref[n], w_ref[cut, :], ((1,), (1,)))
                    else:
                        part = dot(x_ref[n], w_ref[:, cut], ((1,), (0,)))
                    total = part if total is None else total + part
                stages[n][:, c * half : (c + 1) * half] = total.astype(stages[n].dtype)
            loads.add("out", stages[n], outs[n])
        loads.wait("out")

    dtypes = [bf16 if gap & 1 else f32 for gap in gaps]
    outs = call(
        body,
        info,
        arrays,
        [like((T, D), dtype) for dtype in dtypes],
        [pltpu.VMEM((n_gap, T, width), bf16) for width in widths]
        + [pltpu.VMEM(weight.shape, bf16) for _, weight, _ in terms]
        + [pltpu.VMEM((T, D), dtype) for dtype in dtypes]
        + [pltpu.SemaphoreType.DMA((sum(w.copies for _, w, _ in terms) + (n_term + 1) * n_gap,))],
        name=name,
        after=after,
        cost=2 * n_gap * T * D * sum(widths),
    )
    return dict(zip(gaps, outs))


def feed_forward(info, hidden, cot, up, down, gaps, after=()):
    n_gap = len(gaps)
    T = hidden[0].shape[0]
    FW = up.shape[1]
    n_up, n_down = len(up.arrays), len(down.arrays)
    arrays = [*(hidden[gap] for gap in gaps), *(cot[gap] for gap in gaps), *up.arrays, *down.arrays]

    def body(at, *refs):
        ins, outs = refs[: len(arrays)], refs[len(arrays) : len(arrays) + 3 * n_gap]
        x, g, w_up, w_down, acts, grads, *stages, sems = refs[len(arrays) + 3 * n_gap :]
        loads = Loads(sems)
        up.load(loads, "up", at, ins[2 * n_gap : 2 * n_gap + n_up], w_up)
        for n in range(n_gap):
            loads.add(("x", n), ins[n], x.at[n])
        down.load(loads, "down", at, ins[2 * n_gap + n_up :], w_down)
        for n in range(n_gap):
            loads.add(("g", n), ins[n_gap + n], g.at[n])
        loads.wait("up")
        for n in range(n_gap):
            loads.wait(("x", n))
            pre = dot(x[n], w_up[...], ((1,), (0,)))
            below = 0.5 * (1.0 + lax.erf(pre * 0.5**0.5))
            acts[n] = (pre * below).astype(bf16)
            loads.add("out", acts.at[n], outs[n])
            slope = below + pre * jnp.exp(-0.5 * pre * pre) * (0.5 / jnp.pi) ** 0.5
            if n == 0:
                loads.wait("down")
            loads.wait(("g", n))
            grads[n] = (dot(g[n], w_down[...], ((1,), (1,))) * slope).astype(bf16)
            loads.add("out", grads.at[n], outs[n_gap + n])
            half = D // 2
            for c in range(2):
                cut = slice(c * half, (c + 1) * half)
                stages[n][:, cut] = dot(grads[n], w_up[cut, :], ((1,), (1,))).astype(stages[n].dtype)
            loads.add("out", stages[n], outs[2 * n_gap + n])
        loads.wait("out")

    dtypes = [bf16 if gap & 1 else f32 for gap in gaps]
    outs = call(
        body,
        info,
        arrays,
        [like((T, FW), bf16)] * (2 * n_gap) + [like((T, D), dtype) for dtype in dtypes],
        [pltpu.VMEM((n_gap, T, D), bf16)] * 2
        + [pltpu.VMEM(up.shape, bf16), pltpu.VMEM(down.shape, bf16)]
        + [pltpu.VMEM((n_gap, T, FW), bf16)] * 2
        + [pltpu.VMEM((T, D), dtype) for dtype in dtypes]
        + [pltpu.SemaphoreType.DMA((up.copies + down.copies + 5 * n_gap,))],
        name="feed_forward",
        after=after,
        cost=6 * n_gap * T * D * FW,
    )
    return [dict(zip(gaps, outs[n * n_gap : (n + 1) * n_gap])) for n in range(3)]


class Term:
    def __init__(self, x, y, kind=1, shards=False, ordered=True):
        self.x, self.y, self.kind, self.shards, self.ordered = x, y, kind, shards, ordered
        some = x[0] if isinstance(x, dict) else x
        other = y[0] if isinstance(y, dict) else y
        self.tokens = some.shape[0] * (len(x) if isinstance(x, dict) else 1)
        self.columns = some.shape[1] // lax.axis_size("dp")
        self.rows, self.width = self.columns * kind, other.shape[1] // kind
        self.wide = other.shape[1]
        self.xs = list(x.values()) if isinstance(x, dict) else [x]
        self.ys = list(y.values()) if isinstance(y, dict) else [y]
        self.whole = self.columns % 128 != 0
        if self.whole:
            product = dot(self.rows_of(x), self.rows_of(y), ((0,), (0,)))
            self.xs, self.ys = [product.astype(bf16)], []

    def rows_of(self, held):
        if not isinstance(held, dict):
            return held
        rows = held[0].shape[0]
        out = jnp.zeros((len(held) * rows, held[0].shape[1]), bf16)
        for gap, part in held.items():
            start = (lax.axis_index("seq") ^ gap if self.ordered else gap) * rows
            out = lax.dynamic_update_slice_in_dim(out, part, start, 0)
        return out

    def spread(self, at, which, refs, target, cols=None):
        held = self.x if which == "x" else self.y
        for gap, ref in zip(held if isinstance(held, dict) else [None], refs):
            source = ref if cols is None else ref.at[:, cols]
            if gap is None:
                yield source, target
                continue
            rows = ref.shape[0]
            start = block_row(at, gap, rows) if self.ordered else gap * rows
            yield source, target.at[pl.ds(start, rows)]


class Scatter:
    def __init__(self, info, terms, name):
        self.info, self.terms, self.name = info, terms, name
        self.size = lax.axis_size("dp")
        self.ahead, self.back = ring_moves(self.size)
        self.rows = terms[0].rows
        self.cols = sum(term.width for term in terms)
        self.hop = 0
        self.last = ()

    def pieces(self, which, got, write, outs, after=()):
        terms, n_got, n_out, n_w = self.terms, len(got), len(outs), len(which)
        arrays = [a for term in terms for a in (*term.xs, *term.ys)]

        def body(at, *refs):
            ins, recvs = refs[: len(arrays)], refs[len(arrays) : len(arrays) + n_got]
            results = refs[len(arrays) + n_got : len(arrays) + n_got + n_out]
            scratch, sems = refs[len(arrays) + n_got + n_out : -1], refs[-1]
            held = scratch[:n_got]
            buffers = scratch[n_got:]
            loads = Loads(sems)
            start = 0
            for i, term in enumerate(terms):
                x_refs = ins[start : start + len(term.xs)]
                y_refs = ins[start + len(term.xs) : start + len(term.xs) + len(term.ys)]
                start += len(term.xs) + len(term.ys)
                y_buf, *x_bufs = buffers[i * (1 + n_w) : (i + 1) * (1 + n_w)]
                for n, k in enumerate(which):
                    place = at[1 + k + (self.size if term.shards else 0)]
                    cols = pl.ds(pl.multiple_of(place * term.columns, term.columns), term.columns)
                    if term.whole:
                        loads.add((i, n), x_refs[0].at[cols], x_bufs[n])
                        continue
                    for source, target in term.spread(at, "x", x_refs, x_bufs[n], cols):
                        loads.add((i, n), source, target)
                for source, target in term.spread(at, "y", y_refs, y_buf) if y_refs else ():
                    loads.add((i, 0), source, target)
            for source, target in zip(recvs, held):
                loads.add("got", source, target)
            loads.wait("got")
            column = 0
            for i, term in enumerate(terms):
                y_buf, *x_bufs = buffers[i * (1 + n_w) : (i + 1) * (1 + n_w)]
                for n in range(n_w):
                    loads.wait((i, n))
                    for c in range(term.kind):
                        cols = slice(c * term.width, (c + 1) * term.width)
                        if term.whole:
                            values = x_bufs[n][:, cols].astype(f32)
                        else:
                            values = dot(x_bufs[n][...], y_buf[:, cols], ((0,), (0,)))
                        write(n, c * term.columns, term.columns, column, values, held, results)
                column += term.width

        scratch = [pltpu.VMEM(x.shape, x.dtype) for x in got]
        for term in terms:
            scratch += [pltpu.VMEM((8, 128) if term.whole else (term.tokens, term.wide), bf16)]
            shape = (term.columns, term.wide) if term.whole else (term.tokens, term.columns)
            scratch += [pltpu.VMEM(shape, bf16)] * n_w
        copies = n_got + sum(n_w * len(t.xs) + len(t.ys) for t in terms)
        return call(
            body,
            self.info,
            [*arrays, *got],
            outs,
            [*scratch, pltpu.SemaphoreType.DMA((copies,))],
            in_specs=[ANY] * (len(arrays) + n_got),
            out_specs=[VMEM] * n_out,
            name=self.name,
            after=after,
            cost=2 * n_w * sum(t.tokens * t.columns * t.wide for t in terms),
        )

    def step(self, *after):
        m, rows, half = self.size // 2, self.rows, self.rows // 2
        k = m - self.hop
        self.hop += 1

        def write(n, row, count, column, values, got, outs):
            width = values.shape[1]
            for side in range(2) if k == m else [n]:
                for lo, hi in ((0, half), (half, rows)):
                    low, high = max(row, lo), min(row + count, hi)
                    if low >= high or (k == m and lo != side * half):
                        continue
                    part = values[low - row : high - row]
                    cols = slice(column, column + width)
                    if k < m - 1:
                        part = part + got[n][low:high, cols].astype(f32)
                    elif k == m - 1 and lo == n * half:
                        part = part + got[n][low - lo : high - lo, cols].astype(f32)
                    at = lo if k == m else 0
                    outs[side][low - at : high - at, cols] = part.astype(bf16)

        shape = like((half if k == m else rows, self.cols), bf16)
        which = [m] if k == m else [k, self.size - k]
        a, b = self.pieces(which, self.last, write, [shape, shape], after)
        self.sent = (a, b)
        self.last = (lax.ppermute(a, "dp", self.back), lax.ppermute(b, "dp", self.ahead))
        return self

    def own(self, widths, dtypes, after=()):
        while self.hop < self.size // 2:
            self.step()

        def write(n, row, count, column, values, got, outs):
            width = values.shape[1]
            total = values
            for ref in got:
                total = total + ref[row : row + count, column : column + width].astype(f32)
            start = 0
            for out, wide in zip(outs, widths):
                low, high = max(start, column), min(start + wide, column + width)
                if low < high:
                    part = total[:, low - column : high - column]
                    out[row : row + count, low - start : high - start] = part.astype(out.dtype)
                start += wide

        outs = [like((self.rows, w), t) for w, t in zip(widths, dtypes)]
        return self.pieces([0], self.last, write, outs, after)


def split_columns(info, proj_in, ffn_up, proj_out, H, QW, VW, FW):
    size = lax.axis_size("seq")
    rows, G = proj_in.shape[0], lax.axis_size("dp")
    FR = FW // G
    aligned = FR % 128 == 0
    if not aligned:
        ffn_up = ffn_up.reshape(rows, G, size, FR).transpose(0, 2, 1, 3).reshape(rows, size * FW)

    def body(at, w_in, w_up, w_out, *outs):
        outs[-1][...] = w_out[...]
        for gap in range(size):
            who = at[0] ^ gap
            qkv, gate, up = outs[3 * gap : 3 * gap + 3]
            for h in range(H):
                for n in range(2):
                    src = pl.multiple_of(n * D + (who * H + h) * DK, DK)
                    qkv[:, (2 * h + n) * DK : (2 * h + n + 1) * DK] = w_in[:, pl.ds(src, DK)]
            qkv[:, 2 * QW :] = w_in[:, pl.ds(pl.multiple_of(2 * D + who * VW, VW), VW)]
            gate[...] = w_in[:, pl.ds(pl.multiple_of(2 * D + VD + who * VW, VW), VW)]
            if not aligned:
                up[...] = w_up[:, pl.ds(pl.multiple_of(who * FW, FW), FW)]
                continue
            for i in range(G):
                src = pl.multiple_of((i * size + who) * FR, FR)
                up[:, i * FR : (i + 1) * FR] = w_up[:, pl.ds(src, FR)]

    outs = [like((rows, 2 * QW + VW), bf16), like((rows, VW), bf16), like((rows, FW), bf16)] * size
    outs = [*outs, like(proj_out.shape, bf16)]
    return call(
        body,
        info,
        [proj_in, ffn_up, proj_out],
        outs,
        in_specs=[VMEM] * 3,
        out_specs=[VMEM] * len(outs),
        name="split_columns",
    )


def join_pieces(info, parts, extra, fold, after=()):
    size = len(parts)
    rows, width = parts[0].shape
    wide = 0 if extra is None else extra.shape[1] // fold

    def body(at, *refs):
        out = refs[-1]
        for gap in range(size):
            out[pl.ds(pl.multiple_of((at[0] ^ gap) * rows, rows), rows), :width] = refs[gap][...]
        if extra is not None:
            short = size * rows // fold
            for c in range(fold):
                out[c * short : (c + 1) * short, width:] = refs[size][:, c * wide : (c + 1) * wide]

    ins = parts if extra is None else [*parts, extra]
    return call(
        body,
        info,
        ins,
        like((size * rows, width + wide), bf16),
        in_specs=[VMEM] * len(ins),
        out_specs=VMEM,
        name="join_pieces",
        after=after,
    )


def exchange_rows(info, x):
    size = lax.axis_size("seq")
    rows = x.shape[0] // size

    def body(at, src, *outs):
        for gap in range(size):
            outs[gap][...] = src[pl.ds(pl.multiple_of((at[0] ^ gap) * rows, rows), rows), :]

    outs = [like((rows, x.shape[1]), x.dtype)] * size
    parts = call(
        body, info, [x], outs, in_specs=[VMEM], out_specs=[VMEM] * size, name="exchange_rows"
    )
    return [part if gap == 0 else swap_seq(part, gap) for gap, part in enumerate(parts)]


def join_in_columns(info, qkvs, gates, H, QW, VW):
    size = len(qkvs)
    rows = qkvs[0].shape[0]

    def body(at, *refs):
        out = refs[-1]
        for gap in range(size):
            who = at[0] ^ gap
            qkv, gate = refs[gap], refs[size + gap]
            for h in range(H):
                for n in range(2):
                    to = pl.multiple_of(n * D + (who * H + h) * DK, DK)
                    part = qkv[:, (2 * h + n) * DK : (2 * h + n + 1) * DK]
                    out[:, pl.ds(to, DK)] = part.astype(f32)
            out[:, pl.ds(pl.multiple_of(2 * D + who * VW, VW), VW)] = qkv[:, 2 * QW :].astype(f32)
            to = pl.multiple_of(2 * D + VD + who * VW, VW)
            out[:, pl.ds(to, VW)] = gate[...].astype(f32)

    ins = [*qkvs, *gates]
    return call(
        body,
        info,
        ins,
        like((rows, 2 * D + 2 * VD), f32),
        in_specs=[VMEM] * len(ins),
        out_specs=VMEM,
        name="join_in_columns",
    )


def join_up_columns(info, ups, G, after=()):
    size = len(ups)
    rows, FW = ups[0].shape
    FR = FW // G
    aligned = FR % 128 == 0

    def body(at, *refs):
        out = refs[-1]
        for gap in range(size):
            who = at[0] ^ gap
            if not aligned:
                to = pl.multiple_of(who * FW, FW)
                out[:, pl.ds(to, FW)] = refs[gap][...].astype(f32)
                continue
            for i in range(G):
                to = pl.multiple_of((i * size + who) * FR, FR)
                out[:, pl.ds(to, FR)] = refs[gap][:, i * FR : (i + 1) * FR].astype(f32)

    out = call(
        body,
        info,
        ups,
        like((rows, size * FW), f32),
        in_specs=[VMEM] * size,
        out_specs=VMEM,
        name="join_up_columns",
        after=after,
    )
    if aligned:
        return out
    return out.reshape(rows, size, G, FR).transpose(0, 2, 1, 3).reshape(rows, size * FW)


def decays(log_decay, T):
    step = lax.broadcasted_iota(jnp.int32, (T, 1), 0).astype(f32)
    decay_query = jnp.exp((step + 1.0) * log_decay)
    decay_key = jnp.exp((T - 1.0 - step) * log_decay)
    row = lax.broadcasted_iota(jnp.int32, (T, T), 0)
    column = lax.broadcasted_iota(jnp.int32, (T, T), 1)
    gap = (row - column).astype(f32)
    lower = row >= column
    mask = jnp.where(lower, jnp.exp(jnp.where(lower, gap, 0.0) * log_decay), 0.0)
    return decay_query, decay_key, mask


def turn(u, cosine, sine):
    a, c = u[:, :HALF], u[:, HALF:]
    return jnp.concatenate([a * cosine - c * sine, a * sine + c * cosine], axis=1)


def centre(retained):
    average = jnp.mean(retained, axis=-1, keepdims=True)
    centred = retained - average
    spread = jnp.mean(centred * centred, axis=-1, keepdims=True)
    inverse = lax.rsqrt(jnp.maximum(spread, 0.25) + 1e-05)
    return centred, spread, inverse


def retention_forward(info, logs, keep, qk, v, gate, cosine, sine, S, T, H, after=()):
    TG = S * T

    def body(_, logs_ref, keep_ref, qk_ref, v_ref, g_ref, cos_ref, sin_ref, *outs):
        mixed, qk_out, retained_out, state_out, scores_out = outs
        log_decay = logs_ref[pl.program_id(0)]
        decay_query, decay_key, mask = decays(log_decay, T)
        block_decay = jnp.exp(jnp.full((1, 1), T * log_decay, f32))
        carry = jnp.zeros((DK, DV), f32)
        for b in range(S):
            rows = pl.ds(b * T, T)
            co, si = cos_ref[rows], sin_ref[rows]
            q = turn(qk_ref[rows, :DK], co, si).astype(bf16)
            k = (turn(qk_ref[rows, DK:], co, si) * DK ** (-0.5)).astype(bf16)
            qk_out[rows, :DK] = q
            qk_out[rows, DK:] = k
            value = v_ref[rows]
            scores = (dot(q, k, ((1,), (1,))) * mask).astype(bf16)
            scores_out[0, b] = scores
            state = keep_ref[b] * carry
            state_in = state.astype(bf16)
            state_out[0, b] = state_in
            query_decay = (q.astype(f32) * decay_query).astype(bf16)
            key_decay = (k.astype(f32) * decay_key).astype(bf16)
            retained = dot(scores, value, ((1,), (0,))) + dot(query_decay, state_in, ((1,), (0,)))
            retained_out[rows] = retained
            carry = block_decay * state + dot(key_decay, value, ((0,), (0,)))
            centred, _, inverse = centre(retained)
            g = g_ref[rows]
            mixed[rows] = (g * jax.nn.sigmoid(g) * (centred * inverse)).astype(bf16)

    smem = pl.BlockSpec(memory_space=pltpu.SMEM)
    once = lambda width: pl.BlockSpec((TG, width), lambda h, _: (0, 0))
    head = lambda width: pl.BlockSpec((TG, width), lambda h, _: (0, h))
    return call(
        body,
        info,
        [logs, keep, qk, v, gate, cosine, sine],
        [
            like((TG, H * DV), bf16),
            like((TG, 2 * H * DK), bf16),
            like((TG, H * DV), f32),
            like((H, S, DK, DV), bf16),
            like((H, S, T, T), bf16),
        ],
        grid=(H,),
        in_specs=[smem, smem, head(2 * DK), head(DV), head(DV), once(HALF), once(HALF)],
        out_specs=[
            head(DV),
            head(2 * DK),
            head(DV),
            pl.BlockSpec((1, S, DK, DV), lambda h, _: (h, 0, 0, 0)),
            pl.BlockSpec((1, S, T, T), lambda h, _: (h, 0, 0, 0)),
        ],
        name="retention_forward",
        after=after,
        cost=2 * H * S * T * T * (DK + DV) + 4 * H * S * T * DK * DV,
    )


def retention_backward(info, logs, keep, grad_mixed, gate, retained, qk, v, states, scores, cosine, sine, S, T, H, after=()):
    TG = S * T

    def body(_, logs_ref, keep_ref, gm_ref, g_ref, r_ref, qk_ref, v_ref, state_ref, scores_ref, cos_ref, sin_ref, *outs):
        qk_grad, v_grad, g_grad = outs
        log_decay = logs_ref[pl.program_id(0)]
        decay_query, decay_key, mask = decays(log_decay, T)
        block_decay = jnp.exp(jnp.full((1, 1), T * log_decay, f32))
        later = jnp.zeros((DK, DV), f32)
        for b in reversed(range(S)):
            rows = pl.ds(b * T, T)
            gm, g = gm_ref[rows], g_ref[rows]
            centred, spread, inverse = centre(r_ref[rows])
            sig = jax.nn.sigmoid(g)
            swish = g * sig
            normed = centred * inverse
            g_grad[rows] = (gm * normed * (sig + swish * (1.0 - sig))).astype(bf16)
            grad_normed = gm * swish
            passes = jnp.where(spread > 0.25, 1.0, jnp.where(spread == 0.25, 0.5, 0.0))
            pull = jnp.sum(grad_normed * centred, axis=-1, keepdims=True)
            pull = pull * (-inverse * inverse * inverse / DV) * passes
            grad_centred = grad_normed * inverse + pull * centred
            grad_ret = grad_centred - jnp.mean(grad_centred, axis=-1, keepdims=True)
            grad_ret = grad_ret.astype(bf16)
            q, k, value = qk_ref[rows, :DK], qk_ref[rows, DK:], v_ref[rows]
            query_decay = (q.astype(f32) * decay_query).astype(bf16)
            key_decay = (k.astype(f32) * decay_key).astype(bf16)
            grad_raw = (dot(grad_ret, value, ((1,), (1,))) * mask).astype(bf16)
            local = later.astype(bf16)
            grad_q = dot(grad_raw, k, ((1,), (0,)))
            grad_q = grad_q + decay_query * dot(grad_ret, state_ref[0, b], ((1,), (1,)))
            grad_k = dot(grad_raw, q, ((0,), (0,)))
            grad_k = grad_k + decay_key * dot(value, local, ((1,), (1,)))
            grad_v = dot(scores_ref[0, b], grad_ret, ((0,), (0,)))
            grad_v = grad_v + dot(key_decay, local, ((1,), (0,)))
            co, si = cos_ref[rows], -sin_ref[rows]
            qk_grad[rows, :DK] = turn(grad_q, co, si).astype(bf16)
            qk_grad[rows, DK:] = turn(grad_k * DK ** (-0.5), co, si).astype(bf16)
            v_grad[rows] = grad_v.astype(bf16)
            if b > 0:
                here = dot(query_decay, grad_ret, ((0,), (0,)))
                later = keep_ref[b] * (here + block_decay * later)

    smem = pl.BlockSpec(memory_space=pltpu.SMEM)
    once = lambda width: pl.BlockSpec((TG, width), lambda h, _: (0, 0))
    head = lambda width: pl.BlockSpec((TG, width), lambda h, _: (0, h))
    return call(
        body,
        info,
        [logs, keep, grad_mixed, gate, retained, qk, v, states, scores, cosine, sine],
        [like((TG, 2 * H * DK), bf16), like((TG, H * DV), bf16), like((TG, H * DV), bf16)],
        grid=(H,),
        in_specs=[
            smem,
            smem,
            head(DV),
            head(DV),
            head(DV),
            head(2 * DK),
            head(DV),
            pl.BlockSpec((1, S, DK, DV), lambda h, _: (h, 0, 0, 0)),
            pl.BlockSpec((1, S, T, T), lambda h, _: (h, 0, 0, 0)),
            once(HALF),
            once(HALF),
        ],
        out_specs=[head(2 * DK), head(DV), head(DV)],
        name="retention_backward",
        after=after,
        cost=4 * H * S * T * T * (DK + DV) + 8 * H * S * T * DK * DV,
    )


def local(
    layer_in,
    out_grad,
    seq_start,
    norm1_gain,
    norm1_shift,
    proj_in,
    proj_out,
    norm2_gain,
    norm2_shift,
    ffn_up,
    ffn_down,
):
    S, G = lax.axis_size("seq"), lax.axis_size("dp")
    me = lax.axis_index("seq")
    T = layer_in.shape[0]
    TG = S * T
    H = HEADS // S
    QW, VW = H * DK, H * DV
    FW = G * ffn_down.shape[0]
    fold = S // 2
    info = make_info()

    vectors = jnp.stack([norm1_gain, norm1_shift, norm2_gain, norm2_shift])
    norms, norms_dp = gather_all(vectors)
    norms = norms.transpose(1, 0, 2).reshape(4, 1, D).astype(f32)
    gain_one, shift_one, gain_two, shift_two = norms

    to_rank = [(j * G + t, shard_place(t, G) * S + j) for j in range(S) for t in range(G)]
    *parts, out_shard = split_columns(info, proj_in, ffn_up, proj_out, H, QW, VW, FW)
    out_piece = lax.ppermute(out_shard, BOTH, to_rank)

    def exchanged(own, *after):
        return [own[0]] + [
            swap_seq(tie(x, *after) if after else x, gap) for gap, x in enumerate(own) if gap
        ]

    qkv_parts = exchanged(parts[0::3])
    qkv_ring = Gather(join_pieces(info, qkv_parts, None, fold)).step()
    (normed_one,) = norm_forward(layer_in, gain_one, shift_one, (), (qkv_ring.got[0],))
    hidden_one = gather_seq(normed_one)
    early = (*qkv_ring.last, hidden_one[S // 2])
    gate_parts, up_parts = exchanged(parts[1::3], *early), exchanged(parts[2::3], *early)
    qkv_ring.step()
    cot = gather_seq(tie(out_grad, *qkv_ring.last))
    qkv_ring.step().step()
    gate_piece = join_pieces(info, gate_parts, None, fold, qkv_ring.sent)
    gate_ring = Gather(gate_piece).step().step()
    out_ring = Gather(tie(out_piece, *gate_ring.sent)).step()

    factor = jnp.power(10000.0, -jnp.arange(HALF, dtype=f32) / (HALF - 1))
    angles = jnp.arange(TG, dtype=f32)[:, None] * factor[None, :]
    cosine, sine = jnp.cos(angles), jnp.sin(angles)
    log_all = jnp.log(1.0 - jnp.exp2(-5.0 - jnp.arange(HEADS, dtype=f32)))
    logs = lax.dynamic_slice_in_dim(log_all, me * H, H)
    keep = 1.0 - seq_start[0].astype(f32)

    w_qkv = Weight(qkv_ring)
    qk_pre, values = tokens_times(
        info,
        hidden_one,
        w_qkv,
        [(0, 2 * QW, f32), (2 * QW, VW, bf16)],
        False,
        "project_qkv",
        (*gate_ring.sent, *out_ring.sent, cosine, sine, *cot.values()),
    )
    w_qk = Weight(qkv_ring, 1, 0, 2 * QW)
    w_v = Weight(qkv_ring, 1, 2 * QW, VW)
    out_ring.step()
    w_g = Weight(gate_ring)
    ffn_ring = Gather(join_pieces(info, up_parts, ffn_down, fold, out_ring.sent)).step()
    (gate_pre,) = tokens_times(
        info, hidden_one, w_g, [(0, VW, f32)], False, "project_gate", ffn_ring.sent
    )
    mixed, qk, retained, states, scores = retention_forward(
        info, logs, keep, qk_pre, values, gate_pre, cosine, sine, S, T, H, out_ring.step().step().sent
    )
    w_out = Weight(out_ring, shards=True)
    odd, even = [g for g in reversed(range(S)) if g & 1], [g for g in reversed(range(S)) if not g & 1]
    ffn_ring.step()
    attn, attn_got = partial_rows(info, [(mixed, w_out, False)], odd, "attn_odd", ffn_ring.sent), {}
    swap_odd(attn, attn_got)
    attn |= partial_rows(info, [(mixed, w_out, False)], even, "attn_even", (attn[odd[-1]],))
    attn, attn_sent = scatter_seq(attn, attn_got)
    ffn_ring.step()
    middle, normed_two = norm_forward(layer_in, gain_two, shift_two, attn, ffn_ring.sent)
    ffn_ring.step()
    hidden_two = gather_seq(normed_two)
    w_up = Weight(ffn_ring, 1, 0, FW)
    w_down = Weight(ffn_ring, fold, FW, 2 * D // S)
    near, far = [1, 0], list(reversed(range(2, S)))
    active, grad_up, grad_two = feed_forward(info, hidden_two, cot, w_up, w_down, near)
    two_got = {}
    swap_odd(grad_two, two_got)
    more = feed_forward(info, hidden_two, cot, w_up, w_down, far, (grad_two[0],))
    swap_odd(more[2], two_got)
    for whole, extra in zip((active, grad_up, grad_two), more):
        whole |= extra

    grad_two, two_sent = scatter_seq(grad_two, two_got)
    order = sorted(active)
    active, grad_up, cot, hidden_two, hidden_one = (
        {gap: x[gap] for gap in order} for x in (active, grad_up, cot, hidden_two, hidden_one)
    )
    ffn_sum = Scatter(
        info,
        [Term(hidden_two, grad_up, ordered=False), Term(active, cot, fold, ordered=False)],
        "ffn_hop",
    ).step(two_sent)
    down = partial_rows(info, [(active, w_down, False)], odd + even, "down", ffn_sum.sent)
    down_got = {}
    swap_odd(down, down_got)
    grad_middle, grad_attn, two_sums = norm_backward(
        middle, gain_two, out_grad, grad_two, (f32, bf16), (down[0],)
    )

    ffn_sum.step(grad_attn)
    grad_attn = gather_seq(grad_attn, *ffn_sum.sent)
    (grad_mixed,) = tokens_times(info, grad_attn, w_out, [(0, VW, f32)], True, "grad_mixed")
    ffn_sum.step(grad_mixed)
    down, down_sent = scatter_seq(down, down_got, ffn_sum.sent)
    grad_qk, grad_v, grad_g = retention_backward(
        info, logs, keep, grad_mixed, gate_pre, retained, qk, values, states, scores, cosine, sine, S, T, H,
        (*ffn_sum.sent, down_sent),
    )
    gate_sum = Scatter(
        info, [Term(hidden_one, grad_g), Term(mixed, grad_attn, fold, True)], "gate_hop"
    ).step(grad_g)
    ffn_sum.step(*gate_sum.sent)
    qkv_sum = Scatter(info, [Term(hidden_one, grad_qk), Term(hidden_one, grad_v)], "qkv_hop")
    qkv_sum.step(*ffn_sum.sent)
    terms_one = [(grad_g, w_g, True), (grad_v, w_v, True), (grad_qk, w_qk, True)]
    grad_one, one_got = partial_rows(info, terms_one, odd, "grad_one_odd", qkv_sum.sent), {}
    swap_odd(grad_one, one_got)
    gate_sum.step(grad_one[odd[-1]])
    grad_one |= partial_rows(info, terms_one, even, "grad_one_even", gate_sum.sent)
    grad_one, one_sent = scatter_seq(grad_one, one_got)
    qkv_sum.step(one_sent)
    layer_out = add_up([*down, middle], bf16, qkv_sum.sent)
    up_own, down_own = ffn_sum.own((FW, 2 * D // S), (bf16, f32), (layer_out,))
    up_parts = exchange_rows(info, up_own)
    gate_sum.step(up_parts[0])
    in_grad, one_sums = norm_backward(
        layer_in, gain_one, grad_middle, grad_one, (bf16,), gate_sum.sent
    )
    norm_terms = jnp.stack([one_sums[0], one_sums[1], two_sums[0], two_sums[1]])
    down_grad = jnp.concatenate(jnp.split(tie(down_own, in_grad), fold, axis=0), axis=1)
    qkv_sum.step(in_grad)
    gate_sum.step(*qkv_sum.sent)
    up_grad = join_up_columns(info, up_parts, G, gate_sum.sent)
    norm_afters = [qkv_sum.sent]
    qkv_sum.step(up_grad)
    g_own, out_own = gate_sum.own((VW, 2 * D // S), (bf16, bf16), qkv_sum.sent)
    g_parts = exchange_rows(info, g_own)
    out_grad_w = lax.ppermute(out_own, BOTH, [(b, a) for a, b in to_rank])
    norm_grads = scatter_all(
        norm_terms.reshape(4, G * S, -1).transpose(1, 0, 2),
        [*norm_afters, qkv_sum.sent, (g_own,)],
    )
    out_grad_w = jnp.concatenate(jnp.split(out_grad_w, fold, axis=0), axis=1).astype(f32)
    (qkv_own,) = qkv_sum.own((2 * QW + VW,), (bf16,))
    in_grad_w = join_in_columns(info, exchange_rows(info, qkv_own), g_parts, H, QW, VW)
    return (
        layer_out,
        in_grad,
        norm_grads[0],
        norm_grads[1],
        in_grad_w,
        out_grad_w,
        norm_grads[2],
        norm_grads[3],
        up_grad,
        down_grad,
    )


def solution(mesh):
    rows, vector = P(BOTH, None), P(BOTH)
    in_specs = (rows, rows, P("dp", None), vector, vector, rows, rows, vector, vector, rows, rows)
    out_specs = (rows, rows, vector, vector, rows, rows, vector, vector, rows, rows)
    return jax.shard_map(local, mesh=mesh, in_specs=in_specs, out_specs=out_specs, check_vma=False)
```

time: 1140 us -> 804 us (0.71)
  waiting for transfers between devices: 620 us -> 306 us
  Pallas kernels: 0 us -> 311 us
  matrix products: 132 us -> 0 us
  blocking collectives: 130 us -> 0 us
  starting transfers between devices: 26.8 us -> 116 us
  local copies, waits for them, and re-layouts: 127 us -> 44.1 us
  other arithmetic: 77.9 us -> 9.19 us
  between operations: 16.2 us -> 2.14 us
    pallas_call x0 -> x58, Pallas kernels: none -> 311 us  [the longest x36 279 us: call(): pl.pallas_call(inner, out_shape=outs, grid_spec=spec, name=name, cost_est...]
    reduce_scatter x4 -> x0, waiting for transfers between devices: 216 us -> none  [scatter_dp(): lax.psum_scatter(x.astype(bf16), 'dp', scatter_dimension=0, tiled=True)]
    ppermute x18 -> x110, waiting for transfers between devices: 150 us -> 306 us  [the longest x42 106 us: swap_seq(): return lax.ppermute(x, 'seq', [(i, i ^ gap) for i in range(size)])]
    unnamed x10 -> x0, waiting for transfers between devices: 133 us -> none
    dot_general x24 -> x0, matrix products: 132 us -> none  [the longest x12 120 us: dot(): return lax.dot_general(a, b, (dims, ((), ())), preferred_element_type=f32)]
    all_gather x1 -> x0, blocking collectives: 106 us -> none  [local(): lax.all_gather(jnp.stack([norm1_gain, norm1_shift, norm2_gain, norm2_shif...]
    ppermute x18 -> x110, starting transfers between devices: 13.1 us -> 116 us  [the longest x32 50.2 us: step(): a, b = (lax.ppermute(a, 'dp', self.ahead), lax.ppermute(b, 'dp', self.back))]
    all_gather x4 -> x0, waiting for transfers between devices: 99.7 us -> none  [gather_dp(): return lax.all_gather(x, 'dp', axis=0, tiled=True)]
  transfers between devices with their start and end apart: 30 -> 110, of which waited for: 17 -> 41; matrix products, arithmetic and copies ran while one was open for 24% -> 3% of each run, Pallas kernels for 0% -> 35%
where the time goes in v2:
time: 804 us; the launch traced here: 789 us
  Pallas kernels  311 us (39%)
  waiting for transfers between devices  306 us (38%)
  starting transfers between devices  116 us (14%)
  local copies, waits for them, and re-layouts  44.1 us (5%)
  other arithmetic  9.19 us (1%)
    pallas_call x36, Pallas kernels, call(): pl.pallas_call(inner, out_shape=outs, grid_spec=spec, name=name, cost_est...  279 us
    ppermute x42, waiting for transfers between devices, swap_seq(): return lax.ppermute(x, 'seq', [(i, i ^ gap) for i in range(size)])  106 us
    ppermute x32, waiting for transfers between devices, step(): a, b = (lax.ppermute(a, 'dp', self.ahead), lax.ppermute(b, 'dp', self.back))  85.2 us
    ppermute x32, starting transfers between devices, step(): a, b = (lax.ppermute(a, 'dp', self.ahead), lax.ppermute(b, 'dp', self.back))  50.2 us
    ppermute x10, waiting for transfers between devices, swap_all(): return lax.ppermute(x, BOTH, [(i, i ^ gap) for i in range(size)])  44.8 us
    ppermute x12, waiting for transfers between devices, step(): lax.ppermute(a, 'dp', self.back)  44.6 us
    pallas_call x9, Pallas kernels, plain(): pl.pallas_call(inner, out_shape=outs, grid=grid, in_specs=[*in_specs, *[A...  32.4 us
    unnamed x191, local copies, waits for them, and re-layouts  27.4 us
  transfers between devices with their start and end apart: 110, of which 41 were waited for; matrix products, arithmetic and copies ran while one was open for 3% of the time, Pallas kernels for 35%

profile of v2, /device:TPU:0, one launch (start us, length us, event | category | flops | bytes accessed | tf_op | source)
XLA Modules:
  0.0 788.7 jit_solution(11062697436474590301)
XLA Ops:
  9.4 7.2 collective-permute-done.6.refs_2_
  29.1 21.7 %collective-permute-done = bf16[1,1,4,64]{3,0,2,1:T(2,128)(2,1)S(1)} collective-permute-done((bf16[1,1,4,64]{3,0,2,1:T(2,128)(2,1)S(1)}, bf16[1,1,4,64]{3,0,2,1:T(2,128)(2,1)S(1)}, u32[]{:S(2)}, u32[]{:S(2)}) %collective-permute-start) | collective-permute-done | bytes 544 | tf_op jit(solution)/shard_map/ppermute | solution.py:245
  71.5 9.8 %collective-permute-done.14.refs_2_.refs_8_.refs_15_.refs_25_ = bf16[256,2048]{1,0:T(8,128)(2,1)} collective-permute-done((bf16[256,2048]{1,0:T(8,128)(2,1)S(1)}, bf16[256,2048]{1,0:T(8,128)(2,1)}, u32[]{:S(2)}, u32[]{:S(2)}) %collective-permute-start.14) | collective-permute-done | bytes 1048608 | tf_op jit(solution)/shard_map/ppermute | solution.py:330
  83.3 11.3 %collective-permute-done.8.refs_3_.refs_1_.refs_2_.refs_7_ = bf16[256,2048]{1,0:T(8,128)(2,1)S(1)} collective-permute-done((bf16[256,2048]{1,0:T(8,128)(2,1)}, bf16[256,2048]{1,0:T(8,128)(2,1)S(1)}, u32[]{:S(2)}, u32[]{:S(2)}) %collective-permute-start.8) | collective-permute-done | bytes 1048608 | tf_op jit(solution)/shard_map/ppermute | solution.py:78
  118.9 7.2 collective-permute-start.23
  136.3 22.8 %collective-permute-done.35.refs_2_ = bf16[64,1024]{1,0:T(8,128)(2,1)S(1)} collective-permute-done((bf16[64,1024]{1,0:T(8,128)(2,1)}, bf16[64,1024]{1,0:T(8,128)(2,1)S(1)}, u32[]{:S(2)}, u32[]{:S(2)}) %collective-permute-start.35) | collective-permute-done | bytes 131104 | tf_op jit(solution)/shard_map/ppermute | solution.py:78
  166.7 7.5 collective-permute-done.29.refs_8_.refs_5_
  174.2 11.2 %collective-permute-done.38.refs_6_.refs_3_ = bf16[128,2048]{1,0:T(8,128)(2,1)S(1)} collective-permute-done((bf16[128,2048]{1,0:T(8,128)(2,1)}, bf16[128,2048]{1,0:T(8,128)(2,1)S(1)}, u32[]{:S(2)}, u32[]{:S(2)}) %collective-permute-start.38) | collective-permute-done | bytes 524320 | tf_op jit(solution)/shard_map/ppermute | solution.py:330
  200.5 7.5 collective-permute-done.41.refs_5_.refs_8_
  234.7 14.7 %project_qkv.1 = (f32[1024,1024]{1,0:T(8,128)}, bf16[1024,1024]{1,0:T(8,128)(2,1)}) custom-call(s32[17]{0:T(128)} %pad_add_fusion.at, bf16[256,2048]{1,0:T(8,128)(2,1)} %norm_forward.2.refs_0_.refs_5_, bf16[256,2048]{1,0:T(8,128)(2,1)} %copy-done, bf16[256,2048]{1,0:T(8,128)(2,1)} %copy-done.1, bf16[256,2048]{1,0:T(8,128)(2,1)} %copy-done.2, ...), custom_call_target="tpu_custom_call" | custom-call | flops 8589934592 | bytes 18874368 | tf_op jit(solution)/shard_map/project_qkv/pallas_call | solution.py:45
  250.3 10.3 %collective-permute-done.40.refs_6_.refs_9_ = bf16[128,2048]{1,0:T(8,128)(2,1)S(1)} collective-permute-done((bf16[128,2048]{1,0:T(8,128)(2,1)}, bf16[128,2048]{1,0:T(8,128)(2,1)S(1)}, u32[]{:S(2)}, u32[]{:S(2)}) %collective-permute-start.40) | collective-permute-done | bytes 524320 | tf_op jit(solution)/shard_map/ppermute | solution.py:330
  265.0 9.3 %project_gate.1.refs_4_.refs_3_ = f32[1024,1024]{1,0:T(8,128)} custom-call(s32[17]{0:T(128)} %pad_add_fusion.at, bf16[256,2048]{1,0:T(8,128)(2,1)} %norm_forward.2.refs_0_.refs_5_, bf16[256,2048]{1,0:T(8,128)(2,1)} %copy-done, bf16[256,2048]{1,0:T(8,128)(2,1)} %copy-done.1, bf16[256,2048]{1,0:T(8,128)(2,1)} %copy-done.2, ...), custom_call_target="tpu_custom_call" | custom-call | flops 4294967296 | bytes 12582912 | tf_op jit(solution)/shard_map/project_gate/pallas_call | solution.py:45
  274.3 10.1 %retention_forward.1 = (bf16[1024,1024]{1,0:T(8,128)(2,1)}, bf16[1024,1024]{1,0:T(8,128)(2,1)}, f32[1024,1024]{1,0:T(8,128)}, bf16[2,4,256,512]{3,2,1,0:T(8,128)(2,1)}, bf16[2,4,256,256]{3,2,1,0:T(8,128)(2,1)}) custom-call(s32[17]{0:T(128)} %pad_add_fusion.at, f32[2]{0:T(128)} %dynamic_slice.8.refs_0_, f32[4]{0:T(128)} %subtract_bitcast_fusion.refs_1_, ...), custom_call_target="tpu_custom_call" | custom-call | flops 1879048192 | bytes 23068696 | tf_op jit(solution)/shard_map/retention_forward/pallas_call | solution.py:45
  286.0 6.6 attn_odd.1
  295.3 6.9 attn_even.1
  306.2 12.8 %collective-permute-done.51.refs_7_.refs_8_.refs_17_ = bf16[256,2048]{1,0:T(8,128)(2,1)S(1)} collective-permute-done((bf16[256,2048]{1,0:T(8,128)(2,1)}, bf16[256,2048]{1,0:T(8,128)(2,1)S(1)}, u32[]{:S(2)}, u32[]{:S(2)}) %collective-permute-start.51) | collective-permute-done | bytes 1048608 | tf_op jit(solution)/shard_map/ppermute | solution.py:330
  322.5 9.2 %collective-permute-done.49.refs_5_ = bf16[256,2048]{1,0:T(8,128)(2,1)} collective-permute-done((bf16[256,2048]{1,0:T(8,128)(2,1)}, bf16[256,2048]{1,0:T(8,128)(2,1)}, u32[]{:S(2)}, u32[]{:S(2)}) %collective-permute-start.49) | collective-permute-done | bytes 1048608 | tf_op jit(solution)/shard_map/ppermute | solution.py:78
  336.3 8.2 %collective-permute-done.55.refs_10_.refs_19_ = bf16[256,2048]{1,0:T(8,128)(2,1)} collective-permute-done((bf16[256,2048]{1,0:T(8,128)(2,1)S(1)}, bf16[256,2048]{1,0:T(8,128)(2,1)}, u32[]{:S(2)}, u32[]{:S(2)}) %collective-permute-start.55) | collective-permute-done | bytes 1048608 | tf_op jit(solution)/shard_map/ppermute | solution.py:330
  349.0 11.8 %collective-permute-done.52.refs_1_.refs_2_ = bf16[256,2048]{1,0:T(8,128)(2,1)S(1)} collective-permute-done((bf16[256,2048]{1,0:T(8,128)(2,1)}, bf16[256,2048]{1,0:T(8,128)(2,1)S(1)}, u32[]{:S(2)}, u32[]{:S(2)}) %collective-permute-start.52) | collective-permute-done | bytes 1048608 | tf_op jit(solution)/shard_map/ppermute | solution.py:78
  362.8 12.9 %feed_forward.2 = (bf16[256,1024]{1,0:T(8,128)(2,1)}, bf16[256,1024]{1,0:T(8,128)(2,1)}, bf16[256,1024]{1,0:T(8,128)(2,1)}, bf16[256,1024]{1,0:T(8,128)(2,1)}, b...) custom-call(s32[17]{0:T(128)} %pad_add_fusion.at, bf16[256,2048]{1,0:T(8,128)(2,1)} %copy-done.11, ...), custom_call_target="tpu_custom_call" | custom-call | flops 6442450944 | bytes 26214400 | tf_op jit(solution)/shard_map/feed_forward/pallas_call | solution.py:45
  376.7 13.5 %feed_forward.3 = (bf16[256,1024]{1,0:T(8,128)(2,1)}, bf16[256,1024]{1,0:T(8,128)(2,1)}, bf16[256,1024]{1,0:T(8,128)(2,1)}, bf16[256,1024]{1,0:T(8,128)(2,1)}, b...) custom-call(s32[17]{0:T(128)} %pad_add_fusion.at, bf16[256,2048]{1,0:T(8,128)(2,1)} %copy-done.12, ...), custom_call_target="tpu_custom_call" | custom-call | flops 6442450944 | bytes 26214400 | tf_op jit(solution)/shard_map/feed_forward/pallas_call | solution.py:45
  403.5 9.5 %down.1 = (bf16[256,2048]{1,0:T(8,128)(2,1)}, bf16[256,2048]{1,0:T(8,128)(2,1)}, f32[256,2048]{1,0:T(8,128)}, f32[256,2048]{1,0:T(8,128)}) custom-call(s32[17]{0:T(128)} %pad_add_fusion.at, bf16[256,1024]{1,0:T(8,128)(2,1)} %get-tuple-element.126.refs_11_.refs_0_, bf16[256,1024]{1,0:T(8,128)(2,1)} %get-tuple-element.127.refs_9_.refs_1_, ...), custom_call_target="tpu_custom_call" | custom-call | flops 4294967296 | bytes 16777216 | tf_op jit(solution)/shard_map/down/pallas_call | solution.py:45
  413.0 10.2 %collective-permute-done.65.refs_5_ = bf16[256,2048]{1,0:T(8,128)(2,1)S(1)} collective-permute-done((bf16[256,2048]{1,0:T(8,128)(2,1)}, bf16[256,2048]{1,0:T(8,128)(2,1)S(1)}, u32[]{:S(2)}, u32[]{:S(2)}) %collective-permute-start.65) | collective-permute-done | bytes 1048608 | tf_op jit(solution)/shard_map/ppermute | solution.py:78
  432.2 11.3 %collective-permute-done.62.refs_16_ = bf16[128,2048]{1,0:T(8,128)(2,1)S(1)} collective-permute-done((bf16[128,2048]{1,0:T(8,128)(2,1)S(1)}, bf16[128,2048]{1,0:T(8,128)(2,1)S(1)}, u32[]{:S(2)}, u32[]{:S(2)}) %collective-permute-start.62) | collective-permute-done | bytes 524320 | tf_op jit(solution)/shard_map/ppermute | solution.py:675
  446.0 8.6 %ffn_hop.6 = (bf16[256,2048]{1,0:T(8,128)(2,1)}, bf16[256,2048]{1,0:T(8,128)(2,1)}) custom-call(s32[17]{0:T(128)} %pad_add_fusion.at, bf16[256,2048]{1,0:T(8,128)(2,1)} %get-tuple-element.124.refs_1_.refs_0_, bf16[256,2048]{1,0:T(8,128)(2,1)} %copy-done.11, bf16[256,2048]{1,0:T(8,128)(2,1)} %copy-done.10, bf16[256,2048]{1,0:T(8,128)(2,1)} %copy-done.12, ...), custom_call_target="tpu_custom_call" | custom-call | flops 2147483648 | bytes 15728640 | tf_op jit(solution)/shard_map/ffn_hop/pallas_call | solution.py:45
  461.1 9.4 %grad_mixed.1.refs_18_.refs_2_ = f32[1024,1024]{1,0:T(8,128)} custom-call(s32[17]{0:T(128)} %pad_add_fusion.at, bf16[256,2048]{1,0:T(8,128)(2,1)} %get-tuple-element.144.refs_18_.refs_0_.refs_6_, bf16[256,2048]{1,0:T(8,128)(2,1)} %tie.21.refs_1_.refs_7_, bf16[256,2048]{1,0:T(8,128)(2,1)} %copy-done.6, bf16[256,2048]{1,0:T(8,128)(2,1)} %copy-done.7, ...), custom_call_target="tpu_custom_call" | custom-call | flops 4294967296 | bytes 12582912 | tf_op jit(solution)/shard_map/grad_mixed/pallas_call | solution.py:45
  470.5 11.2 %collective-permute-done.66.refs_16_ = bf16[256,2048]{1,0:T(8,128)(2,1)S(1)} collective-permute-done((bf16[256,2048]{1,0:T(8,128)(2,1)}, bf16[256,2048]{1,0:T(8,128)(2,1)S(1)}, u32[]{:S(2)}, u32[]{:S(2)}) %collective-permute-start.66) | collective-permute-done | bytes 1048608 | tf_op jit(solution)/shard_map/ppermute | solution.py:675
  483.4 8.9 %ffn_hop.7 = (bf16[256,2048]{1,0:T(8,128)(2,1)}, bf16[256,2048]{1,0:T(8,128)(2,1)}) custom-call(s32[17]{0:T(128)} %pad_add_fusion.at, bf16[256,2048]{1,0:T(8,128)(2,1)} %get-tuple-element.124.refs_1_.refs_0_, bf16[256,2048]{1,0:T(8,128)(2,1)} %copy-done.11, bf16[256,2048]{1,0:T(8,128)(2,1)} %copy-done.10, bf16[256,2048]{1,0:T(8,128)(2,1)} %copy-done.12, ...), custom_call_target="tpu_custom_call" | custom-call | flops 2147483648 | bytes 16777216 | tf_op jit(solution)/shard_map/ffn_hop/pallas_call | solution.py:45
  499.7 15.6 %retention_backward.1 = (bf16[1024,1024]{1,0:T(8,128)(2,1)}, bf16[1024,1024]{1,0:T(8,128)(2,1)}, bf16[1024,1024]{1,0:T(8,128)(2,1)}) custom-call(s32[17]{0:T(128)} %pad_add_fusion.at, f32[2]{0:T(128)} %dynamic_slice.8.refs_0_, f32[4]{0:T(128)} %subtract_bitcast_fusion.refs_1_, f32[1024,1024]{1,0:T(8,128)} %grad_mixed.1.refs_18_.refs_2_, ...), custom_call_target="tpu_custom_call" | custom-call | flops 3758096384 | bytes 27263000 | tf_op jit(solution)/shard_map/retention_backward/pallas_call | solution.py:45
  524.1 8.9 %ffn_hop.8 = (bf16[256,2048]{1,0:T(8,128)(2,1)}, bf16[256,2048]{1,0:T(8,128)(2,1)}) custom-call(s32[17]{0:T(128)} %pad_add_fusion.at, bf16[256,2048]{1,0:T(8,128)(2,1)} %get-tuple-element.124.refs_1_.refs_0_, bf16[256,2048]{1,0:T(8,128)(2,1)} %copy-done.11, bf16[256,2048]{1,0:T(8,128)(2,1)} %copy-done.10, bf16[256,2048]{1,0:T(8,128)(2,1)} %copy-done.12, ...), custom_call_target="tpu_custom_call" | custom-call | flops 2147483648 | bytes 16777216 | tf_op jit(solution)/shard_map/ffn_hop/pallas_call | solution.py:45
  538.2 14.2 %grad_one_odd.1 = (bf16[256,2048]{1,0:T(8,128)(2,1)}, bf16[256,2048]{1,0:T(8,128)(2,1)}) custom-call(s32[17]{0:T(128)} %pad_add_fusion.at, bf16[1024,1024]{1,0:T(8,128)(2,1)} %get-tuple-element.155.refs_4_.refs_10_.refs_0_, bf16[256,1024]{1,0:T(8,128)(2,1)} %join_pieces.4.refs_4_.refs_1_, ...), custom_call_target="tpu_custom_call" | custom-call | flops 6442450944 | bytes 29360128 | tf_op jit(solution)/shard_map/grad_one_odd/pallas_call | solution.py:45
  555.4 11.9 %collective-permute-done.77.refs_11_ = bf16[128,2048]{1,0:T(8,128)(2,1)S(1)} collective-permute-done((bf16[128,2048]{1,0:T(8,128)(2,1)S(1)}, bf16[128,2048]{1,0:T(8,128)(2,1)S(1)}, u32[]{:S(2)}, u32[]{:S(2)}) %collective-permute-start.77) | collective-permute-done | bytes 524320 | tf_op jit(solution)/shard_map/ppermute | solution.py:675
  568.8 8.6 %gate_hop.6 = (bf16[256,2048]{1,0:T(8,128)(2,1)}, bf16[256,2048]{1,0:T(8,128)(2,1)}) custom-call(s32[17]{0:T(128)} %pad_add_fusion.at, bf16[256,2048]{1,0:T(8,128)(2,1)} %norm_forward.2.refs_0_.refs_5_, bf16[256,2048]{1,0:T(8,128)(2,1)} %copy-done.1, bf16[256,2048]{1,0:T(8,128)(2,1)} %copy-done, bf16[256,2048]{1,0:T(8,128)(2,1)} %copy-done.2, ...), custom_call_target="tpu_custom_call" | custom-call | flops 2147483648 | bytes 15728640 | tf_op jit(solution)/shard_map/gate_hop/pallas_call | solution.py:45
  580.6 14.4 %grad_one_even.1 = (f32[256,2048]{1,0:T(8,128)}, f32[256,2048]{1,0:T(8,128)}) custom-call(s32[17]{0:T(128)} %pad_add_fusion.at, bf16[1024,1024]{1,0:T(8,128)(2,1)} %get-tuple-element.155.refs_4_.refs_10_.refs_0_, bf16[256,1024]{1,0:T(8,128)(2,1)} %join_pieces.4.refs_4_.refs_1_, bf16[256,1024]{1,0:T(8,128)(2,1)} %collective-permute-done.22.refs_1_.refs_13_.refs_5_.refs_2_, ...), custom_call_target="tpu_custom_call" | custom-call | flops 6442450944 | bytes 31457280 | tf_op jit(solution)/shard_map/grad_one_even/pallas_call | solution.py:45
  598.7 8.0 %qkv_hop.6 = (bf16[256,2048]{1,0:T(8,128)(2,1)}, bf16[256,2048]{1,0:T(8,128)(2,1)}) custom-call(s32[17]{0:T(128)} %pad_add_fusion.at, bf16[256,2048]{1,0:T(8,128)(2,1)} %norm_forward.2.refs_0_.refs_5_, bf16[256,2048]{1,0:T(8,128)(2,1)} %copy-done.1, bf16[256,2048]{1,0:T(8,128)(2,1)} %copy-done, bf16[256,2048]{1,0:T(8,128)(2,1)} %copy-done.2, ...), custom_call_target="tpu_custom_call" | custom-call | flops 2147483648 | bytes 15728640 | tf_op jit(solution)/shard_map/qkv_hop/pallas_call | solution.py:45
  608.5 7.6 collective-permute-done.81.refs_10_
  620.2 7.1 ffn_hop.9
  629.9 8.9 %gate_hop.7 = (bf16[256,2048]{1,0:T(8,128)(2,1)}, bf16[256,2048]{1,0:T(8,128)(2,1)}) custom-call(s32[17]{0:T(128)} %pad_add_fusion.at, bf16[256,2048]{1,0:T(8,128)(2,1)} %norm_forward.2.refs_0_.refs_5_, bf16[256,2048]{1,0:T(8,128)(2,1)} %copy-done.1, bf16[256,2048]{1,0:T(8,128)(2,1)} %copy-done, bf16[256,2048]{1,0:T(8,128)(2,1)} %copy-done.2, ...), custom_call_target="tpu_custom_call" | custom-call | flops 2147483648 | bytes 16777216 | tf_op jit(solution)/shard_map/gate_hop/pallas_call | solution.py:45
  649.5 8.4 %qkv_hop.7 = (bf16[256,2048]{1,0:T(8,128)(2,1)}, bf16[256,2048]{1,0:T(8,128)(2,1)}) custom-call(s32[17]{0:T(128)} %pad_add_fusion.at, bf16[256,2048]{1,0:T(8,128)(2,1)} %norm_forward.2.refs_0_.refs_5_, bf16[256,2048]{1,0:T(8,128)(2,1)} %copy-done.1, bf16[256,2048]{1,0:T(8,128)(2,1)} %copy-done, bf16[256,2048]{1,0:T(8,128)(2,1)} %copy-done.2, ...), custom_call_target="tpu_custom_call" | custom-call | flops 2147483648 | bytes 16777216 | tf_op jit(solution)/shard_map/qkv_hop/pallas_call | solution.py:45
  661.5 9.6 %collective-permute-done.95.refs_11_ = bf16[256,2048]{1,0:T(8,128)(2,1)} collective-permute-done((bf16[256,2048]{1,0:T(8,128)(2,1)}, bf16[256,2048]{1,0:T(8,128)(2,1)}, u32[]{:S(2)}, u32[]{:S(2)}) %collective-permute-start.95) | collective-permute-done | bytes 1048608 | tf_op jit(solution)/shard_map/ppermute | solution.py:675
  672.9 8.8 %gate_hop.8 = (bf16[256,2048]{1,0:T(8,128)(2,1)}, bf16[256,2048]{1,0:T(8,128)(2,1)}) custom-call(s32[17]{0:T(128)} %pad_add_fusion.at, bf16[256,2048]{1,0:T(8,128)(2,1)} %norm_forward.2.refs_0_.refs_5_, bf16[256,2048]{1,0:T(8,128)(2,1)} %copy-done.1, bf16[256,2048]{1,0:T(8,128)(2,1)} %copy-done, bf16[256,2048]{1,0:T(8,128)(2,1)} %copy-done.2, ...), custom_call_target="tpu_custom_call" | custom-call | flops 2147483648 | bytes 16777216 | tf_op jit(solution)/shard_map/gate_hop/pallas_call | solution.py:45
  686.7 8.8 %collective-permute-done.85.refs_0_ = f32[16,4,64]{2,1,0:T(4,128)S(1)} collective-permute-done((f32[16,4,64]{2,1,0:T(4,128)S(1)}, f32[16,4,64]{2,1,0:T(4,128)S(1)}, u32[]{:S(2)}, u32[]{:S(2)}) %collective-permute-start.85) | collective-permute-done | bytes 16416 | tf_op jit(solution)/shard_map/ppermute | solution.py:245
  699.4 8.4 %qkv_hop.8 = (bf16[256,2048]{1,0:T(8,128)(2,1)}, bf16[256,2048]{1,0:T(8,128)(2,1)}) custom-call(s32[17]{0:T(128)} %pad_add_fusion.at, bf16[256,2048]{1,0:T(8,128)(2,1)} %norm_forward.2.refs_0_.refs_5_, bf16[256,2048]{1,0:T(8,128)(2,1)} %copy-done.1, bf16[256,2048]{1,0:T(8,128)(2,1)} %copy-done, bf16[256,2048]{1,0:T(8,128)(2,1)} %copy-done.2, ...), custom_call_target="tpu_custom_call" | custom-call | flops 2147483648 | bytes 16777216 | tf_op jit(solution)/shard_map/qkv_hop/pallas_call | solution.py:45
  707.8 7.1 collective-permute-done.88.refs_0_
  717.3 6.9 gate_hop.9
  736.7 14.5 %collective-permute-done.101.refs_10_ = bf16[256,2048]{1,0:T(8,128)(2,1)S(1)} collective-permute-done((bf16[256,2048]{1,0:T(8,128)(2,1)S(1)}, bf16[256,2048]{1,0:T(8,128)(2,1)S(1)}, u32[]{:S(2)}, u32[]{:S(2)}) %collective-permute-start.101) | collective-permute-done | bytes 1048608 | tf_op jit(solution)/shard_map/ppermute | solution.py:675
  753.1 6.6 qkv_hop.9.refs_0_
  766.7 16.9 %collective-permute-done.108.refs_7_ = bf16[64,1024]{1,0:T(8,128)(2,1)S(1)} collective-permute-done((bf16[64,1024]{1,0:T(8,128)(2,1)S(1)}, bf16[64,1024]{1,0:T(8,128)(2,1)S(1)}, u32[]{:S(2)}, u32[]{:S(2)}) %collective-permute-start.108) | collective-permute-done | bytes 131104 | tf_op jit(solution)/shard_map/ppermute | solution.py:78
  (474 shorter events, 283.6 us)
Async XLA Ops:
  25.4 32.7 %collective-permute-start.12 = (bf16[256,2048]{1,0:T(8,128)(2,1)}, bf16[256,2048]{1,0:T(8,128)(2,1)S(1)}, u32[]{:S(2)}, u32[]{:S(2)}) collective-permute-start(bf16[256,2048]{1,0:T(8,128)(2,1)} %join_pieces.3.refs_3_.refs_4_.refs_11_.refs_21_), channel_id=1, source_target_pairs={{4,0},{12,4},{20,12},{28,20},{24,28},{16,24},{8,16},{0,8},{5,1},{1... | collective-permute-start | bytes 3145736 | tf_op jit(solution)/shard_map/ppermute | solution.py:330
  27.0 33.1 %collective-permute-start.11 = (bf16[256,2048]{1,0:T(8,128)(2,1)}, bf16[256,2048]{1,0:T(8,128)(2,1)S(1)}, u32[]{:S(2)}, u32[]{:S(2)}) collective-permute-start(bf16[256,2048]{1,0:T(8,128)(2,1)} %join_pieces.3.refs_3_.refs_4_.refs_11_.refs_21_), channel_id=1, source_target_pairs={{0,4},{4,12},{12,20},{20,28},{28,24},{24,16},{16,8},{8,0},{1,5},{5... | collective-permute-start | bytes 3145736 | tf_op jit(solution)/shard_map/ppermute | solution.py:330
  83.2 43.9 %collective-permute-start.9 = (bf16[256,2048]{1,0:T(8,128)(2,1)}, bf16[256,2048]{1,0:T(8,128)(2,1)S(1)}, u32[]{:S(2)}, u32[]{:S(2)}) collective-permute-start(bf16[256,2048]{1,0:T(8,128)(2,1)} %norm_forward.2.refs_0_.refs_5_), channel_id=1, source_target_pairs={{0,1},{1,0},{2,3},{3,2},{4,5},{5,4},{6,7},{7,6},{8,9},{9,8},{10,11... | collective-permute-start | bytes 3145736 | tf_op jit(solution)/shard_map/ppermute | solution.py:78
  95.6 30.5 %collective-permute-start.24 = (bf16[128,2048]{1,0:T(8,128)(2,1)}, bf16[128,2048]{1,0:T(8,128)(2,1)}, u32[]{:S(2)}, u32[]{:S(2)}) collective-permute-start(bf16[128,2048]{1,0:T(8,128)(2,1)} %get-tuple-element.112), channel_id=1, source_target_pairs={{0,0},{1,8},{2,16},{3,24},{4,4},{5,12},{6,20},{7,28},{8,1},{9,9},{... | collective-permute-start | bytes 1572872 | tf_op jit(solution)/shard_map/ppermute | solution.py:1030
  101.0 60.0 %collective-permute-start.10 = (bf16[256,2048]{1,0:T(8,128)(2,1)}, bf16[256,2048]{1,0:T(8,128)(2,1)S(1)}, u32[]{:S(2)}, u32[]{:S(2)}) collective-permute-start(bf16[256,2048]{1,0:T(8,128)(2,1)} %copy-done), channel_id=1, source_target_pairs={{0,1},{1,0},{2,3},{3,2},{4,5},{5,4},{6,7},{7,6},{8,9},{9,8},{10,11... | collective-permute-start | bytes 3145736 | tf_op jit(solution)/shard_map/ppermute | solution.py:78
  127.2 35.9 %collective-permute-start.26 = (bf16[256,2048]{1,0:T(8,128)(2,1)}, bf16[256,2048]{1,0:T(8,128)(2,1)S(1)}, u32[]{:S(2)}, u32[]{:S(2)}) collective-permute-start(bf16[256,2048]{1,0:T(8,128)(2,1)} %tie.17.refs_19_.refs_3_.refs_12_), channel_id=1, source_target_pairs={{0,1},{1,0},{2,3},{3,2},{4,5},{5,4},{6,7},{7,6},{8,9},{9,8},{10,11... | collective-permute-start | bytes 3145736 | tf_op jit(solution)/shard_map/ppermute | solution.py:78
  127.7 61.5 %collective-permute-start.25 = (bf16[256,2048]{1,0:T(8,128)(2,1)}, bf16[256,2048]{1,0:T(8,128)(2,1)}, u32[]{:S(2)}, u32[]{:S(2)}) collective-permute-start(bf16[256,2048]{1,0:T(8,128)(2,1)} %tie.17.refs_19_.refs_3_.refs_12_), channel_id=1, source_target_pairs={{0,2},{1,3},{2,0},{3,1},{4,6},{5,7},{6,4},{7,5},{8,10},{9,11},{10,... | collective-permute-start | bytes 3145736 | tf_op jit(solution)/shard_map/ppermute | solution.py:78
  133.2 26.0 %collective-permute-start.35 = (bf16[64,1024]{1,0:T(8,128)(2,1)}, bf16[64,1024]{1,0:T(8,128)(2,1)S(1)}, u32[]{:S(2)}, u32[]{:S(2)}) collective-permute-start(bf16[64,1024]{1,0:T(8,128)(2,1)} %tie.19), channel_id=1, source_target_pairs={{0,2},{1,3},{2,0},{3,1},{4,6},{5,7},{6,4},{7,5},{8,10},{9,11},{10,... | collective-permute-start | bytes 393224 | tf_op jit(solution)/shard_map/ppermute | solution.py:78
  163.0 26.2 %collective-permute-start.37 = (bf16[128,2048]{1,0:T(8,128)(2,1)}, bf16[128,2048]{1,0:T(8,128)(2,1)}, u32[]{:S(2)}, u32[]{:S(2)}) collective-permute-start(bf16[128,2048]{1,0:T(8,128)(2,1)} %tie.16.refs_15_.refs_16_.refs_1_.refs_4_), channel_id=1, source_target_pairs={{0,4},{4,12},{12,20},{20,28},{28,24},{24,16},{16,8},{8,0},{1,5},{5... | collective-permute-start | bytes 1572872 | tf_op jit(solution)/shard_map/ppermute | solution.py:330
  185.5 26.3 %collective-permute-start.30 = (bf16[256,1024]{1,0:T(8,128)(2,1)S(1)}, bf16[256,1024]{1,0:T(8,128)(2,1)}, u32[]{:S(2)}, u32[]{:S(2)}) collective-permute-start(bf16[256,1024]{1,0:T(8,128)(2,1)S(1)} %collective-permute-done.28.refs_7_.refs_4_), channel_id=1, source_target_pairs={{0,4},{4,12},{12,20},{20,28},{28,24},{24,16},{16,8},{8,0},{1,5},{5... | collective-permute-start | bytes 1572872 | tf_op jit(solution)/shard_map/ppermute | solution.py:330
  189.2 35.0 %collective-permute-start.27 = (bf16[256,2048]{1,0:T(8,128)(2,1)}, bf16[256,2048]{1,0:T(8,128)(2,1)S(1)}, u32[]{:S(2)}, u32[]{:S(2)}) collective-permute-start(bf16[256,2048]{1,0:T(8,128)(2,1)} %collective-permute-done.25.refs_20_.refs_3_.refs_14_), channel_id=1, source_target_pairs={{0,1},{1,0},{2,3},{3,2},{4,5},{5,4},{6,7},{7,6},{8,9},{9,8},{10,11... | collective-permute-start | bytes 3145736 | tf_op jit(solution)/shard_map/ppermute | solution.py:78
  189.3 32.8 %collective-permute-start.18 = (bf16[128,2048]{1,0:T(8,128)(2,1)}, bf16[128,2048]{1,0:T(8,128)(2,1)}, u32[]{:S(2)}, u32[]{:S(2)}) collective-permute-start(bf16[128,2048]{1,0:T(8,128)(2,1)} %slice.119.refs_5_), channel_id=1, source_target_pairs={{4,0},{12,4},{20,12},{28,20},{24,28},{16,24},{8,16},{0,8},{5,1},{1... | collective-permute-start | bytes 1572872 | tf_op jit(solution)/shard_map/ppermute | solution.py:330
  222.1 62.4 %collective-permute-start.46 = (bf16[256,2048]{1,0:T(8,128)(2,1)}, bf16[256,2048]{1,0:T(8,128)(2,1)S(1)}, u32[]{:S(2)}, u32[]{:S(2)}) collective-permute-start(bf16[256,2048]{1,0:T(8,128)(2,1)} %join_pieces.5.refs_13_.refs_14_.refs_4_), channel_id=1, source_target_pairs={{4,0},{12,4},{20,12},{28,20},{24,28},{16,24},{8,16},{0,8},{5,1},{1... | collective-permute-start | bytes 3145736 | tf_op jit(solution)/shard_map/ppermute | solution.py:330
  222.1 62.4 %collective-permute-start.45 = (bf16[256,2048]{1,0:T(8,128)(2,1)}, bf16[256,2048]{1,0:T(8,128)(2,1)S(1)}, u32[]{:S(2)}, u32[]{:S(2)}) collective-permute-start(bf16[256,2048]{1,0:T(8,128)(2,1)} %join_pieces.5.refs_13_.refs_14_.refs_4_), channel_id=1, source_target_pairs={{0,4},{4,12},{12,20},{20,28},{28,24},{24,16},{16,8},{8,0},{1,5},{5... | collective-permute-start | bytes 3145736 | tf_op jit(solution)/shard_map/ppermute | solution.py:330
  224.2 37.9 %collective-permute-start.33 = (bf16[128,1024]{1,0:T(8,128)(2,1)}, bf16[128,1024]{1,0:T(8,128)(2,1)S(1)}, u32[]{:S(2)}, u32[]{:S(2)}) collective-permute-start(bf16[128,1024]{1,0:T(8,128)(2,1)} %slice.121), channel_id=1, source_target_pairs={{4,0},{12,4},{20,12},{28,20},{24,28},{16,24},{8,16},{0,8},{5,1},{1... | collective-permute-start | bytes 786440 | tf_op jit(solution)/shard_map/ppermute | solution.py:330
  224.2 40.0 %collective-permute-start.32 = (bf16[128,1024]{1,0:T(8,128)(2,1)S(1)}, bf16[128,1024]{1,0:T(8,128)(2,1)S(1)}, u32[]{:S(2)}, u32[]{:S(2)}) collective-permute-start(bf16[128,1024]{1,0:T(8,128)(2,1)S(1)} %slice.120), channel_id=1, source_target_pairs={{0,4},{4,12},{12,20},{20,28},{28,24},{24,16},{16,8},{8,0},{1,5},{5... | collective-permute-start | bytes 786440 | tf_op jit(solution)/shard_map/ppermute | solution.py:330
  230.5 30.1 %collective-permute-start.40 = (bf16[128,2048]{1,0:T(8,128)(2,1)}, bf16[128,2048]{1,0:T(8,128)(2,1)S(1)}, u32[]{:S(2)}, u32[]{:S(2)}) collective-permute-start(bf16[128,2048]{1,0:T(8,128)(2,1)} %collective-permute-done.39.refs_4_.refs_7_), channel_id=1, source_target_pairs={{0,4},{4,12},{12,20},{20,28},{28,24},{24,16},{16,8},{8,0},{1,5},{5... | collective-permute-start | bytes 1572872 | tf_op jit(solution)/shard_map/ppermute | solution.py:330
  292.7 26.4 %collective-permute-start.51 = (bf16[256,2048]{1,0:T(8,128)(2,1)}, bf16[256,2048]{1,0:T(8,128)(2,1)S(1)}, u32[]{:S(2)}, u32[]{:S(2)}) collective-permute-start(bf16[256,2048]{1,0:T(8,128)(2,1)} %copy-done.21), channel_id=1, source_target_pairs={{4,0},{12,4},{20,12},{28,20},{24,28},{16,24},{8,16},{0,8},{5,1},{1... | collective-permute-start | bytes 3145736 | tf_op jit(solution)/shard_map/ppermute | solution.py:330
  294.5 25.7 %collective-permute-start.50 = (bf16[256,2048]{1,0:T(8,128)(2,1)}, bf16[256,2048]{1,0:T(8,128)(2,1)S(1)}, u32[]{:S(2)}, u32[]{:S(2)}) collective-permute-start(bf16[256,2048]{1,0:T(8,128)(2,1)} %copy-done.22), channel_id=1, source_target_pairs={{0,4},{4,12},{12,20},{20,28},{28,24},{24,16},{16,8},{8,0},{1,5},{5... | collective-permute-start | bytes 3145736 | tf_op jit(solution)/shard_map/ppermute | solution.py:330
  295.2 27.3 %collective-permute-start.47 = (bf16[256,2048]{1,0:T(8,128)(2,1)}, bf16[256,2048]{1,0:T(8,128)(2,1)S(1)}, u32[]{:S(2)}, u32[]{:S(2)}) collective-permute-start(bf16[256,2048]{1,0:T(8,128)(2,1)} %get-tuple-element.120.refs_10_), channel_id=1, source_target_pairs={{0,1},{1,0},{2,3},{3,2},{4,5},{5,4},{6,7},{7,6},{8,9},{9,8},{10,11... | collective-permute-start | bytes 3145736 | tf_op jit(solution)/shard_map/ppermute | solution.py:78
  305.9 25.8 %collective-permute-start.49 = (bf16[256,2048]{1,0:T(8,128)(2,1)}, bf16[256,2048]{1,0:T(8,128)(2,1)}, u32[]{:S(2)}, u32[]{:S(2)}) collective-permute-start(bf16[256,2048]{1,0:T(8,128)(2,1)} %add_up.5), channel_id=1, source_target_pairs={{0,2},{1,3},{2,0},{3,1},{4,6},{5,7},{6,4},{7,5},{8,10},{9,11},{10,... | collective-permute-start | bytes 3145736 | tf_op jit(solution)/shard_map/ppermute | solution.py:78
  320.3 26.1 %collective-permute-start.54 = (bf16[256,2048]{1,0:T(8,128)(2,1)S(1)}, bf16[256,2048]{1,0:T(8,128)(2,1)}, u32[]{:S(2)}, u32[]{:S(2)}) collective-permute-start(bf16[256,2048]{1,0:T(8,128)(2,1)S(1)} %collective-permute-done.50.refs_6_.refs_7_.refs_16_), channel_id=1, source_target_pairs={{0,4},{4,12},{12,20},{20,28},{28,24},{24,16},{16,8},{8,0},{1,5},{5... | collective-permute-start | bytes 3145736 | tf_op jit(solution)/shard_map/ppermute | solution.py:330
  397.6 25.6 %collective-permute-start.65 = (bf16[256,2048]{1,0:T(8,128)(2,1)}, bf16[256,2048]{1,0:T(8,128)(2,1)S(1)}, u32[]{:S(2)}, u32[]{:S(2)}) collective-permute-start(bf16[256,2048]{1,0:T(8,128)(2,1)} %add_up.6.refs_16_), channel_id=1, source_target_pairs={{0,2},{1,3},{2,0},{3,1},{4,6},{5,7},{6,4},{7,5},{8,10},{9,11},{10,... | collective-permute-start | bytes 3145736 | tf_op jit(solution)/shard_map/ppermute | solution.py:78
  432.2 26.8 %collective-permute-start.69 = (bf16[256,2048]{1,0:T(8,128)(2,1)}, bf16[256,2048]{1,0:T(8,128)(2,1)S(1)}, u32[]{:S(2)}, u32[]{:S(2)}) collective-permute-start(bf16[256,2048]{1,0:T(8,128)(2,1)} %get-tuple-element.144.refs_18_.refs_0_.refs_6_), channel_id=1, source_target_pairs={{0,1},{1,0},{2,3},{3,2},{4,5},{5,4},{6,7},{7,6},{8,9},{9,8},{10,11... | collective-permute-start | bytes 3145736 | tf_op jit(solution)/shard_map/ppermute | solution.py:78
  455.7 26.1 %collective-permute-start.66 = (bf16[256,2048]{1,0:T(8,128)(2,1)}, bf16[256,2048]{1,0:T(8,128)(2,1)S(1)}, u32[]{:S(2)}, u32[]{:S(2)}) collective-permute-start(bf16[256,2048]{1,0:T(8,128)(2,1)} %get-tuple-element.145.refs_1_), channel_id=1, source_target_pairs={{4,0},{12,4},{20,12},{28,20},{24,28},{16,24},{8,16},{0,8},{5,1},{1... | collective-permute-start | bytes 3145736 | tf_op jit(solution)/shard_map/ppermute | solution.py:675
  459.0 35.4 %collective-permute-start.61 = (bf16[256,2048]{1,0:T(8,128)(2,1)}, bf16[256,2048]{1,0:T(8,128)(2,1)S(1)}, u32[]{:S(2)}, u32[]{:S(2)}) collective-permute-start(bf16[256,2048]{1,0:T(8,128)(2,1)} %get-tuple-element.141), channel_id=1, source_target_pairs={{0,1},{1,0},{2,3},{3,2},{4,5},{5,4},{6,7},{7,6},{8,9},{9,8},{10,11... | collective-permute-start | bytes 3145736 | tf_op jit(solution)/shard_map/ppermute | solution.py:78
  492.3 30.4 %collective-permute-start.72 = (bf16[256,2048]{1,0:T(8,128)(2,1)}, bf16[256,2048]{1,0:T(8,128)(2,1)S(1)}, u32[]{:S(2)}, u32[]{:S(2)}) collective-permute-start(bf16[256,2048]{1,0:T(8,128)(2,1)} %get-tuple-element.147.refs_2_.refs_11_), channel_id=1, source_target_pairs={{4,0},{12,4},{20,12},{28,20},{24,28},{16,24},{8,16},{0,8},{5,1},{1... | collective-permute-start | bytes 3145736 | tf_op jit(solution)/shard_map/ppermute | solution.py:675
  494.5 28.3 %collective-permute-start.73 = (bf16[256,2048]{1,0:T(8,128)(2,1)}, bf16[256,2048]{1,0:T(8,128)(2,1)S(1)}, u32[]{:S(2)}, u32[]{:S(2)}) collective-permute-start(bf16[256,2048]{1,0:T(8,128)(2,1)} %get-tuple-element.148.refs_3_.refs_12_), channel_id=1, source_target_pairs={{0,4},{4,12},{12,20},{20,28},{28,24},{24,16},{16,8},{8,0},{1,5},{5... | collective-permute-start | bytes 3145736 | tf_op jit(solution)/shard_map/ppermute | solution.py:675
  494.5 58.4 %collective-permute-start.60 = (bf16[256,2048]{1,0:T(8,128)(2,1)}, bf16[256,2048]{1,0:T(8,128)(2,1)S(1)}, u32[]{:S(2)}, u32[]{:S(2)}) collective-permute-start(bf16[256,2048]{1,0:T(8,128)(2,1)} %get-tuple-element.139), channel_id=1, source_target_pairs={{0,1},{1,0},{2,3},{3,2},{4,5},{5,4},{6,7},{7,6},{8,9},{9,8},{10,11... | collective-permute-start | bytes 3145736 | tf_op jit(solution)/shard_map/ppermute | solution.py:78
  498.2 79.2 %collective-permute-start.71 = (bf16[256,2048]{1,0:T(8,128)(2,1)}, bf16[256,2048]{1,0:T(8,128)(2,1)S(1)}, u32[]{:S(2)}, u32[]{:S(2)}) collective-permute-start(bf16[256,2048]{1,0:T(8,128)(2,1)} %add_up.7.refs_13_), channel_id=1, source_target_pairs={{0,2},{1,3},{2,0},{3,1},{4,6},{5,7},{6,4},{7,5},{8,10},{9,11},{10,... | collective-permute-start | bytes 3145736 | tf_op jit(solution)/shard_map/ppermute | solution.py:78
  520.7 33.9 %collective-permute-start.76 = (bf16[128,2048]{1,0:T(8,128)(2,1)}, bf16[128,2048]{1,0:T(8,128)(2,1)S(1)}, u32[]{:S(2)}, u32[]{:S(2)}) collective-permute-start(bf16[128,2048]{1,0:T(8,128)(2,1)} %get-tuple-element.156.refs_18_), channel_id=1, source_target_pairs={{4,0},{12,4},{20,12},{28,20},{24,28},{16,24},{8,16},{0,8},{5,1},{1... | collective-permute-start | bytes 1572872 | tf_op jit(solution)/shard_map/ppermute | solution.py:675
  552.4 27.1 %collective-permute-start.78 = (bf16[256,2048]{1,0:T(8,128)(2,1)}, bf16[256,2048]{1,0:T(8,128)(2,1)}, u32[]{:S(2)}, u32[]{:S(2)}) collective-permute-start(bf16[256,2048]{1,0:T(8,128)(2,1)} %get-tuple-element.166), channel_id=1, source_target_pairs={{0,1},{1,0},{2,3},{3,2},{4,5},{5,4},{6,7},{7,6},{8,9},{9,8},{10,11... | collective-permute-start | bytes 3145736 | tf_op jit(solution)/shard_map/ppermute | solution.py:78
  567.3 30.5 %collective-permute-start.83 = (bf16[256,2048]{1,0:T(8,128)(2,1)}, bf16[256,2048]{1,0:T(8,128)(2,1)S(1)}, u32[]{:S(2)}, u32[]{:S(2)}) collective-permute-start(bf16[256,2048]{1,0:T(8,128)(2,1)} %get-tuple-element.158.refs_10_), channel_id=1, source_target_pairs={{4,0},{12,4},{20,12},{28,20},{24,28},{16,24},{8,16},{0,8},{5,1},{1... | collective-permute-start | bytes 3145736 | tf_op jit(solution)/shard_map/ppermute | solution.py:675
  577.5 29.2 %collective-permute-start.84 = (bf16[256,2048]{1,0:T(8,128)(2,1)S(1)}, bf16[256,2048]{1,0:T(8,128)(2,1)}, u32[]{:S(2)}, u32[]{:S(2)}) collective-permute-start(bf16[256,2048]{1,0:T(8,128)(2,1)S(1)} %copy-done.28), channel_id=1, source_target_pairs={{0,4},{4,12},{12,20},{20,28},{28,24},{24,16},{16,8},{8,0},{1,5},{5... | collective-permute-start | bytes 3145736 | tf_op jit(solution)/shard_map/ppermute | solution.py:675
  578.0 38.0 %collective-permute-start.81 = (bf16[256,2048]{1,0:T(8,128)(2,1)}, bf16[256,2048]{1,0:T(8,128)(2,1)S(1)}, u32[]{:S(2)}, u32[]{:S(2)}) collective-permute-start(bf16[256,2048]{1,0:T(8,128)(2,1)} %get-tuple-element.163.refs_30_), channel_id=1, source_target_pairs={{4,0},{12,4},{20,12},{28,20},{24,28},{16,24},{8,16},{0,8},{5,1},{1... | collective-permute-start | bytes 3145736 | tf_op jit(solution)/shard_map/ppermute | solution.py:675
  579.6 61.0 %collective-permute-start.79 = (bf16[256,2048]{1,0:T(8,128)(2,1)S(1)}, bf16[256,2048]{1,0:T(8,128)(2,1)}, u32[]{:S(2)}, u32[]{:S(2)}) collective-permute-start(bf16[256,2048]{1,0:T(8,128)(2,1)S(1)} %copy-done.25), channel_id=1, source_target_pairs={{0,1},{1,0},{2,3},{3,2},{4,5},{5,4},{6,7},{7,6},{8,9},{9,8},{10,11... | collective-permute-start | bytes 3145736 | tf_op jit(solution)/shard_map/ppermute | solution.py:78
  579.6 50.3 %collective-permute-start.82 = (bf16[256,2048]{1,0:T(8,128)(2,1)}, bf16[256,2048]{1,0:T(8,128)(2,1)}, u32[]{:S(2)}, u32[]{:S(2)}) collective-permute-start(bf16[256,2048]{1,0:T(8,128)(2,1)} %get-tuple-element.164.refs_31_), channel_id=1, source_target_pairs={{0,4},{4,12},{12,20},{20,28},{28,24},{24,16},{16,8},{8,0},{1,5},{5... | collective-permute-start | bytes 3145736 | tf_op jit(solution)/shard_map/ppermute | solution.py:675
  597.8 44.1 %collective-permute-start.80 = (bf16[256,2048]{1,0:T(8,128)(2,1)}, bf16[256,2048]{1,0:T(8,128)(2,1)}, u32[]{:S(2)}, u32[]{:S(2)}) collective-permute-start(bf16[256,2048]{1,0:T(8,128)(2,1)} %add_up.8.refs_12_), channel_id=1, source_target_pairs={{0,2},{1,3},{2,0},{3,1},{4,6},{5,7},{6,4},{7,5},{8,10},{9,11},{10,... | collective-permute-start | bytes 3145736 | tf_op jit(solution)/shard_map/ppermute | solution.py:78
  606.7 41.5 %collective-permute-start.86 = (bf16[256,2048]{1,0:T(8,128)(2,1)}, bf16[256,2048]{1,0:T(8,128)(2,1)S(1)}, u32[]{:S(2)}, u32[]{:S(2)}) collective-permute-start(bf16[256,2048]{1,0:T(8,128)(2,1)} %get-tuple-element.167.refs_4_), channel_id=1, source_target_pairs={{4,0},{12,4},{20,12},{28,20},{24,28},{16,24},{8,16},{0,8},{5,1},{1... | collective-permute-start | bytes 3145736 | tf_op jit(solution)/shard_map/ppermute | solution.py:675
  616.1 32.5 %collective-permute-start.87 = (bf16[256,2048]{1,0:T(8,128)(2,1)}, bf16[256,2048]{1,0:T(8,128)(2,1)S(1)}, u32[]{:S(2)}, u32[]{:S(2)}) collective-permute-start(bf16[256,2048]{1,0:T(8,128)(2,1)} %get-tuple-element.168.refs_5_), channel_id=1, source_target_pairs={{0,4},{4,12},{12,20},{20,28},{28,24},{24,16},{16,8},{8,0},{1,5},{5... | collective-permute-start | bytes 3145736 | tf_op jit(solution)/shard_map/ppermute | solution.py:675
  640.5 30.6 %collective-permute-start.95 = (bf16[256,2048]{1,0:T(8,128)(2,1)}, bf16[256,2048]{1,0:T(8,128)(2,1)}, u32[]{:S(2)}, u32[]{:S(2)}) collective-permute-start(bf16[256,2048]{1,0:T(8,128)(2,1)} %get-tuple-element.174.refs_7_), channel_id=1, source_target_pairs={{0,4},{4,12},{12,20},{20,28},{28,24},{24,16},{16,8},{8,0},{1,5},{5... | collective-permute-start | bytes 3145736 | tf_op jit(solution)/shard_map/ppermute | solution.py:675
  657.9 39.5 %collective-permute-start.89 = (bf16[256,2048]{1,0:T(8,128)(2,1)}, bf16[256,2048]{1,0:T(8,128)(2,1)S(1)}, u32[]{:S(2)}, u32[]{:S(2)}) collective-permute-start(bf16[256,2048]{1,0:T(8,128)(2,1)} %get-tuple-element.178.refs_1_.refs_12_), channel_id=1, source_target_pairs={{4,0},{12,4},{20,12},{28,20},{24,28},{16,24},{8,16},{0,8},{5,1},{1... | collective-permute-start | bytes 3145736 | tf_op jit(solution)/shard_map/ppermute | solution.py:675
  659.5 37.9 %collective-permute-start.90 = (bf16[256,2048]{1,0:T(8,128)(2,1)}, bf16[256,2048]{1,0:T(8,128)(2,1)S(1)}, u32[]{:S(2)}, u32[]{:S(2)}) collective-permute-start(bf16[256,2048]{1,0:T(8,128)(2,1)} %get-tuple-element.179.refs_2_.refs_13_), channel_id=1, source_target_pairs={{0,4},{4,12},{12,20},{20,28},{28,24},{24,16},{16,8},{8,0},{1,5},{5... | collective-permute-start | bytes 3145736 | tf_op jit(solution)/shard_map/ppermute | solution.py:675
  681.7 34.6 %collective-permute-start.97 = (bf16[256,2048]{1,0:T(8,128)(2,1)}, bf16[256,2048]{1,0:T(8,128)(2,1)S(1)}, u32[]{:S(2)}, u32[]{:S(2)}) collective-permute-start(bf16[256,2048]{1,0:T(8,128)(2,1)} %get-tuple-element.183.refs_4_), channel_id=1, source_target_pairs={{4,0},{12,4},{20,12},{28,20},{24,28},{16,24},{8,16},{0,8},{5,1},{1... | collective-permute-start | bytes 3145736 | tf_op jit(solution)/shard_map/ppermute | solution.py:675
  682.5 33.8 %collective-permute-start.98 = (bf16[256,2048]{1,0:T(8,128)(2,1)}, bf16[256,2048]{1,0:T(8,128)(2,1)}, u32[]{:S(2)}, u32[]{:S(2)}) collective-permute-start(bf16[256,2048]{1,0:T(8,128)(2,1)} %get-tuple-element.184.refs_5_), channel_id=1, source_target_pairs={{0,4},{4,12},{12,20},{20,28},{28,24},{24,16},{16,8},{8,0},{1,5},{5... | collective-permute-start | bytes 3145736 | tf_op jit(solution)/shard_map/ppermute | solution.py:675
  732.9 31.8 %collective-permute-start.106 = (bf16[64,1024]{1,0:T(8,128)(2,1)}, bf16[64,1024]{1,0:T(8,128)(2,1)S(1)}, u32[]{:S(2)}, u32[]{:S(2)}) collective-permute-start(bf16[64,1024]{1,0:T(8,128)(2,1)} %get-tuple-element.193), channel_id=1, source_target_pairs={{0,1},{1,0},{2,3},{3,2},{4,5},{5,4},{6,7},{7,6},{8,9},{9,8},{10,11... | collective-permute-start | bytes 393224 | tf_op jit(solution)/shard_map/ppermute | solution.py:78
  733.4 33.3 %collective-permute-start.107 = (bf16[64,1024]{1,0:T(8,128)(2,1)}, bf16[64,1024]{1,0:T(8,128)(2,1)S(1)}, u32[]{:S(2)}, u32[]{:S(2)}) collective-permute-start(bf16[64,1024]{1,0:T(8,128)(2,1)} %get-tuple-element.194), channel_id=1, source_target_pairs={{0,2},{1,3},{2,0},{3,1},{4,6},{5,7},{6,4},{7,5},{8,10},{9,11},{10,... | collective-permute-start | bytes 393224 | tf_op jit(solution)/shard_map/ppermute | solution.py:78
  734.4 29.3 %collective-permute-start.109 = (bf16[256,1024]{1,0:T(8,128)(2,1)}, bf16[256,1024]{1,0:T(8,128)(2,1)S(1)}, u32[]{:S(2)}, u32[]{:S(2)}) collective-permute-start(bf16[256,1024]{1,0:T(8,128)(2,1)} %get-tuple-element.196), channel_id=1, source_target_pairs={{0,0},{8,1},{16,2},{24,3},{4,4},{12,5},{20,6},{28,7},{1,8},{9,9},{... | collective-permute-start | bytes 1572872 | tf_op jit(solution)/shard_map/ppermute | solution.py:1155
  (157 other events, 1947.1 us)

commit v3 on v2

--- a/solution.py
+++ b/solution.py
@@ -105,6 +105,14 @@
             new = {g: tie(part, *after) for g, part in new.items()}
         held.update(new)
     return held
+
+
+def far_blocks(x, *after):
+    held = {0: x}
+    for gap in reversed(seq_gaps(lax.axis_size("seq"))[1:]):
+        held.update({g ^ gap: tie(swap_seq(part, gap), *after) for g, part in list(held.items())})
+    del held[0]
+    return held | {g ^ 1: swap_seq(part, 1) for g, part in held.items()}
 
 
 ROWS = 128
@@ -249,37 +257,37 @@
     return lax.axis_index("dp") * lax.axis_size("seq") + lax.axis_index("seq")
 
 
-def gather_all(x):
-    S, G = lax.axis_size("seq"), lax.axis_size("dp")
-    me = flat_index()
-    held = x[None, None]
-    middle = None
-    for gap in [S * g for g in seq_gaps(G)] + seq_gaps(S):
-        axis = 0 if gap >= S else 1
-        other = swap_all(held, gap)
-        held = jnp.where(
-            (me & gap) != 0,
-            jnp.concatenate([other, held], axis=axis),
-            jnp.concatenate([held, other], axis=axis),
+class GatherAll:
+    def __init__(self, x):
+        S, G = lax.axis_size("seq"), lax.axis_size("dp")
+        self.held, self.gaps = x[None, None], [S * g for g in seq_gaps(G)] + seq_gaps(S)
+
+    def step(self, *after):
+        gap, *self.gaps = self.gaps
+        axis = 0 if gap >= lax.axis_size("seq") else 1
+        other = swap_all(self.held, gap)
+        if after:
+            other = tie(other, *after)
+        self.held = jnp.where(
+            (flat_index() & gap) != 0,
+            jnp.concatenate([other, self.held], axis=axis),
+            jnp.concatenate([self.held, other], axis=axis),
         )
-        if gap == S * G // 2:
-            middle = held
-    return held.reshape((G * S,) + x.shape), middle
-
-
-def scatter_all(x, afters):
-    me = flat_index()
-    held = x
-    for n, gap in enumerate(reversed(seq_gaps(x.shape[0]))):
-        half = held.shape[0] // 2
-        upper = (me & gap) != 0
-        keep = jnp.where(upper, held[half:], held[:half])
-        give = jnp.where(upper, held[:half], held[half:])
-        got = swap_all(give, gap)
-        if n < len(afters):
-            got = tie(got, *afters[n])
-        held = keep + got
-    return held[0]
+        return self
+
+
+class ScatterAll:
+    def __init__(self, x):
+        S, G = lax.axis_size("seq"), lax.axis_size("dp")
+        self.held, self.gaps = x, seq_gaps(S)[::-1] + [S * g for g in seq_gaps(G)[::-1]]
+
+    def step(self):
+        gap, *self.gaps = self.gaps
+        axis = 0 if gap >= lax.axis_size("seq") else 1
+        low, high = jnp.split(self.held, 2, axis=axis)
+        upper = (flat_index() & gap) != 0
+        self.held = jnp.where(upper, high, low) + swap_all(jnp.where(upper, low, high), gap)
+        return self
 
 
 def cycle(size):
@@ -319,10 +327,13 @@
         self.got = {0: x}
         self.hop = 0
 
-    def step(self):
+    def step(self, *after):
         size, half = self.size, self.got[0].shape[0] // 2
         self.hop += 1
         k = self.hop
+        if after and k > 1:
+            for n in {k - 1, (size - k + 1) % size}:
+                self.got[n] = tie(self.got[n], *after)
         a, b = self.got[k - 1], self.got[(size - k + 1) % size]
         if k == size // 2:
             a, b = a[:half], b[half:]
@@ -396,17 +407,20 @@
         loads = Loads(sems)
         weight.load(loads, "w", at, w_refs, w)
         for n, piece in enumerate(pieces):
-            loads.add(n, piece, x.at[n])
+            loads.add(n // 2, piece, x.at[pl.ds(n * T, T)])
         loads.wait("w")
-        for n, gap in enumerate(gaps):
-            loads.wait(n)
+        for n in range(0, S, 2):
+            loads.wait(n // 2)
+            rows = pl.ds(n * T, 2 * T)
             for (first, width, dtype), out, stage in zip(cols, outs, stages):
                 if across:
-                    result = dot(x[n], w[first : first + width, :], ((1,), (1,)))
+                    result = dot(x[rows], w[first : first + width, :], ((1,), (1,)))
                 else:
-                    result = dot(x[n], w[:, first : first + width], ((1,), (0,)))
-                stage[n] = result.astype(dtype)
-                loads.add("out", stage.at[n], out.at[pl.ds(block_row(at, gap, T), T)])
+                    result = dot(x[rows], w[:, first : first + width], ((1,), (0,)))
+                stage[rows] = result.astype(dtype)
+                for m in (n, n + 1):
+                    target = out.at[pl.ds(block_row(at, gaps[m], T), T)]
+                    loads.add("out", stage.at[pl.ds(m * T, T)], target)
         loads.wait("out")
 
     return call(
@@ -414,8 +428,8 @@
         info,
         [*held.values(), *weight.arrays],
         [like((S * T, width), dtype) for _, width, dtype in cols],
-        [pltpu.VMEM((S, T, K), bf16), pltpu.VMEM(weight.shape, bf16)]
-        + [pltpu.VMEM((S, T, width), dtype) for _, width, dtype in cols]
+        [pltpu.VMEM((S * T, K), bf16), pltpu.VMEM(weight.shape, bf16)]
+        + [pltpu.VMEM((S * T, width), dtype) for _, width, dtype in cols]
         + [pltpu.SemaphoreType.DMA((S + weight.copies + S * n_out,))],
         name=name,
         after=after,
@@ -423,7 +437,7 @@
     )
 
 
-def partial_rows(info, terms, gaps, name, after=()):
+def partial_rows(info, terms, gaps, name, after=(), ordered=False):
     arrays, picks = [], []
     for x, weight, _ in terms:
         mine = [x[gap] for gap in gaps] if isinstance(x, dict) else [x]
@@ -435,8 +449,9 @@
     n_term, n_gap = len(terms), len(gaps)
 
     def body(at, *refs):
-        ins, outs = refs[: len(arrays)], refs[len(arrays) : len(arrays) + n_gap]
-        scratch = refs[len(arrays) + n_gap :]
+        n_out = 1 if ordered else n_gap
+        ins, outs = refs[: len(arrays)], refs[len(arrays) : len(arrays) + n_out]
+        scratch = refs[len(arrays) + n_out :]
         xs, ws, stages, sems = scratch[:n_term], scratch[n_term : 2 * n_term], scratch[2 * n_term : -1], scratch[-1]
         loads = Loads(sems)
         for (x, weight, across), (start, count, by_gap), x_ref, w_ref in zip(terms, picks, xs, ws):
@@ -445,32 +460,33 @@
                     source = ins[start + n]
                 else:
                     source = ins[start].at[pl.ds(block_row(at, gap, T), T)]
-                loads.add("x", source, x_ref.at[n])
+                loads.add("x", source, x_ref.at[pl.ds(n * T, T)])
             weight.load(loads, "w", at, ins[start + count : start + count + len(weight.arrays)], w_ref)
         loads.wait("x")
         loads.wait("w")
-        for n in range(n_gap):
-            half = D // 2
-            for c in range(2):
-                total = None
-                for (_, _, across), x_ref, w_ref in zip(terms, xs, ws):
-                    cut = slice(c * half, (c + 1) * half)
-                    if across:
-                        part = dot(x_ref[n], w_ref[cut, :], ((1,), (1,)))
-                    else:
-                        part = dot(x_ref[n], w_ref[:, cut], ((1,), (0,)))
-                    total = part if total is None else total + part
-                stages[n][:, c * half : (c + 1) * half] = total.astype(stages[n].dtype)
-            loads.add("out", stages[n], outs[n])
+        for c in range(4):
+            cut = slice(c * (D // 4), (c + 1) * (D // 4))
+            total = None
+            for (_, _, across), x_ref, w_ref in zip(terms, xs, ws):
+                if across:
+                    part = dot(x_ref[...], w_ref[cut, :], ((1,), (1,)))
+                else:
+                    part = dot(x_ref[...], w_ref[:, cut], ((1,), (0,)))
+                total = part if total is None else total + part
+            for n in range(n_gap):
+                stages[n][:, cut] = total[n * T : (n + 1) * T].astype(stages[n].dtype)
+        for n, gap in enumerate(gaps):
+            target = outs[0].at[pl.ds(block_row(at, gap, T), T)] if ordered else outs[n]
+            loads.add("out", stages[n], target)
         loads.wait("out")
 
-    dtypes = [bf16 if gap & 1 else f32 for gap in gaps]
+    dtypes = [bf16 if gap & 1 or ordered else f32 for gap in gaps]
     outs = call(
         body,
         info,
         arrays,
-        [like((T, D), dtype) for dtype in dtypes],
-        [pltpu.VMEM((n_gap, T, width), bf16) for width in widths]
+        [like((n_gap * T, D), bf16)] if ordered else [like((T, D), dtype) for dtype in dtypes],
+        [pltpu.VMEM((n_gap * T, width), bf16) for width in widths]
         + [pltpu.VMEM(weight.shape, bf16) for _, weight, _ in terms]
         + [pltpu.VMEM((T, D), dtype) for dtype in dtypes]
         + [pltpu.SemaphoreType.DMA((sum(w.copies for _, w, _ in terms) + (n_term + 1) * n_gap,))],
@@ -478,7 +494,7 @@
         after=after,
         cost=2 * n_gap * T * D * sum(widths),
     )
-    return dict(zip(gaps, outs))
+    return outs[0] if ordered else dict(zip(gaps, outs))
 
 
 def feed_forward(info, hidden, cot, up, down, gaps, after=()):
@@ -486,36 +502,44 @@
     T = hidden[0].shape[0]
     FW = up.shape[1]
     n_up, n_down = len(up.arrays), len(down.arrays)
-    arrays = [*(hidden[gap] for gap in gaps), *(cot[gap] for gap in gaps), *up.arrays, *down.arrays]
+    arrays = [*(hidden[gap] for gap in gaps), cot, *up.arrays, *down.arrays]
 
     def body(at, *refs):
         ins, outs = refs[: len(arrays)], refs[len(arrays) : len(arrays) + 3 * n_gap]
         x, g, w_up, w_down, acts, grads, *stages, sems = refs[len(arrays) + 3 * n_gap :]
         loads = Loads(sems)
-        up.load(loads, "up", at, ins[2 * n_gap : 2 * n_gap + n_up], w_up)
+        up.load(loads, "up", at, ins[n_gap + 1 : n_gap + 1 + n_up], w_up)
         for n in range(n_gap):
-            loads.add(("x", n), ins[n], x.at[n])
-        down.load(loads, "down", at, ins[2 * n_gap + n_up :], w_down)
-        for n in range(n_gap):
-            loads.add(("g", n), ins[n_gap + n], g.at[n])
+            loads.add(("x", n // 2), ins[n], x.at[pl.ds(n * T, T)])
+        down.load(loads, "down", at, ins[n_gap + 1 + n_up :], w_down)
+        for n, gap in enumerate(gaps):
+            source = ins[n_gap].at[pl.ds(block_row(at, gap, T), T)]
+            loads.add(("g", n // 2), source, g.at[pl.ds(n * T, T)])
         loads.wait("up")
-        for n in range(n_gap):
-            loads.wait(("x", n))
-            pre = dot(x[n], w_up[...], ((1,), (0,)))
+        for n in range(0, n_gap, 2):
+            rows = pl.ds(n * T, 2 * T)
+            both = [(m, pl.ds(m * T, T)) for m in (n, n + 1)]
+            loads.wait(("x", n // 2))
+            pre = dot(x[rows], w_up[...], ((1,), (0,)))
             below = 0.5 * (1.0 + lax.erf(pre * 0.5**0.5))
-            acts[n] = (pre * below).astype(bf16)
-            loads.add("out", acts.at[n], outs[n])
+            acts[rows] = (pre * below).astype(bf16)
+            for m, part in both:
+                loads.add("out", acts.at[part], outs[m])
             slope = below + pre * jnp.exp(-0.5 * pre * pre) * (0.5 / jnp.pi) ** 0.5
             if n == 0:
                 loads.wait("down")
-            loads.wait(("g", n))
-            grads[n] = (dot(g[n], w_down[...], ((1,), (1,))) * slope).astype(bf16)
-            loads.add("out", grads.at[n], outs[n_gap + n])
-            half = D // 2
-            for c in range(2):
-                cut = slice(c * half, (c + 1) * half)
-                stages[n][:, cut] = dot(grads[n], w_up[cut, :], ((1,), (1,))).astype(stages[n].dtype)
-            loads.add("out", stages[n], outs[2 * n_gap + n])
+            loads.wait(("g", n // 2))
+            grads[rows] = (dot(g[rows], w_down[...], ((1,), (1,))) * slope).astype(bf16)
+            for m, part in both:
+                loads.add("out", grads.at[part], outs[n_gap + m])
+            for c in range(4):
+                cut = slice(c * (D // 4), (c + 1) * (D // 4))
+                result = dot(grads[rows], w_up[cut, :], ((1,), (1,)))
+                for m, part in both:
+                    value = result[(m - n) * T : (m - n + 1) * T]
+                    stages[m][:, cut] = value.astype(stages[m].dtype)
+            for m, part in both:
+                loads.add("out", stages[m], outs[2 * n_gap + m])
         loads.wait("out")
 
     dtypes = [bf16 if gap & 1 else f32 for gap in gaps]
@@ -524,9 +548,9 @@
         info,
         arrays,
         [like((T, FW), bf16)] * (2 * n_gap) + [like((T, D), dtype) for dtype in dtypes],
-        [pltpu.VMEM((n_gap, T, D), bf16)] * 2
+        [pltpu.VMEM((n_gap * T, D), bf16)] * 2
         + [pltpu.VMEM(up.shape, bf16), pltpu.VMEM(down.shape, bf16)]
-        + [pltpu.VMEM((n_gap, T, FW), bf16)] * 2
+        + [pltpu.VMEM((n_gap * T, FW), bf16)] * 2
         + [pltpu.VMEM((T, D), dtype) for dtype in dtypes]
         + [pltpu.SemaphoreType.DMA((up.copies + down.copies + 5 * n_gap,))],
         name="feed_forward",
@@ -600,39 +624,42 @@
                 x_refs = ins[start : start + len(term.xs)]
                 y_refs = ins[start + len(term.xs) : start + len(term.xs) + len(term.ys)]
                 start += len(term.xs) + len(term.ys)
-                y_buf, *x_bufs = buffers[i * (1 + n_w) : (i + 1) * (1 + n_w)]
+                y_buf, x_buf = buffers[2 * i : 2 * i + 2]
                 for n, k in enumerate(which):
+                    mine = pl.ds(n * term.columns, term.columns)
+                    x_part = x_buf.at[mine] if term.whole else x_buf.at[:, mine]
                     place = at[1 + k + (self.size if term.shards else 0)]
                     cols = pl.ds(pl.multiple_of(place * term.columns, term.columns), term.columns)
                     if term.whole:
-                        loads.add((i, n), x_refs[0].at[cols], x_bufs[n])
+                        loads.add(i, x_refs[0].at[cols], x_part)
                         continue
-                    for source, target in term.spread(at, "x", x_refs, x_bufs[n], cols):
-                        loads.add((i, n), source, target)
+                    for source, target in term.spread(at, "x", x_refs, x_part, cols):
+                        loads.add(i, source, target)
                 for source, target in term.spread(at, "y", y_refs, y_buf) if y_refs else ():
-                    loads.add((i, 0), source, target)
+                    loads.add(i, source, target)
             for source, target in zip(recvs, held):
                 loads.add("got", source, target)
             loads.wait("got")
             column = 0
             for i, term in enumerate(terms):
-                y_buf, *x_bufs = buffers[i * (1 + n_w) : (i + 1) * (1 + n_w)]
-                for n in range(n_w):
-                    loads.wait((i, n))
-                    for c in range(term.kind):
-                        cols = slice(c * term.width, (c + 1) * term.width)
-                        if term.whole:
-                            values = x_bufs[n][:, cols].astype(f32)
-                        else:
-                            values = dot(x_bufs[n][...], y_buf[:, cols], ((0,), (0,)))
-                        write(n, c * term.columns, term.columns, column, values, held, results)
+                y_buf, x_buf = buffers[2 * i : 2 * i + 2]
+                loads.wait(i)
+                for c in range(term.kind):
+                    cols = slice(c * term.width, (c + 1) * term.width)
+                    if term.whole:
+                        values = x_buf[:, cols].astype(f32)
+                    else:
+                        values = dot(x_buf[...], y_buf[:, cols], ((0,), (0,)))
+                    for n in range(n_w):
+                        piece = values[n * term.columns : (n + 1) * term.columns]
+                        write(n, c * term.columns, term.columns, column, piece, held, results)
                 column += term.width
 
         scratch = [pltpu.VMEM(x.shape, x.dtype) for x in got]
         for term in terms:
             scratch += [pltpu.VMEM((8, 128) if term.whole else (term.tokens, term.wide), bf16)]
-            shape = (term.columns, term.wide) if term.whole else (term.tokens, term.columns)
-            scratch += [pltpu.VMEM(shape, bf16)] * n_w
+            many = n_w * term.columns
+            scratch += [pltpu.VMEM((many, term.wide) if term.whole else (term.tokens, many), bf16)]
         copies = n_got + sum(n_w * len(t.xs) + len(t.ys) for t in terms)
         return call(
             body,
@@ -696,7 +723,7 @@
         return self.pieces([0], self.last, write, outs, after)
 
 
-def split_columns(info, proj_in, ffn_up, proj_out, H, QW, VW, FW):
+def split_columns(info, proj_in, ffn_up, H, QW, VW, FW):
     size = lax.axis_size("seq")
     rows, G = proj_in.shape[0], lax.axis_size("dp")
     FR = FW // G
@@ -704,46 +731,44 @@
     if not aligned:
         ffn_up = ffn_up.reshape(rows, G, size, FR).transpose(0, 2, 1, 3).reshape(rows, size * FW)
 
-    def body(at, w_in, w_up, w_out, *outs):
-        outs[-1][...] = w_out[...]
+    def body(at, w_in, w_up, *outs):
         for gap in range(size):
             who = at[0] ^ gap
-            qkv, gate, up = outs[3 * gap : 3 * gap + 3]
+            qkv, gate = outs[2 * gap : 2 * gap + 2]
             for h in range(H):
                 for n in range(2):
                     src = pl.multiple_of(n * D + (who * H + h) * DK, DK)
                     qkv[:, (2 * h + n) * DK : (2 * h + n + 1) * DK] = w_in[:, pl.ds(src, DK)]
             qkv[:, 2 * QW :] = w_in[:, pl.ds(pl.multiple_of(2 * D + who * VW, VW), VW)]
-            gate[...] = w_in[:, pl.ds(pl.multiple_of(2 * D + VD + who * VW, VW), VW)]
+            gate[:, :VW] = w_in[:, pl.ds(pl.multiple_of(2 * D + VD + who * VW, VW), VW)]
             if not aligned:
-                up[...] = w_up[:, pl.ds(pl.multiple_of(who * FW, FW), FW)]
+                gate[:, VW:] = w_up[:, pl.ds(pl.multiple_of(who * FW, FW), FW)]
                 continue
             for i in range(G):
                 src = pl.multiple_of((i * size + who) * FR, FR)
-                up[:, i * FR : (i + 1) * FR] = w_up[:, pl.ds(src, FR)]
-
-    outs = [like((rows, 2 * QW + VW), bf16), like((rows, VW), bf16), like((rows, FW), bf16)] * size
-    outs = [*outs, like(proj_out.shape, bf16)]
+                gate[:, VW + i * FR : VW + (i + 1) * FR] = w_up[:, pl.ds(src, FR)]
+
+    outs = [like((rows, 2 * QW + VW), bf16), like((rows, VW + FW), bf16)] * size
     return call(
         body,
         info,
-        [proj_in, ffn_up, proj_out],
+        [proj_in, ffn_up],
         outs,
-        in_specs=[VMEM] * 3,
+        in_specs=[VMEM] * 2,
         out_specs=[VMEM] * len(outs),
         name="split_columns",
     )
 
 
-def join_pieces(info, parts, extra, fold, after=()):
+def join_pieces(info, parts, extra, fold, after=(), first=0, width=None):
     size = len(parts)
-    rows, width = parts[0].shape
+    rows, width = parts[0].shape[0], width or parts[0].shape[1]
     wide = 0 if extra is None else extra.shape[1] // fold
 
     def body(at, *refs):
         out = refs[-1]
         for gap in range(size):
-            out[pl.ds(pl.multiple_of((at[0] ^ gap) * rows, rows), rows), :width] = refs[gap][...]
+            out[pl.ds(pl.multiple_of((at[0] ^ gap) * rows, rows), rows), :width] = refs[gap][:, first : first + width]
         if extra is not None:
             short = size * rows // fold
             for c in range(fold):
@@ -777,7 +802,7 @@
     return [part if gap == 0 else swap_seq(part, gap) for gap, part in enumerate(parts)]
 
 
-def join_in_columns(info, qkvs, gates, H, QW, VW):
+def join_in_columns(info, qkvs, gates, H, QW, VW, after=()):
     size = len(qkvs)
     rows = qkvs[0].shape[0]
 
@@ -804,6 +829,7 @@
         in_specs=[VMEM] * len(ins),
         out_specs=VMEM,
         name="join_in_columns",
+        after=after,
     )
 
 
@@ -1020,31 +1046,36 @@
     fold = S // 2
     info = make_info()
 
+    to_rank = [(j * G + t, shard_place(t, G) * S + j) for j in range(S) for t in range(G)]
+    parts = split_columns(info, proj_in, ffn_up, H, QW, VW, FW)
+
     vectors = jnp.stack([norm1_gain, norm1_shift, norm2_gain, norm2_shift])
-    norms, norms_dp = gather_all(vectors)
-    norms = norms.transpose(1, 0, 2).reshape(4, 1, D).astype(f32)
+    norms = GatherAll(tie(vectors, parts[0]))
+    while norms.gaps:
+        norms.step()
+    norms = norms.held.transpose(2, 0, 1, 3).reshape(4, 1, D).astype(f32)
     gain_one, shift_one, gain_two, shift_two = norms
 
-    to_rank = [(j * G + t, shard_place(t, G) * S + j) for j in range(S) for t in range(G)]
-    *parts, out_shard = split_columns(info, proj_in, ffn_up, proj_out, H, QW, VW, FW)
-    out_piece = lax.ppermute(out_shard, BOTH, to_rank)
+    out_piece = lax.ppermute(tie(proj_out, norms), BOTH, to_rank)
 
     def exchanged(own, *after):
         return [own[0]] + [
             swap_seq(tie(x, *after) if after else x, gap) for gap, x in enumerate(own) if gap
         ]
 
-    qkv_parts = exchanged(parts[0::3])
-    qkv_ring = Gather(join_pieces(info, qkv_parts, None, fold)).step()
+    qkv_parts = exchanged(parts[0::2])
+    qkv_ring = Gather(join_pieces(info, qkv_parts, None, fold, (norms,))).step()
     (normed_one,) = norm_forward(layer_in, gain_one, shift_one, (), (qkv_ring.got[0],))
     hidden_one = gather_seq(normed_one)
     early = (*qkv_ring.last, hidden_one[S // 2])
-    gate_parts, up_parts = exchanged(parts[1::3], *early), exchanged(parts[2::3], *early)
     qkv_ring.step()
-    cot = gather_seq(tie(out_grad, *qkv_ring.last))
+    gate_parts = exchanged(parts[1::2], *early)
+    cot = lax.all_gather(tie(out_grad, *early), "seq", axis=0, tiled=True)
     qkv_ring.step().step()
-    gate_piece = join_pieces(info, gate_parts, None, fold, qkv_ring.sent)
-    gate_ring = Gather(gate_piece).step().step()
+    gate_piece = join_pieces(
+        info, gate_parts, None, fold, (*qkv_ring.sent, hidden_one[1], hidden_one[S - 1]), 0, VW
+    )
+    gate_ring = Gather(gate_piece).step().step(*qkv_ring.last)
     out_ring = Gather(tie(out_piece, *gate_ring.sent)).step()
 
     factor = jnp.power(10000.0, -jnp.arange(HALF, dtype=f32) / (HALF - 1))
@@ -1062,34 +1093,40 @@
         [(0, 2 * QW, f32), (2 * QW, VW, bf16)],
         False,
         "project_qkv",
-        (*gate_ring.sent, *out_ring.sent, cosine, sine, *cot.values()),
+        (*gate_ring.sent, *out_ring.sent, cosine, sine),
     )
     w_qk = Weight(qkv_ring, 1, 0, 2 * QW)
     w_v = Weight(qkv_ring, 1, 2 * QW, VW)
+    gate_ring.step(qk_pre)
+    out_ring.step(qk_pre)
+    gate_ring.step()
     out_ring.step()
     w_g = Weight(gate_ring)
-    ffn_ring = Gather(join_pieces(info, up_parts, ffn_down, fold, out_ring.sent)).step()
     (gate_pre,) = tokens_times(
-        info, hidden_one, w_g, [(0, VW, f32)], False, "project_gate", ffn_ring.sent
-    )
+        info, hidden_one, w_g, [(0, VW, f32)], False, "project_gate", out_ring.sent
+    )
+    out_ring.step(gate_pre)
+    ffn_ring = Gather(join_pieces(info, gate_parts, ffn_down, fold, out_ring.sent, VW, FW)).step()
     mixed, qk, retained, states, scores = retention_forward(
-        info, logs, keep, qk_pre, values, gate_pre, cosine, sine, S, T, H, out_ring.step().step().sent
+        info, logs, keep, qk_pre, values, gate_pre, cosine, sine, S, T, H,
+        (*out_ring.sent, ffn_ring.got[0]),
     )
     w_out = Weight(out_ring, shards=True)
     odd, even = [g for g in reversed(range(S)) if g & 1], [g for g in reversed(range(S)) if not g & 1]
     ffn_ring.step()
-    attn, attn_got = partial_rows(info, [(mixed, w_out, False)], odd, "attn_odd", ffn_ring.sent), {}
+    attn, attn_got = partial_rows(info, [(mixed, w_out, False)], odd, "attn_odd", (ffn_ring.got[0],)), {}
     swap_odd(attn, attn_got)
     attn |= partial_rows(info, [(mixed, w_out, False)], even, "attn_even", (attn[odd[-1]],))
     attn, attn_sent = scatter_seq(attn, attn_got)
     ffn_ring.step()
     middle, normed_two = norm_forward(layer_in, gain_two, shift_two, attn, ffn_ring.sent)
     ffn_ring.step()
-    hidden_two = gather_seq(normed_two)
     w_up = Weight(ffn_ring, 1, 0, FW)
     w_down = Weight(ffn_ring, fold, FW, 2 * D // S)
     near, far = [1, 0], list(reversed(range(2, S)))
+    hidden_two = {0: normed_two, 1: swap_seq(normed_two, 1)}
     active, grad_up, grad_two = feed_forward(info, hidden_two, cot, w_up, w_down, near)
+    hidden_two |= far_blocks(normed_two)
     two_got = {}
     swap_odd(grad_two, two_got)
     more = feed_forward(info, hidden_two, cot, w_up, w_down, far, (grad_two[0],))
@@ -1099,29 +1136,29 @@
 
     grad_two, two_sent = scatter_seq(grad_two, two_got)
     order = sorted(active)
-    active, grad_up, cot, hidden_two, hidden_one = (
-        {gap: x[gap] for gap in order} for x in (active, grad_up, cot, hidden_two, hidden_one)
+    active, grad_up, hidden_two, hidden_one = (
+        {gap: x[gap] for gap in order} for x in (active, grad_up, hidden_two, hidden_one)
     )
     ffn_sum = Scatter(
         info,
-        [Term(hidden_two, grad_up, ordered=False), Term(active, cot, fold, ordered=False)],
+        [Term(hidden_two, grad_up), Term(active, cot, fold)],
         "ffn_hop",
     ).step(two_sent)
-    down = partial_rows(info, [(active, w_down, False)], odd + even, "down", ffn_sum.sent)
-    down_got = {}
-    swap_odd(down, down_got)
+    down = partial_rows(
+        info, [(active, w_down, False)], odd + even, "down", ffn_sum.sent, True
+    )
     grad_middle, grad_attn, two_sums = norm_backward(
-        middle, gain_two, out_grad, grad_two, (f32, bf16), (down[0],)
+        middle, gain_two, out_grad, grad_two, (f32, bf16), (down, *ffn_sum.last)
     )
 
     ffn_sum.step(grad_attn)
-    grad_attn = gather_seq(grad_attn, *ffn_sum.sent)
+    grad_attn = gather_seq(grad_attn, *ffn_sum.last)
     (grad_mixed,) = tokens_times(info, grad_attn, w_out, [(0, VW, f32)], True, "grad_mixed")
     ffn_sum.step(grad_mixed)
-    down, down_sent = scatter_seq(down, down_got, ffn_sum.sent)
+    down = lax.psum_scatter(tie(down, *ffn_sum.sent), "seq", scatter_dimension=0, tiled=True)
     grad_qk, grad_v, grad_g = retention_backward(
         info, logs, keep, grad_mixed, gate_pre, retained, qk, values, states, scores, cosine, sine, S, T, H,
-        (*ffn_sum.sent, down_sent),
+        ffn_sum.sent,
     )
     gate_sum = Scatter(
         info, [Term(hidden_one, grad_g), Term(mixed, grad_attn, fold, True)], "gate_hop"
@@ -1136,10 +1173,10 @@
     grad_one |= partial_rows(info, terms_one, even, "grad_one_even", gate_sum.sent)
     grad_one, one_sent = scatter_seq(grad_one, one_got)
     qkv_sum.step(one_sent)
-    layer_out = add_up([*down, middle], bf16, qkv_sum.sent)
-    up_own, down_own = ffn_sum.own((FW, 2 * D // S), (bf16, f32), (layer_out,))
+    up_own, down_own = ffn_sum.own((FW, 2 * D // S), (bf16, f32), qkv_sum.sent)
     up_parts = exchange_rows(info, up_own)
-    gate_sum.step(up_parts[0])
+    layer_out = add_up([down, middle], bf16, (up_parts[0],))
+    gate_sum.step(layer_out)
     in_grad, one_sums = norm_backward(
         layer_in, gain_one, grad_middle, grad_one, (bf16,), gate_sum.sent
     )
@@ -1148,18 +1185,22 @@
     qkv_sum.step(in_grad)
     gate_sum.step(*qkv_sum.sent)
     up_grad = join_up_columns(info, up_parts, G, gate_sum.sent)
-    norm_afters = [qkv_sum.sent]
-    qkv_sum.step(up_grad)
+    norm_sum = ScatterAll(norm_terms.reshape(4, G, S, -1).transpose(1, 2, 0, 3))
+    for _ in seq_gaps(S):
+        norm_sum.step()
+    qkv_sum.step(up_grad, norm_sum.held)
     g_own, out_own = gate_sum.own((VW, 2 * D // S), (bf16, bf16), qkv_sum.sent)
     g_parts = exchange_rows(info, g_own)
     out_grad_w = lax.ppermute(out_own, BOTH, [(b, a) for a, b in to_rank])
-    norm_grads = scatter_all(
-        norm_terms.reshape(4, G * S, -1).transpose(1, 0, 2),
-        [*norm_afters, qkv_sum.sent, (g_own,)],
-    )
+    norm_sum.step()
+    (qkv_own,) = qkv_sum.own((2 * QW + VW,), (bf16,), (g_parts[0], norm_sum.held))
+    qkv_parts = exchange_rows(info, qkv_own)
+    norm_sum.held = tie(norm_sum.held, qkv_parts[S // 2])
+    while norm_sum.gaps:
+        norm_sum.step()
+    norm_grads = norm_sum.held[0, 0]
+    in_grad_w = join_in_columns(info, qkv_parts, g_parts, H, QW, VW, (out_grad_w,))
     out_grad_w = jnp.concatenate(jnp.split(out_grad_w, fold, axis=0), axis=1).astype(f32)
-    (qkv_own,) = qkv_sum.own((2 * QW + VW,), (bf16,))
-    in_grad_w = join_in_columns(info, exchange_rows(info, qkv_own), g_parts, H, QW, VW)
     return (
         layer_out,
         in_grad,

time: 804 us -> 763 us (0.949)
  waiting for transfers between devices: 306 us -> 235 us
  between operations: 2.14 us -> 15.7 us
  local copies, waits for them, and re-layouts: 44.1 us -> 57 us
    ppermute x42 -> x33, waiting for transfers between devices: 106 us -> 57.2 us  [swap_seq(): return lax.ppermute(x, 'seq', [(i, i ^ gap) for i in range(size)])]
    ppermute x12, waiting for transfers between devices: 25.2 us -> 5.14 us  [step(): lax.ppermute(b, 'dp', self.ahead)]
    unnamed x191 -> x194, local copies, waits for them, and re-layouts: 27.4 us -> 39 us
    ppermute x32, starting transfers between devices: 50.2 us -> 59.3 us  [step(): a, b = (lax.ppermute(a, 'dp', self.ahead), lax.ppermute(b, 'dp', self.back))]
    ppermute x32, waiting for transfers between devices: 85.2 us -> 93.6 us  [step(): a, b = (lax.ppermute(a, 'dp', self.ahead), lax.ppermute(b, 'dp', self.back))]
    pallas_call x9 -> x8, Pallas kernels: 32.4 us -> 28.1 us  [plain(): pl.pallas_call(inner, out_shape=outs, grid=grid, in_specs=[*in_specs, *[A...]
    ppermute x42 -> x33, starting transfers between devices: 21.2 us -> 20.2 us  [swap_seq(): return lax.ppermute(x, 'seq', [(i, i ^ gap) for i in range(size)])]
  transfers between devices with their start and end apart: 110 -> 103, of which waited for: 41 -> 40; matrix products, arithmetic and copies ran while one was open for 3% -> 4% of each run, Pallas kernels for 35% -> 33%
where the time goes in v3:
time: 763 us; the launch traced here: 752 us
  Pallas kernels  311 us (41%)
  waiting for transfers between devices  235 us (31%)
  starting transfers between devices  123 us (16%)
  local copies, waits for them, and re-layouts  57 us (7%)
  between operations  15.7 us (2%)
  other arithmetic  11.1 us (1%)
    pallas_call x36, Pallas kernels, call(): pl.pallas_call(inner, out_shape=outs, grid_spec=spec, name=name, cost_est...  282 us
    ppermute x32, waiting for transfers between devices, step(): a, b = (lax.ppermute(a, 'dp', self.ahead), lax.ppermute(b, 'dp', self.back))  93.6 us
    ppermute x32, starting transfers between devices, step(): a, b = (lax.ppermute(a, 'dp', self.ahead), lax.ppermute(b, 'dp', self.back))  59.3 us
    ppermute x33, waiting for transfers between devices, swap_seq(): return lax.ppermute(x, 'seq', [(i, i ^ gap) for i in range(size)])  57.2 us
    ppermute x10, waiting for transfers between devices, swap_all(): return lax.ppermute(x, BOTH, [(i, i ^ gap) for i in range(size)])  40.6 us
    unnamed x194, local copies, waits for them, and re-layouts  39 us
    ppermute x12, waiting for transfers between devices, step(): lax.ppermute(a, 'dp', self.back)  38.1 us
    pallas_call x8, Pallas kernels, plain(): pl.pallas_call(inner, out_shape=outs, grid=grid, in_specs=[*in_specs, *[A...  28.1 us
  transfers between devices with their start and end apart: 103, of which 40 were waited for; matrix products, arithmetic and copies ran while one was open for 4% of the time, Pallas kernels for 33%

profile of v3, /device:TPU:0, one launch (start us, length us, event | category | flops | bytes accessed | tf_op | source)
XLA Modules:
  0.0 752.0 jit_solution(8077470725746760306)
XLA Ops:
  40.9 22.4 %collective-permute-done.11.refs_1_.refs_5_.refs_12_.refs_22_ = bf16[256,2048]{1,0:T(8,128)(2,1)S(1)} collective-permute-done((bf16[256,2048]{1,0:T(8,128)(2,1)}, bf16[256,2048]{1,0:T(8,128)(2,1)S(1)}, u32[]{:S(2)}, u32[]{:S(2)}) %collective-permute-start.11) | collective-permute-done | bytes 1048608 | tf_op jit(solution)/shard_map/ppermute | solution.py:341
  71.2 15.6 %collective-permute-done.13.refs_7_.refs_14_.refs_24_ = bf16[256,2048]{1,0:T(8,128)(2,1)} collective-permute-done((bf16[256,2048]{1,0:T(8,128)(2,1)S(1)}, bf16[256,2048]{1,0:T(8,128)(2,1)}, u32[]{:S(2)}, u32[]{:S(2)}) %collective-permute-start.13) | collective-permute-done | bytes 1048608 | tf_op jit(solution)/shard_map/ppermute | solution.py:341
  93.5 16.0 %collective-permute-done.15.refs_9_.refs_16_.refs_26_ = bf16[256,2048]{1,0:T(8,128)(2,1)} collective-permute-done((bf16[256,2048]{1,0:T(8,128)(2,1)}, bf16[256,2048]{1,0:T(8,128)(2,1)}, u32[]{:S(2)}, u32[]{:S(2)}) %collective-permute-start.15) | collective-permute-done | bytes 1048608 | tf_op jit(solution)/shard_map/ppermute | solution.py:341
  133.4 7.2 collective-permute-done.22.refs_0_
  146.4 10.6 %collective-permute-start.33 = (bf16[128,2048]{1,0:T(8,128)(2,1)}, bf16[128,2048]{1,0:T(8,128)(2,1)S(1)}, u32[]{:S(2)}, u32[]{:S(2)}) collective-permute-start(bf16[128,2048]{1,0:T(8,128)(2,1)} %tie.27.refs_15_.refs_16_.refs_1_.refs_4_), channel_id=1, source_target_pairs={{4,0},{12,4},{20,12},{28,20},{24,28},{16,24},{8,16},{0,8},{5,1},{1... | collective-permute-start | bytes 1572872 | tf_op jit(solution)/shard_map/ppermute | solution.py:341
  157.0 14.9 %project_qkv.1 = (f32[1024,1024]{1,0:T(8,128)}, bf16[1024,1024]{1,0:T(8,128)(2,1)}) custom-call(s32[17]{0:T(128)} %pad_add_fusion.at, bf16[256,2048]{1,0:T(8,128)(2,1)} %norm_forward.2.refs_0_.refs_5_, bf16[256,2048]{1,0:T(8,128)(2,1)} %copy-done, bf16[256,2048]{1,0:T(8,128)(2,1)} %copy-done.1, bf16[256,2048]{1,0:T(8,128)(2,1)} %copy-done.2, ...), custom_call_target="tpu_custom_call" | custom-call | flops 8589934592 | bytes 18874368 | tf_op jit(solution)/shard_map/project_qkv/pallas_call | solution.py:45
  176.1 5.6 collective-permute-start.28
  198.7 5.6 collective-permute-done.32.refs_13_.refs_4_.refs_7_
  215.3 9.6 %project_gate.1.refs_1_.refs_4_.refs_3_ = f32[1024,1024]{1,0:T(8,128)} custom-call(s32[17]{0:T(128)} %pad_add_fusion.at, bf16[256,2048]{1,0:T(8,128)(2,1)} %norm_forward.2.refs_0_.refs_5_, bf16[256,2048]{1,0:T(8,128)(2,1)} %copy-done, bf16[256,2048]{1,0:T(8,128)(2,1)} %copy-done.1, bf16[256,2048]{1,0:T(8,128)(2,1)} %copy-done.2, ...), custom_call_target="tpu_custom_call" | custom-call | flops 4294967296 | bytes 12582912 | tf_op jit(solution)/shard_map/project_gate/pallas_call | solution.py:45
  236.4 10.2 %retention_forward.1 = (bf16[1024,1024]{1,0:T(8,128)(2,1)}, bf16[1024,1024]{1,0:T(8,128)(2,1)}, f32[1024,1024]{1,0:T(8,128)}, bf16[2,4,256,512]{3,2,1,0:T(8,128)(2,1)}, bf16[2,4,256,256]{3,2,1,0:T(8,128)(2,1)}) custom-call(s32[17]{0:T(128)} %pad_add_fusion.at, f32[2]{0:T(128)} %dynamic_slice.8.refs_0_, f32[4]{0:T(128)} %subtract_bitcast_fusion.refs_1_, ...), custom_call_target="tpu_custom_call" | custom-call | flops 1879048192 | bytes 23068696 | tf_op jit(solution)/shard_map/retention_forward/pallas_call | solution.py:45
  247.4 6.8 attn_odd.1
  254.8 4.2 collective-permute-done.42.refs_4_.refs_13_.refs_5_
  261.3 7.5 %attn_even.1 = (f32[256,2048]{1,0:T(8,128)}, f32[256,2048]{1,0:T(8,128)}) custom-call(s32[17]{0:T(128)} %pad_add_fusion.at, bf16[1024,1024]{1,0:T(8,128)(2,1)} %get-tuple-element.105.refs_0_.refs_5_, bf16[128,2048]{1,0:T(8,128)(2,1)} %tie.27.refs_15_.refs_16_.refs_1_.refs_4_, bf16[128,2048]{1,0:T(8,128)(2,1)} %tie.30.refs_2_.refs_5_, ...), custom_call_target="tpu_custom_call" | custom-call | flops 2147483648 | bytes 10485760 | tf_op jit(solution)/shard_map/attn_even/pallas_call | solution.py:45
  274.2 8.5 %collective-permute-done.43.refs_6_.refs_15_.refs_7_ = bf16[256,2048]{1,0:T(8,128)(2,1)S(1)} collective-permute-done((bf16[256,2048]{1,0:T(8,128)(2,1)S(1)}, bf16[256,2048]{1,0:T(8,128)(2,1)S(1)}, u32[]{:S(2)}, u32[]{:S(2)}) %collective-permute-start.43) | collective-permute-done | bytes 1048608 | tf_op jit(solution)/shard_map/ppermute | solution.py:341
  286.8 9.8 %collective-permute-done.41.refs_5_ = bf16[256,2048]{1,0:T(8,128)(2,1)S(1)} collective-permute-done((bf16[256,2048]{1,0:T(8,128)(2,1)}, bf16[256,2048]{1,0:T(8,128)(2,1)S(1)}, u32[]{:S(2)}, u32[]{:S(2)}) %collective-permute-start.41) | collective-permute-done | bytes 1048608 | tf_op jit(solution)/shard_map/ppermute | solution.py:78
  312.5 12.2 %collective-permute-done.46.refs_0_ = bf16[256,2048]{1,0:T(8,128)(2,1)S(1)} collective-permute-done((bf16[256,2048]{1,0:T(8,128)(2,1)}, bf16[256,2048]{1,0:T(8,128)(2,1)S(1)}, u32[]{:S(2)}, u32[]{:S(2)}) %collective-permute-start.46) | collective-permute-done | bytes 1048608 | tf_op jit(solution)/shard_map/ppermute | solution.py:78
  327.8 12.9 %feed_forward.2 = (bf16[256,1024]{1,0:T(8,128)(2,1)}, bf16[256,1024]{1,0:T(8,128)(2,1)}, bf16[256,1024]{1,0:T(8,128)(2,1)}, bf16[256,1024]{1,0:T(8,128)(2,1)}, b...) custom-call(s32[17]{0:T(128)} %pad_add_fusion.at, bf16[256,2048]{1,0:T(8,128)(2,1)} %copy-done.11, ...), custom_call_target="tpu_custom_call" | custom-call | flops 6442450944 | bytes 28311552 | tf_op jit(solution)/shard_map/feed_forward/pallas_call | solution.py:45
  341.6 13.0 %feed_forward.3 = (bf16[256,1024]{1,0:T(8,128)(2,1)}, bf16[256,1024]{1,0:T(8,128)(2,1)}, bf16[256,1024]{1,0:T(8,128)(2,1)}, bf16[256,1024]{1,0:T(8,128)(2,1)}, b...) custom-call(s32[17]{0:T(128)} %pad_add_fusion.at, bf16[256,2048]{1,0:T(8,128)(2,1)} %copy-done.8, ...), custom_call_target="tpu_custom_call" | custom-call | flops 6442450944 | bytes 28311552 | tf_op jit(solution)/shard_map/feed_forward/pallas_call | solution.py:45
  361.7 5.5 ffn_hop.5
  369.3 9.9 %down.1.refs_6_.refs_0_ = bf16[1024,2048]{1,0:T(8,128)(2,1)} custom-call(s32[17]{0:T(128)} %pad_add_fusion.at, bf16[256,1024]{1,0:T(8,128)(2,1)} %get-tuple-element.112.refs_11_.refs_0_, bf16[256,1024]{1,0:T(8,128)(2,1)} %get-tuple-element.113.refs_9_.refs_1_, bf16[256,1024]{1,0:T(8,128)(2,1)} %get-tuple-element.114.refs_10_.refs_2_, ...), custom_call_target="tpu_custom_call" | custom-call | flops 4294967296 | bytes 14680064 | tf_op jit(solution)/shard_map/down/pallas_call | solution.py:45
  382.6 4.4 collective-permute-done.57.refs_5_
  388.1 5.2 norm_backward.2
  393.3 8.5 %ffn_hop.6 = (bf16[256,2048]{1,0:T(8,128)(2,1)}, bf16[256,2048]{1,0:T(8,128)(2,1)}) custom-call(s32[17]{0:T(128)} %pad_add_fusion.at, bf16[256,2048]{1,0:T(8,128)(2,1)} %get-tuple-element.110.refs_1_.refs_0_, bf16[256,2048]{1,0:T(8,128)(2,1)} %copy-done.11, bf16[256,2048]{1,0:T(8,128)(2,1)} %tie.34.refs_1_.refs_2_, bf16[256,2048]{1,0:T(8,128)(2,1)} %copy-done.8, ...), custom_call_target="tpu_custom_call" | custom-call | flops 2147483648 | bytes 15728640 | tf_op jit(solution)/shard_map/ffn_hop/pallas_call | solution.py:45
  404.6 22.1 %collective-permute-done.58.refs_1_.refs_13_ = bf16[256,2048]{1,0:T(8,128)(2,1)S(1)} collective-permute-done((bf16[256,2048]{1,0:T(8,128)(2,1)}, bf16[256,2048]{1,0:T(8,128)(2,1)S(1)}, u32[]{:S(2)}, u32[]{:S(2)}) %collective-permute-start.58) | collective-permute-done | bytes 1048608 | tf_op jit(solution)/shard_map/ppermute | solution.py:702
  434.2 9.7 %grad_mixed.1.refs_15_.refs_2_ = f32[1024,1024]{1,0:T(8,128)} custom-call(s32[17]{0:T(128)} %pad_add_fusion.at, bf16[256,2048]{1,0:T(8,128)(2,1)} %get-tuple-element.126.refs_15_.refs_0_.refs_6_, bf16[256,2048]{1,0:T(8,128)(2,1)} %tie.36.refs_1_.refs_7_, bf16[256,2048]{1,0:T(8,128)(2,1)} %copy-done.9, bf16[256,2048]{1,0:T(8,128)(2,1)} %copy-done.10, ...), custom_call_target="tpu_custom_call" | custom-call | flops 4294967296 | bytes 12582912 | tf_op jit(solution)/shard_map/grad_mixed/pallas_call | solution.py:45
  443.8 8.8 %ffn_hop.7 = (bf16[256,2048]{1,0:T(8,128)(2,1)}, bf16[256,2048]{1,0:T(8,128)(2,1)}) custom-call(s32[17]{0:T(128)} %pad_add_fusion.at, bf16[256,2048]{1,0:T(8,128)(2,1)} %get-tuple-element.110.refs_1_.refs_0_, bf16[256,2048]{1,0:T(8,128)(2,1)} %copy-done.11, bf16[256,2048]{1,0:T(8,128)(2,1)} %tie.34.refs_1_.refs_2_, bf16[256,2048]{1,0:T(8,128)(2,1)} %copy-done.8, ...), custom_call_target="tpu_custom_call" | custom-call | flops 2147483648 | bytes 16777216 | tf_op jit(solution)/shard_map/ffn_hop/pallas_call | solution.py:45
  455.9 17.6 %retention_backward.1 = (bf16[1024,1024]{1,0:T(8,128)(2,1)}, bf16[1024,1024]{1,0:T(8,128)(2,1)}, bf16[1024,1024]{1,0:T(8,128)(2,1)}) custom-call(s32[17]{0:T(128)} %pad_add_fusion.at, f32[2]{0:T(128)} %dynamic_slice.8.refs_0_, f32[4]{0:T(128)} %subtract_bitcast_fusion.refs_1_, f32[1024,1024]{1,0:T(8,128)} %grad_mixed.1.refs_15_.refs_2_, ...), custom_call_target="tpu_custom_call" | custom-call | flops 3758096384 | bytes 27263000 | tf_op jit(solution)/shard_map/retention_backward/pallas_call | solution.py:45
  473.5 5.5 gate_hop.5
  483.2 8.8 %ffn_hop.8 = (bf16[256,2048]{1,0:T(8,128)(2,1)}, bf16[256,2048]{1,0:T(8,128)(2,1)}) custom-call(s32[17]{0:T(128)} %pad_add_fusion.at, bf16[256,2048]{1,0:T(8,128)(2,1)} %get-tuple-element.110.refs_1_.refs_0_, bf16[256,2048]{1,0:T(8,128)(2,1)} %copy-done.11, bf16[256,2048]{1,0:T(8,128)(2,1)} %tie.34.refs_1_.refs_2_, bf16[256,2048]{1,0:T(8,128)(2,1)} %copy-done.8, ...), custom_call_target="tpu_custom_call" | custom-call | flops 2147483648 | bytes 16777216 | tf_op jit(solution)/shard_map/ffn_hop/pallas_call | solution.py:45
  492.0 5.1 qkv_hop.5
  499.2 14.9 %grad_one_odd.1 = (bf16[256,2048]{1,0:T(8,128)(2,1)}, bf16[256,2048]{1,0:T(8,128)(2,1)}) custom-call(s32[17]{0:T(128)} %pad_add_fusion.at, bf16[1024,1024]{1,0:T(8,128)(2,1)} %get-tuple-element.135.refs_4_.refs_10_.refs_0_, bf16[256,1024]{1,0:T(8,128)(2,1)} %join_pieces.4.refs_4_.refs_1_, bf16[256,1024]{1,0:T(8,128)(2,1)} %tie.24.refs_1_.refs_13_.refs_5_.refs_2_, ...), custom_call_target="tpu_custom_call" | custom-call | flops 6442450944 | bytes 29360128 | tf_op jit(solution)/shard_map/grad_one_odd/pallas_call | solution.py:45
  516.3 8.4 %gate_hop.6 = (bf16[256,2048]{1,0:T(8,128)(2,1)}, bf16[256,2048]{1,0:T(8,128)(2,1)}) custom-call(s32[17]{0:T(128)} %pad_add_fusion.at, bf16[256,2048]{1,0:T(8,128)(2,1)} %norm_forward.2.refs_0_.refs_5_, bf16[256,2048]{1,0:T(8,128)(2,1)} %copy-done.1, bf16[256,2048]{1,0:T(8,128)(2,1)} %copy-done, bf16[256,2048]{1,0:T(8,128)(2,1)} %copy-done.2, ...), custom_call_target="tpu_custom_call" | custom-call | flops 2147483648 | bytes 15728640 | tf_op jit(solution)/shard_map/gate_hop/pallas_call | solution.py:45
  527.8 15.4 %grad_one_even.1 = (f32[256,2048]{1,0:T(8,128)}, f32[256,2048]{1,0:T(8,128)}) custom-call(s32[17]{0:T(128)} %pad_add_fusion.at, bf16[1024,1024]{1,0:T(8,128)(2,1)} %get-tuple-element.135.refs_4_.refs_10_.refs_0_, bf16[256,1024]{1,0:T(8,128)(2,1)} %join_pieces.4.refs_4_.refs_1_, bf16[256,1024]{1,0:T(8,128)(2,1)} %tie.24.refs_1_.refs_13_.refs_5_.refs_2_, ...), custom_call_target="tpu_custom_call" | custom-call | flops 6442450944 | bytes 31457280 | tf_op jit(solution)/shard_map/grad_one_even/pallas_call | solution.py:45
  546.2 7.9 %qkv_hop.6 = (bf16[256,2048]{1,0:T(8,128)(2,1)}, bf16[256,2048]{1,0:T(8,128)(2,1)}) custom-call(s32[17]{0:T(128)} %pad_add_fusion.at, bf16[256,2048]{1,0:T(8,128)(2,1)} %norm_forward.2.refs_0_.refs_5_, bf16[256,2048]{1,0:T(8,128)(2,1)} %copy-done.1, bf16[256,2048]{1,0:T(8,128)(2,1)} %copy-done, bf16[256,2048]{1,0:T(8,128)(2,1)} %copy-done.2, ...), custom_call_target="tpu_custom_call" | custom-call | flops 2147483648 | bytes 15728640 | tf_op jit(solution)/shard_map/qkv_hop/pallas_call | solution.py:45
  555.8 7.1 collective-permute-done.74.refs_10_
  564.4 7.0 ffn_hop.9
  576.8 8.7 %gate_hop.7 = (bf16[256,2048]{1,0:T(8,128)(2,1)}, bf16[256,2048]{1,0:T(8,128)(2,1)}) custom-call(s32[17]{0:T(128)} %pad_add_fusion.at, bf16[256,2048]{1,0:T(8,128)(2,1)} %norm_forward.2.refs_0_.refs_5_, bf16[256,2048]{1,0:T(8,128)(2,1)} %copy-done.1, bf16[256,2048]{1,0:T(8,128)(2,1)} %copy-done, bf16[256,2048]{1,0:T(8,128)(2,1)} %copy-done.2, ...), custom_call_target="tpu_custom_call" | custom-call | flops 2147483648 | bytes 16777216 | tf_op jit(solution)/shard_map/gate_hop/pallas_call | solution.py:45
  587.8 5.1 norm_backward.3
  594.0 8.4 %qkv_hop.7 = (bf16[256,2048]{1,0:T(8,128)(2,1)}, bf16[256,2048]{1,0:T(8,128)(2,1)}) custom-call(s32[17]{0:T(128)} %pad_add_fusion.at, bf16[256,2048]{1,0:T(8,128)(2,1)} %norm_forward.2.refs_0_.refs_5_, bf16[256,2048]{1,0:T(8,128)(2,1)} %copy-done.1, bf16[256,2048]{1,0:T(8,128)(2,1)} %copy-done, bf16[256,2048]{1,0:T(8,128)(2,1)} %copy-done.2, ...), custom_call_target="tpu_custom_call" | custom-call | flops 2147483648 | bytes 16777216 | tf_op jit(solution)/shard_map/qkv_hop/pallas_call | solution.py:45
  614.4 8.7 %gate_hop.8 = (bf16[256,2048]{1,0:T(8,128)(2,1)}, bf16[256,2048]{1,0:T(8,128)(2,1)}) custom-call(s32[17]{0:T(128)} %pad_add_fusion.at, bf16[256,2048]{1,0:T(8,128)(2,1)} %norm_forward.2.refs_0_.refs_5_, bf16[256,2048]{1,0:T(8,128)(2,1)} %copy-done.1, bf16[256,2048]{1,0:T(8,128)(2,1)} %copy-done, bf16[256,2048]{1,0:T(8,128)(2,1)} %copy-done.2, ...), custom_call_target="tpu_custom_call" | custom-call | flops 2147483648 | bytes 16777216 | tf_op jit(solution)/shard_map/gate_hop/pallas_call | solution.py:45
  629.0 5.3 collective-permute-done.81.refs_10_
  636.0 8.2 %qkv_hop.8 = (bf16[256,2048]{1,0:T(8,128)(2,1)}, bf16[256,2048]{1,0:T(8,128)(2,1)}) custom-call(s32[17]{0:T(128)} %pad_add_fusion.at, bf16[256,2048]{1,0:T(8,128)(2,1)} %norm_forward.2.refs_0_.refs_5_, bf16[256,2048]{1,0:T(8,128)(2,1)} %copy-done.1, bf16[256,2048]{1,0:T(8,128)(2,1)} %copy-done, bf16[256,2048]{1,0:T(8,128)(2,1)} %copy-done.2, ...), custom_call_target="tpu_custom_call" | custom-call | flops 2147483648 | bytes 16777216 | tf_op jit(solution)/shard_map/qkv_hop/pallas_call | solution.py:45
  649.0 30.8 %collective-permute-done.78 = f32[4,1,4,64]{3,2,1,0:T(4,128)S(1)} collective-permute-done((f32[4,1,4,64]{3,2,1,0:T(4,128)S(1)}, f32[4,1,4,64]{3,2,1,0:T(4,128)S(1)}, u32[]{:S(2)}, u32[]{:S(2)}) %collective-permute-start.78) | collective-permute-done | bytes 4128 | tf_op jit(solution)/shard_map/ppermute | solution.py:253
  682.4 6.8 gate_hop.9
  693.1 6.6 qkv_hop.9.refs_0_
  702.6 6.6 collective-permute-done.92.refs_1_.refs_2_
  721.7 5.8 collective-permute-start.99
  728.6 9.7 %collective-permute-done.98.refs_6_ = bf16[64,1024]{1,0:T(8,128)(2,1)S(1)} collective-permute-done((bf16[64,1024]{1,0:T(8,128)(2,1)S(1)}, bf16[64,1024]{1,0:T(8,128)(2,1)S(1)}, u32[]{:S(2)}, u32[]{:S(2)}) %collective-permute-start.98) | collective-permute-done | bytes 131104 | tf_op jit(solution)/shard_map/ppermute | solution.py:78
  (473 shorter events, 260.9 us)
Async XLA Ops:
  7.2 318.5 %all-gather.2.cloned.1.call-start = ((), (), s32[]{:S(2)}) async-start(), calls=%async_computation.1 | async-start | bytes 5242880 | tf_op jit(solution)/shard_map/all_gather | solution.py:1073
  38.9 24.5 %collective-permute-start.11 = (bf16[256,2048]{1,0:T(8,128)(2,1)}, bf16[256,2048]{1,0:T(8,128)(2,1)S(1)}, u32[]{:S(2)}, u32[]{:S(2)}) collective-permute-start(bf16[256,2048]{1,0:T(8,128)(2,1)} %join_pieces.3.refs_3_.refs_4_.refs_11_.refs_21_), channel_id=1, source_target_pairs={{0,4},{4,12},{12,20},{20,28},{28,24},{24,16},{16,8},{8,0},{1,5},{5... | collective-permute-start | bytes 3145736 | tf_op jit(solution)/shard_map/ppermute | solution.py:341
  40.7 24.3 %collective-permute-start.12 = (bf16[256,2048]{1,0:T(8,128)(2,1)}, bf16[256,2048]{1,0:T(8,128)(2,1)S(1)}, u32[]{:S(2)}, u32[]{:S(2)}) collective-permute-start(bf16[256,2048]{1,0:T(8,128)(2,1)} %join_pieces.3.refs_3_.refs_4_.refs_11_.refs_21_), channel_id=1, source_target_pairs={{4,0},{12,4},{20,12},{28,20},{24,28},{16,24},{8,16},{0,8},{5,1},{1... | collective-permute-start | bytes 3145736 | tf_op jit(solution)/shard_map/ppermute | solution.py:341
  88.8 25.8 %collective-permute-start.9 = (bf16[256,2048]{1,0:T(8,128)(2,1)}, bf16[256,2048]{1,0:T(8,128)(2,1)S(1)}, u32[]{:S(2)}, u32[]{:S(2)}) collective-permute-start(bf16[256,2048]{1,0:T(8,128)(2,1)} %norm_forward.2.refs_0_.refs_5_), channel_id=1, source_target_pairs={{0,1},{1,0},{2,3},{3,2},{4,5},{5,4},{6,7},{7,6},{8,9},{9,8},{10,11... | collective-permute-start | bytes 3145736 | tf_op jit(solution)/shard_map/ppermute | solution.py:78
  92.5 28.2 %collective-permute-start.10 = (bf16[256,2048]{1,0:T(8,128)(2,1)S(1)}, bf16[256,2048]{1,0:T(8,128)(2,1)S(1)}, u32[]{:S(2)}, u32[]{:S(2)}) collective-permute-start(bf16[256,2048]{1,0:T(8,128)(2,1)S(1)} %collective-permute-done.8.refs_3_.refs_1_.refs_2_.refs_7_), channel_id=1, source_target_pairs={{0,1},{1,0},{2,3},{3,2},{4,5},{5,4},{6,7},{7,6},{8,9},{9,8},{10,11... | collective-permute-start | bytes 3145736 | tf_op jit(solution)/shard_map/ppermute | solution.py:78
  130.5 443.5 %reduce-scatter.2.cloned.1.call-start = ((), (), s32[]{:S(2)}) async-start(), calls=%async_computation.2 | async-start | bytes 5242880 | tf_op jit(solution)/shard_map/reduce_scatter | solution.py:1158
  141.4 30.5 %collective-permute-start.25 = (bf16[256,1024]{1,0:T(8,128)(2,1)}, bf16[256,1024]{1,0:T(8,128)(2,1)S(1)}, u32[]{:S(2)}, u32[]{:S(2)}) collective-permute-start(bf16[256,1024]{1,0:T(8,128)(2,1)} %tie.24.refs_1_.refs_13_.refs_5_.refs_2_), channel_id=1, source_target_pairs={{0,4},{4,12},{12,20},{20,28},{28,24},{24,16},{16,8},{8,0},{1,5},{5... | collective-permute-start | bytes 1572872 | tf_op jit(solution)/shard_map/ppermute | solution.py:341
  143.6 31.7 %collective-permute-start.26 = (bf16[256,1024]{1,0:T(8,128)(2,1)}, bf16[256,1024]{1,0:T(8,128)(2,1)S(1)}, u32[]{:S(2)}, u32[]{:S(2)}) collective-permute-start(bf16[256,1024]{1,0:T(8,128)(2,1)} %tie.25.refs_2_.refs_14_.refs_6_.refs_3_), channel_id=1, source_target_pairs={{4,0},{12,4},{20,12},{28,20},{24,28},{16,24},{8,16},{0,8},{5,1},{1... | collective-permute-start | bytes 1572872 | tf_op jit(solution)/shard_map/ppermute | solution.py:341
  145.0 36.7 %collective-permute-start.31 = (bf16[128,2048]{1,0:T(8,128)(2,1)}, bf16[128,2048]{1,0:T(8,128)(2,1)S(1)}, u32[]{:S(2)}, u32[]{:S(2)}) collective-permute-start(bf16[128,2048]{1,0:T(8,128)(2,1)} %tie.27.refs_15_.refs_16_.refs_1_.refs_4_), channel_id=1, source_target_pairs={{0,4},{4,12},{12,20},{20,28},{28,24},{24,16},{16,8},{8,0},{1,5},{5... | collective-permute-start | bytes 1572872 | tf_op jit(solution)/shard_map/ppermute | solution.py:341
  146.4 39.1 %collective-permute-start.33 = (bf16[128,2048]{1,0:T(8,128)(2,1)}, bf16[128,2048]{1,0:T(8,128)(2,1)S(1)}, u32[]{:S(2)}, u32[]{:S(2)}) collective-permute-start(bf16[128,2048]{1,0:T(8,128)(2,1)} %tie.27.refs_15_.refs_16_.refs_1_.refs_4_), channel_id=1, source_target_pairs={{4,0},{12,4},{20,12},{28,20},{24,28},{16,24},{8,16},{0,8},{5,1},{1... | collective-permute-start | bytes 1572872 | tf_op jit(solution)/shard_map/ppermute | solution.py:341
  234.3 24.7 %collective-permute-start.42 = (bf16[256,2048]{1,0:T(8,128)(2,1)}, bf16[256,2048]{1,0:T(8,128)(2,1)S(1)}, u32[]{:S(2)}, u32[]{:S(2)}) collective-permute-start(bf16[256,2048]{1,0:T(8,128)(2,1)} %join_pieces.5.refs_9_.refs_10_.refs_3_.refs_12_.refs_4_), channel_id=1, source_target_pairs={{0,4},{4,12},{12,20},{20,28},{28,24},{24,16},{16,8},{8,0},{1,5},{5... | collective-permute-start | bytes 3145736 | tf_op jit(solution)/shard_map/ppermute | solution.py:341
  236.4 24.9 %collective-permute-start.44 = (bf16[256,2048]{1,0:T(8,128)(2,1)}, bf16[256,2048]{1,0:T(8,128)(2,1)S(1)}, u32[]{:S(2)}, u32[]{:S(2)}) collective-permute-start(bf16[256,2048]{1,0:T(8,128)(2,1)} %join_pieces.5.refs_9_.refs_10_.refs_3_.refs_12_.refs_4_), channel_id=1, source_target_pairs={{4,0},{12,4},{20,12},{28,20},{24,28},{16,24},{8,16},{0,8},{5,1},{1... | collective-permute-start | bytes 3145736 | tf_op jit(solution)/shard_map/ppermute | solution.py:341
  254.3 32.5 %collective-permute-start.39 = (bf16[256,2048]{1,0:T(8,128)(2,1)}, bf16[256,2048]{1,0:T(8,128)(2,1)S(1)}, u32[]{:S(2)}, u32[]{:S(2)}) collective-permute-start(bf16[256,2048]{1,0:T(8,128)(2,1)} %get-tuple-element.106.refs_10_), channel_id=1, source_target_pairs={{0,1},{1,0},{2,3},{3,2},{4,5},{5,4},{6,7},{7,6},{8,9},{9,8},{10,11... | collective-permute-start | bytes 3145736 | tf_op jit(solution)/shard_map/ppermute | solution.py:78
  261.3 23.9 %collective-permute-start.45 = (bf16[256,2048]{1,0:T(8,128)(2,1)S(1)}, bf16[256,2048]{1,0:T(8,128)(2,1)}, u32[]{:S(2)}, u32[]{:S(2)}) collective-permute-start(bf16[256,2048]{1,0:T(8,128)(2,1)S(1)} %collective-permute-done.44.refs_5_.refs_14_.refs_6_), channel_id=1, source_target_pairs={{4,0},{12,4},{20,12},{28,20},{24,28},{16,24},{8,16},{0,8},{5,1},{1... | collective-permute-start | bytes 3145736 | tf_op jit(solution)/shard_map/ppermute | solution.py:341
  272.7 23.9 %collective-permute-start.41 = (bf16[256,2048]{1,0:T(8,128)(2,1)}, bf16[256,2048]{1,0:T(8,128)(2,1)S(1)}, u32[]{:S(2)}, u32[]{:S(2)}) collective-permute-start(bf16[256,2048]{1,0:T(8,128)(2,1)} %add_up.4), channel_id=1, source_target_pairs={{0,2},{1,3},{2,0},{3,1},{4,6},{5,7},{6,4},{7,5},{8,10},{9,11},{10,... | collective-permute-start | bytes 3145736 | tf_op jit(solution)/shard_map/ppermute | solution.py:78
  285.2 25.0 %collective-permute-start.49 = (bf16[256,2048]{1,0:T(8,128)(2,1)}, bf16[256,2048]{1,0:T(8,128)(2,1)}, u32[]{:S(2)}, u32[]{:S(2)}) collective-permute-start(bf16[256,2048]{1,0:T(8,128)(2,1)} %collective-permute-done.45.refs_7_.refs_16_.refs_8_), channel_id=1, source_target_pairs={{4,0},{12,4},{20,12},{28,20},{24,28},{16,24},{8,16},{0,8},{5,1},{1... | collective-permute-start | bytes 3145736 | tf_op jit(solution)/shard_map/ppermute | solution.py:341
  302.0 23.8 %collective-permute-start.52 = (bf16[256,2048]{1,0:T(8,128)(2,1)}, bf16[256,2048]{1,0:T(8,128)(2,1)S(1)}, u32[]{:S(2)}, u32[]{:S(2)}) collective-permute-start(bf16[256,2048]{1,0:T(8,128)(2,1)} %get-tuple-element.110.refs_1_.refs_0_), channel_id=1, source_target_pairs={{0,1},{1,0},{2,3},{3,2},{4,5},{5,4},{6,7},{7,6},{8,9},{9,8},{10,11... | collective-permute-start | bytes 3145736 | tf_op jit(solution)/shard_map/ppermute | solution.py:78
  355.2 24.1 %collective-permute-start.56 = (bf16[256,2048]{1,0:T(8,128)(2,1)S(1)}, bf16[256,2048]{1,0:T(8,128)(2,1)S(1)}, u32[]{:S(2)}, u32[]{:S(2)}) collective-permute-start(bf16[256,2048]{1,0:T(8,128)(2,1)S(1)} %copy-done.83), channel_id=1, source_target_pairs={{0,1},{1,0},{2,3},{3,2},{4,5},{5,4},{6,7},{7,6},{8,9},{9,8},{10,11... | collective-permute-start | bytes 3145736 | tf_op jit(solution)/shard_map/ppermute | solution.py:78
  361.4 25.6 %collective-permute-start.57 = (bf16[256,2048]{1,0:T(8,128)(2,1)}, bf16[256,2048]{1,0:T(8,128)(2,1)S(1)}, u32[]{:S(2)}, u32[]{:S(2)}) collective-permute-start(bf16[256,2048]{1,0:T(8,128)(2,1)} %add_up.5.refs_13_), channel_id=1, source_target_pairs={{0,2},{1,3},{2,0},{3,1},{4,6},{5,7},{6,4},{7,5},{8,10},{9,11},{10,... | collective-permute-start | bytes 3145736 | tf_op jit(solution)/shard_map/ppermute | solution.py:78
  401.8 24.9 %collective-permute-start.58 = (bf16[256,2048]{1,0:T(8,128)(2,1)}, bf16[256,2048]{1,0:T(8,128)(2,1)S(1)}, u32[]{:S(2)}, u32[]{:S(2)}) collective-permute-start(bf16[256,2048]{1,0:T(8,128)(2,1)} %get-tuple-element.127), channel_id=1, source_target_pairs={{4,0},{12,4},{20,12},{28,20},{24,28},{16,24},{8,16},{0,8},{5,1},{1... | collective-permute-start | bytes 3145736 | tf_op jit(solution)/shard_map/ppermute | solution.py:702
  402.0 26.4 %collective-permute-start.59 = (bf16[256,2048]{1,0:T(8,128)(2,1)}, bf16[256,2048]{1,0:T(8,128)(2,1)S(1)}, u32[]{:S(2)}, u32[]{:S(2)}) collective-permute-start(bf16[256,2048]{1,0:T(8,128)(2,1)} %get-tuple-element.128), channel_id=1, source_target_pairs={{0,4},{4,12},{12,20},{20,28},{28,24},{24,16},{16,8},{8,0},{1,5},{5... | collective-permute-start | bytes 3145736 | tf_op jit(solution)/shard_map/ppermute | solution.py:702
  404.3 25.0 %collective-permute-start.60 = (bf16[256,2048]{1,0:T(8,128)(2,1)S(1)}, bf16[256,2048]{1,0:T(8,128)(2,1)S(1)}, u32[]{:S(2)}, u32[]{:S(2)}) collective-permute-start(bf16[256,2048]{1,0:T(8,128)(2,1)S(1)} %copy-done.6), channel_id=1, source_target_pairs={{0,2},{1,3},{2,0},{3,1},{4,6},{5,7},{6,4},{7,5},{8,10},{9,11},{10,... | collective-permute-start | bytes 3145736 | tf_op jit(solution)/shard_map/ppermute | solution.py:78
  404.6 25.7 %collective-permute-start.61 = (bf16[256,2048]{1,0:T(8,128)(2,1)S(1)}, bf16[256,2048]{1,0:T(8,128)(2,1)S(1)}, u32[]{:S(2)}, u32[]{:S(2)}) collective-permute-start(bf16[256,2048]{1,0:T(8,128)(2,1)S(1)} %copy-done.6), channel_id=1, source_target_pairs={{0,1},{1,0},{2,3},{3,2},{4,5},{5,4},{6,7},{7,6},{8,9},{9,8},{10,11... | collective-permute-start | bytes 3145736 | tf_op jit(solution)/shard_map/ppermute | solution.py:78
  453.9 27.3 %collective-permute-start.63 = (bf16[256,2048]{1,0:T(8,128)(2,1)S(1)}, bf16[256,2048]{1,0:T(8,128)(2,1)S(1)}, u32[]{:S(2)}, u32[]{:S(2)}) collective-permute-start(bf16[256,2048]{1,0:T(8,128)(2,1)S(1)} %copy-done.20), channel_id=1, source_target_pairs={{4,0},{12,4},{20,12},{28,20},{24,28},{16,24},{8,16},{0,8},{5,1},{1... | collective-permute-start | bytes 3145736 | tf_op jit(solution)/shard_map/ppermute | solution.py:702
  455.6 25.6 %collective-permute-start.64 = (bf16[256,2048]{1,0:T(8,128)(2,1)S(1)}, bf16[256,2048]{1,0:T(8,128)(2,1)S(1)}, u32[]{:S(2)}, u32[]{:S(2)}) collective-permute-start(bf16[256,2048]{1,0:T(8,128)(2,1)S(1)} %copy-done.19), channel_id=1, source_target_pairs={{0,4},{4,12},{12,20},{20,28},{28,24},{24,16},{16,8},{8,0},{1,5},{5... | collective-permute-start | bytes 3145736 | tf_op jit(solution)/shard_map/ppermute | solution.py:702
  479.0 35.2 %collective-permute-start.69 = (bf16[128,2048]{1,0:T(8,128)(2,1)}, bf16[128,2048]{1,0:T(8,128)(2,1)S(1)}, u32[]{:S(2)}, u32[]{:S(2)}) collective-permute-start(bf16[128,2048]{1,0:T(8,128)(2,1)} %get-tuple-element.136.refs_15_), channel_id=1, source_target_pairs={{4,0},{12,4},{20,12},{28,20},{24,28},{16,24},{8,16},{0,8},{5,1},{1... | collective-permute-start | bytes 1572872 | tf_op jit(solution)/shard_map/ppermute | solution.py:702
  480.8 35.1 %collective-permute-start.70 = (bf16[128,2048]{1,0:T(8,128)(2,1)}, bf16[128,2048]{1,0:T(8,128)(2,1)}, u32[]{:S(2)}, u32[]{:S(2)}) collective-permute-start(bf16[128,2048]{1,0:T(8,128)(2,1)} %get-tuple-element.137.refs_16_), channel_id=1, source_target_pairs={{0,4},{4,12},{12,20},{20,28},{28,24},{24,16},{16,8},{8,0},{1,5},{5... | collective-permute-start | bytes 1572872 | tf_op jit(solution)/shard_map/ppermute | solution.py:702
  497.1 27.6 %collective-permute-start.67 = (bf16[128,2048]{1,0:T(8,128)(2,1)}, bf16[128,2048]{1,0:T(8,128)(2,1)S(1)}, u32[]{:S(2)}, u32[]{:S(2)}) collective-permute-start(bf16[128,2048]{1,0:T(8,128)(2,1)} %get-tuple-element.142.refs_30_), channel_id=1, source_target_pairs={{4,0},{12,4},{20,12},{28,20},{24,28},{16,24},{8,16},{0,8},{5,1},{1... | collective-permute-start | bytes 1572872 | tf_op jit(solution)/shard_map/ppermute | solution.py:702
  498.9 27.5 %collective-permute-start.68 = (bf16[128,2048]{1,0:T(8,128)(2,1)}, bf16[128,2048]{1,0:T(8,128)(2,1)S(1)}, u32[]{:S(2)}, u32[]{:S(2)}) collective-permute-start(bf16[128,2048]{1,0:T(8,128)(2,1)} %get-tuple-element.143.refs_31_), channel_id=1, source_target_pairs={{0,4},{4,12},{12,20},{20,28},{28,24},{24,16},{16,8},{8,0},{1,5},{5... | collective-permute-start | bytes 1572872 | tf_op jit(solution)/shard_map/ppermute | solution.py:702
  514.1 29.2 %collective-permute-start.71 = (bf16[256,2048]{1,0:T(8,128)(2,1)}, bf16[256,2048]{1,0:T(8,128)(2,1)}, u32[]{:S(2)}, u32[]{:S(2)}) collective-permute-start(bf16[256,2048]{1,0:T(8,128)(2,1)} %get-tuple-element.148), channel_id=1, source_target_pairs={{0,1},{1,0},{2,3},{3,2},{4,5},{5,4},{6,7},{7,6},{8,9},{9,8},{10,11... | collective-permute-start | bytes 3145736 | tf_op jit(solution)/shard_map/ppermute | solution.py:78
  514.2 31.9 %collective-permute-start.65 = (bf16[256,2048]{1,0:T(8,128)(2,1)}, bf16[256,2048]{1,0:T(8,128)(2,1)S(1)}, u32[]{:S(2)}, u32[]{:S(2)}) collective-permute-start(bf16[256,2048]{1,0:T(8,128)(2,1)} %get-tuple-element.138.refs_10_), channel_id=1, source_target_pairs={{4,0},{12,4},{20,12},{28,20},{24,28},{16,24},{8,16},{0,8},{5,1},{1... | collective-permute-start | bytes 3145736 | tf_op jit(solution)/shard_map/ppermute | solution.py:702
  515.9 38.3 %collective-permute-start.66 = (bf16[256,2048]{1,0:T(8,128)(2,1)S(1)}, bf16[256,2048]{1,0:T(8,128)(2,1)S(1)}, u32[]{:S(2)}, u32[]{:S(2)}) collective-permute-start(bf16[256,2048]{1,0:T(8,128)(2,1)S(1)} %copy-done.37), channel_id=1, source_target_pairs={{0,4},{4,12},{12,20},{20,28},{28,24},{24,16},{16,8},{8,0},{1,5},{5... | collective-permute-start | bytes 3145736 | tf_op jit(solution)/shard_map/ppermute | solution.py:702
  524.8 38.1 %collective-permute-start.74 = (bf16[256,2048]{1,0:T(8,128)(2,1)}, bf16[256,2048]{1,0:T(8,128)(2,1)S(1)}, u32[]{:S(2)}, u32[]{:S(2)}) collective-permute-start(bf16[256,2048]{1,0:T(8,128)(2,1)} %get-tuple-element.145.refs_30_), channel_id=1, source_target_pairs={{4,0},{12,4},{20,12},{28,20},{24,28},{16,24},{8,16},{0,8},{5,1},{1... | collective-permute-start | bytes 3145736 | tf_op jit(solution)/shard_map/ppermute | solution.py:702
  527.2 49.5 %collective-permute-start.75 = (bf16[256,2048]{1,0:T(8,128)(2,1)}, bf16[256,2048]{1,0:T(8,128)(2,1)}, u32[]{:S(2)}, u32[]{:S(2)}) collective-permute-start(bf16[256,2048]{1,0:T(8,128)(2,1)} %get-tuple-element.146.refs_31_), channel_id=1, source_target_pairs={{0,4},{4,12},{12,20},{20,28},{28,24},{24,16},{16,8},{8,0},{1,5},{5... | collective-permute-start | bytes 3145736 | tf_op jit(solution)/shard_map/ppermute | solution.py:702
  543.3 43.6 %collective-permute-start.72 = (bf16[256,2048]{1,0:T(8,128)(2,1)S(1)}, bf16[256,2048]{1,0:T(8,128)(2,1)}, u32[]{:S(2)}, u32[]{:S(2)}) collective-permute-start(bf16[256,2048]{1,0:T(8,128)(2,1)S(1)} %copy-done.34), channel_id=1, source_target_pairs={{0,1},{1,0},{2,3},{3,2},{4,5},{5,4},{6,7},{7,6},{8,9},{9,8},{10,11... | collective-permute-start | bytes 3145736 | tf_op jit(solution)/shard_map/ppermute | solution.py:78
  546.1 41.7 %collective-permute-start.73 = (bf16[256,2048]{1,0:T(8,128)(2,1)}, bf16[256,2048]{1,0:T(8,128)(2,1)}, u32[]{:S(2)}, u32[]{:S(2)}) collective-permute-start(bf16[256,2048]{1,0:T(8,128)(2,1)} %add_up.6.refs_12_), channel_id=1, source_target_pairs={{0,2},{1,3},{2,0},{3,1},{4,6},{5,7},{6,4},{7,5},{8,10},{9,11},{10,... | collective-permute-start | bytes 3145736 | tf_op jit(solution)/shard_map/ppermute | solution.py:78
  554.1 39.8 %collective-permute-start.79 = (bf16[256,2048]{1,0:T(8,128)(2,1)}, bf16[256,2048]{1,0:T(8,128)(2,1)}, u32[]{:S(2)}, u32[]{:S(2)}) collective-permute-start(bf16[256,2048]{1,0:T(8,128)(2,1)} %get-tuple-element.149.refs_15_), channel_id=1, source_target_pairs={{4,0},{12,4},{20,12},{28,20},{24,28},{16,24},{8,16},{0,8},{5,1},{1... | collective-permute-start | bytes 3145736 | tf_op jit(solution)/shard_map/ppermute | solution.py:702
  562.9 31.0 %collective-permute-start.80 = (bf16[256,2048]{1,0:T(8,128)(2,1)}, bf16[256,2048]{1,0:T(8,128)(2,1)}, u32[]{:S(2)}, u32[]{:S(2)}) collective-permute-start(bf16[256,2048]{1,0:T(8,128)(2,1)} %get-tuple-element.150.refs_16_), channel_id=1, source_target_pairs={{0,4},{4,12},{12,20},{20,28},{28,24},{24,16},{16,8},{8,0},{1,5},{5... | collective-permute-start | bytes 3145736 | tf_op jit(solution)/shard_map/ppermute | solution.py:702
  585.4 26.4 %collective-permute-start.86 = (bf16[256,2048]{1,0:T(8,128)(2,1)}, bf16[256,2048]{1,0:T(8,128)(2,1)S(1)}, u32[]{:S(2)}, u32[]{:S(2)}) collective-permute-start(bf16[256,2048]{1,0:T(8,128)(2,1)} %get-tuple-element.155.refs_6_), channel_id=1, source_target_pairs={{4,0},{12,4},{20,12},{28,20},{24,28},{16,24},{8,16},{0,8},{5,1},{1... | collective-permute-start | bytes 3145736 | tf_op jit(solution)/shard_map/ppermute | solution.py:702
  586.9 26.5 %collective-permute-start.87 = (bf16[256,2048]{1,0:T(8,128)(2,1)}, bf16[256,2048]{1,0:T(8,128)(2,1)S(1)}, u32[]{:S(2)}, u32[]{:S(2)}) collective-permute-start(bf16[256,2048]{1,0:T(8,128)(2,1)} %get-tuple-element.156.refs_7_), channel_id=1, source_target_pairs={{0,4},{4,12},{12,20},{20,28},{28,24},{24,16},{16,8},{8,0},{1,5},{5... | collective-permute-start | bytes 3145736 | tf_op jit(solution)/shard_map/ppermute | solution.py:702
  602.4 31.9 %collective-permute-start.81 = (bf16[256,2048]{1,0:T(8,128)(2,1)}, bf16[256,2048]{1,0:T(8,128)(2,1)S(1)}, u32[]{:S(2)}, u32[]{:S(2)}) collective-permute-start(bf16[256,2048]{1,0:T(8,128)(2,1)} %get-tuple-element.160.refs_12_), channel_id=1, source_target_pairs={{4,0},{12,4},{20,12},{28,20},{24,28},{16,24},{8,16},{0,8},{5,1},{1... | collective-permute-start | bytes 3145736 | tf_op jit(solution)/shard_map/ppermute | solution.py:702
  603.8 32.2 %collective-permute-start.82 = (bf16[256,2048]{1,0:T(8,128)(2,1)}, bf16[256,2048]{1,0:T(8,128)(2,1)}, u32[]{:S(2)}, u32[]{:S(2)}) collective-permute-start(bf16[256,2048]{1,0:T(8,128)(2,1)} %get-tuple-element.161.refs_13_), channel_id=1, source_target_pairs={{0,4},{4,12},{12,20},{20,28},{28,24},{24,16},{16,8},{8,0},{1,5},{5... | collective-permute-start | bytes 3145736 | tf_op jit(solution)/shard_map/ppermute | solution.py:702
  623.1 57.4 %collective-permute-start.90 = (bf16[256,2048]{1,0:T(8,128)(2,1)}, bf16[256,2048]{1,0:T(8,128)(2,1)S(1)}, u32[]{:S(2)}, u32[]{:S(2)}) collective-permute-start(bf16[256,2048]{1,0:T(8,128)(2,1)} %get-tuple-element.165.refs_4_), channel_id=1, source_target_pairs={{4,0},{12,4},{20,12},{28,20},{24,28},{16,24},{8,16},{0,8},{5,1},{1... | collective-permute-start | bytes 3145736 | tf_op jit(solution)/shard_map/ppermute | solution.py:702
  624.8 55.7 %collective-permute-start.91 = (bf16[256,2048]{1,0:T(8,128)(2,1)}, bf16[256,2048]{1,0:T(8,128)(2,1)S(1)}, u32[]{:S(2)}, u32[]{:S(2)}) collective-permute-start(bf16[256,2048]{1,0:T(8,128)(2,1)} %get-tuple-element.166.refs_5_), channel_id=1, source_target_pairs={{0,4},{4,12},{12,20},{20,28},{28,24},{24,16},{16,8},{8,0},{1,5},{5... | collective-permute-start | bytes 3145736 | tf_op jit(solution)/shard_map/ppermute | solution.py:702
  644.2 47.6 %collective-permute-start.88 = (bf16[256,2048]{1,0:T(8,128)(2,1)}, bf16[256,2048]{1,0:T(8,128)(2,1)S(1)}, u32[]{:S(2)}, u32[]{:S(2)}) collective-permute-start(bf16[256,2048]{1,0:T(8,128)(2,1)} %get-tuple-element.167.refs_12_), channel_id=1, source_target_pairs={{4,0},{12,4},{20,12},{28,20},{24,28},{16,24},{8,16},{0,8},{5,1},{1... | collective-permute-start | bytes 3145736 | tf_op jit(solution)/shard_map/ppermute | solution.py:702
  645.9 45.9 %collective-permute-start.89 = (bf16[256,2048]{1,0:T(8,128)(2,1)}, bf16[256,2048]{1,0:T(8,128)(2,1)S(1)}, u32[]{:S(2)}, u32[]{:S(2)}) collective-permute-start(bf16[256,2048]{1,0:T(8,128)(2,1)} %get-tuple-element.168.refs_13_), channel_id=1, source_target_pairs={{0,4},{4,12},{12,20},{20,28},{28,24},{24,16},{16,8},{8,0},{1,5},{5... | collective-permute-start | bytes 3145736 | tf_op jit(solution)/shard_map/ppermute | solution.py:702
  646.3 33.6 %collective-permute-start.78 = (f32[4,1,4,64]{3,2,1,0:T(4,128)S(1)}, f32[4,1,4,64]{3,2,1,0:T(4,128)S(1)}, u32[]{:S(2)}, u32[]{:S(2)}) collective-permute-start(f32[4,1,4,64]{3,2,1,0:T(4,128)S(1)} %slice_select_fusion.2), channel_id=1, source_target_pairs={{0,16},{1,17},{2,18},{3,19},{4,20},{5,21},{6,22},{7,23},{8,24},{9,... | collective-permute-start | bytes 12296 | tf_op jit(solution)/shard_map/ppermute | solution.py:253
  715.9 24.1 %collective-permute-start.95 = (bf16[64,2048]{1,0:T(8,128)(2,1)S(1)}, bf16[64,2048]{1,0:T(8,128)(2,1)S(1)}, u32[]{:S(2)}, u32[]{:S(2)}) collective-permute-start(bf16[64,2048]{1,0:T(8,128)(2,1)S(1)} %copy-done.88), channel_id=1, source_target_pairs={{0,1},{1,0},{2,3},{3,2},{4,5},{5,4},{6,7},{7,6},{8,9},{9,8},{10,11... | collective-permute-start | bytes 786440 | tf_op jit(solution)/shard_map/ppermute | solution.py:78
  (151 other events, 1344.1 us)
Sparse Core Ops, SparseCore 0:
  130.6 44.0 all-gather.1
  452.8 44.4 reduce-scatter.1

commit v4 on v3

--- a/solution.py
+++ b/solution.py
@@ -1143,18 +1143,17 @@
         info,
         [Term(hidden_two, grad_up), Term(active, cot, fold)],
         "ffn_hop",
-    ).step(two_sent)
+    ).step(two_sent).step()
+    grad_middle, grad_attn, two_sums = norm_backward(
+        middle, gain_two, out_grad, grad_two, (f32, bf16), ffn_sum.sent
+    )
+
     down = partial_rows(
-        info, [(active, w_down, False)], odd + even, "down", ffn_sum.sent, True
-    )
-    grad_middle, grad_attn, two_sums = norm_backward(
-        middle, gain_two, out_grad, grad_two, (f32, bf16), (down, *ffn_sum.last)
-    )
-
-    ffn_sum.step(grad_attn)
-    grad_attn = gather_seq(grad_attn, *ffn_sum.last)
-    (grad_mixed,) = tokens_times(info, grad_attn, w_out, [(0, VW, f32)], True, "grad_mixed")
-    ffn_sum.step(grad_mixed)
+        info, [(active, w_down, False)], odd + even, "down", (grad_attn,), True
+    )
+    grad_attn = gather_seq(grad_attn, down, *ffn_sum.last)
+    ffn_sum.step(grad_attn[S // 2])
+    (grad_mixed,) = tokens_times(info, grad_attn, w_out, [(0, VW, f32)], True, "grad_mixed", ffn_sum.sent)
     down = lax.psum_scatter(tie(down, *ffn_sum.sent), "seq", scatter_dimension=0, tiled=True)
     grad_qk, grad_v, grad_g = retention_backward(
         info, logs, keep, grad_mixed, gate_pre, retained, qk, values, states, scores, cosine, sine, S, T, H,
@@ -1192,14 +1191,13 @@
     g_own, out_own = gate_sum.own((VW, 2 * D // S), (bf16, bf16), qkv_sum.sent)
     g_parts = exchange_rows(info, g_own)
     out_grad_w = lax.ppermute(out_own, BOTH, [(b, a) for a, b in to_rank])
-    norm_sum.step()
-    (qkv_own,) = qkv_sum.own((2 * QW + VW,), (bf16,), (g_parts[0], norm_sum.held))
+    (qkv_own,) = qkv_sum.own((2 * QW + VW,), (bf16,), (g_parts[0],))
     qkv_parts = exchange_rows(info, qkv_own)
-    norm_sum.held = tie(norm_sum.held, qkv_parts[S // 2])
+    norm_sum.held = tie(norm_sum.held, qkv_parts[S // 2], out_grad_w)
     while norm_sum.gaps:
         norm_sum.step()
     norm_grads = norm_sum.held[0, 0]
-    in_grad_w = join_in_columns(info, qkv_parts, g_parts, H, QW, VW, (out_grad_w,))
+    in_grad_w = join_in_columns(info, qkv_parts, g_parts, H, QW, VW)
     out_grad_w = jnp.concatenate(jnp.split(out_grad_w, fold, axis=0), axis=1).astype(f32)
     return (
         layer_out,

time: 763 us -> 739 us (0.969)
  waiting for transfers between devices: 235 us -> 206 us
  starting transfers between devices: 123 us -> 135 us
    ppermute x10, waiting for transfers between devices: 40.6 us -> 9.36 us  [swap_all(): return lax.ppermute(x, BOTH, [(i, i ^ gap) for i in range(size)])]
    ppermute x10, starting transfers between devices: 15 us -> 25.6 us  [swap_all(): return lax.ppermute(x, BOTH, [(i, i ^ gap) for i in range(size)])]
    unnamed x194 -> x188, local copies, waits for them, and re-layouts: 39 us -> 35.2 us
  transfers between devices with their start and end apart: 103 -> 103, of which waited for: 40 -> 42; matrix products, arithmetic and copies ran while one was open for 4% -> 4% of each run, Pallas kernels for 33% -> 39%
where the time goes in v4:
time: 739 us; the launch traced here: 729 us
  Pallas kernels  309 us (42%)
  waiting for transfers between devices  206 us (28%)
  starting transfers between devices  135 us (18%)
  local copies, waits for them, and re-layouts  52 us (7%)
  between operations  15.7 us (2%)
  other arithmetic  10.5 us (1%)
    pallas_call x36, Pallas kernels, call(): pl.pallas_call(inner, out_shape=outs, grid_spec=spec, name=name, cost_est...  281 us
    ppermute x32, waiting for transfers between devices, step(): a, b = (lax.ppermute(a, 'dp', self.ahead), lax.ppermute(b, 'dp', self.back))  93.1 us
    ppermute x32, starting transfers between devices, step(): a, b = (lax.ppermute(a, 'dp', self.ahead), lax.ppermute(b, 'dp', self.back))  59.4 us
    ppermute x33, waiting for transfers between devices, swap_seq(): return lax.ppermute(x, 'seq', [(i, i ^ gap) for i in range(size)])  53.8 us
    ppermute x12, waiting for transfers between devices, step(): lax.ppermute(a, 'dp', self.back)  45.6 us
    unnamed x188, local copies, waits for them, and re-layouts  35.2 us
    pallas_call x8, Pallas kernels, plain(): pl.pallas_call(inner, out_shape=outs, grid=grid, in_specs=[*in_specs, *[A...  28.1 us
    ppermute x10, starting transfers between devices, swap_all(): return lax.ppermute(x, BOTH, [(i, i ^ gap) for i in range(size)])  25.6 us
  transfers between devices with their start and end apart: 103, of which 42 were waited for; matrix products, arithmetic and copies ran while one was open for 4% of the time, Pallas kernels for 39%

profile of v4, /device:TPU:0, one launch (start us, length us, event | category | flops | bytes accessed | tf_op | source)
XLA Modules:
  0.0 729.4 jit_solution(5231633832014818044)
XLA Ops:
  40.9 22.4 %collective-permute-done.11.refs_1_.refs_5_.refs_12_.refs_22_ = bf16[256,2048]{1,0:T(8,128)(2,1)S(1)} collective-permute-done((bf16[256,2048]{1,0:T(8,128)(2,1)}, bf16[256,2048]{1,0:T(8,128)(2,1)S(1)}, u32[]{:S(2)}, u32[]{:S(2)}) %collective-permute-start.11) | collective-permute-done | bytes 1048608 | tf_op jit(solution)/shard_map/ppermute | solution.py:341
  71.2 15.6 %collective-permute-done.13.refs_7_.refs_14_.refs_24_ = bf16[256,2048]{1,0:T(8,128)(2,1)} collective-permute-done((bf16[256,2048]{1,0:T(8,128)(2,1)S(1)}, bf16[256,2048]{1,0:T(8,128)(2,1)}, u32[]{:S(2)}, u32[]{:S(2)}) %collective-permute-start.13) | collective-permute-done | bytes 1048608 | tf_op jit(solution)/shard_map/ppermute | solution.py:341
  93.5 16.0 %collective-permute-done.15.refs_9_.refs_16_.refs_26_ = bf16[256,2048]{1,0:T(8,128)(2,1)} collective-permute-done((bf16[256,2048]{1,0:T(8,128)(2,1)}, bf16[256,2048]{1,0:T(8,128)(2,1)}, u32[]{:S(2)}, u32[]{:S(2)}) %collective-permute-start.15) | collective-permute-done | bytes 1048608 | tf_op jit(solution)/shard_map/ppermute | solution.py:341
  133.5 7.1 collective-permute-done.22.refs_0_
  146.4 10.6 %collective-permute-start.33 = (bf16[128,2048]{1,0:T(8,128)(2,1)}, bf16[128,2048]{1,0:T(8,128)(2,1)S(1)}, u32[]{:S(2)}, u32[]{:S(2)}) collective-permute-start(bf16[128,2048]{1,0:T(8,128)(2,1)} %tie.27.refs_15_.refs_16_.refs_1_.refs_4_), channel_id=1, source_target_pairs={{4,0},{12,4},{20,12},{28,20},{24,28},{16,24},{8,16},{0,8},{5,1},{1... | collective-permute-start | bytes 1572872 | tf_op jit(solution)/shard_map/ppermute | solution.py:341
  157.1 14.9 %project_qkv.1 = (f32[1024,1024]{1,0:T(8,128)}, bf16[1024,1024]{1,0:T(8,128)(2,1)}) custom-call(s32[17]{0:T(128)} %pad_add_fusion.at, bf16[256,2048]{1,0:T(8,128)(2,1)} %norm_forward.2.refs_0_.refs_5_, bf16[256,2048]{1,0:T(8,128)(2,1)} %copy-done, bf16[256,2048]{1,0:T(8,128)(2,1)} %copy-done.1, bf16[256,2048]{1,0:T(8,128)(2,1)} %copy-done.2, ...), custom_call_target="tpu_custom_call" | custom-call | flops 8589934592 | bytes 18874368 | tf_op jit(solution)/shard_map/project_qkv/pallas_call | solution.py:45
  176.2 5.6 collective-permute-start.28
  198.7 5.6 collective-permute-done.32.refs_13_.refs_4_.refs_7_
  215.3 9.6 %project_gate.1.refs_1_.refs_4_.refs_3_ = f32[1024,1024]{1,0:T(8,128)} custom-call(s32[17]{0:T(128)} %pad_add_fusion.at, bf16[256,2048]{1,0:T(8,128)(2,1)} %norm_forward.2.refs_0_.refs_5_, bf16[256,2048]{1,0:T(8,128)(2,1)} %copy-done, bf16[256,2048]{1,0:T(8,128)(2,1)} %copy-done.1, bf16[256,2048]{1,0:T(8,128)(2,1)} %copy-done.2, ...), custom_call_target="tpu_custom_call" | custom-call | flops 4294967296 | bytes 12582912 | tf_op jit(solution)/shard_map/project_gate/pallas_call | solution.py:45
  236.4 10.3 %retention_forward.1 = (bf16[1024,1024]{1,0:T(8,128)(2,1)}, bf16[1024,1024]{1,0:T(8,128)(2,1)}, f32[1024,1024]{1,0:T(8,128)}, bf16[2,4,256,512]{3,2,1,0:T(8,128)(2,1)}, bf16[2,4,256,256]{3,2,1,0:T(8,128)(2,1)}) custom-call(s32[17]{0:T(128)} %pad_add_fusion.at, f32[2]{0:T(128)} %dynamic_slice.8.refs_0_, f32[4]{0:T(128)} %subtract_bitcast_fusion.refs_1_, ...), custom_call_target="tpu_custom_call" | custom-call | flops 1879048192 | bytes 23068696 | tf_op jit(solution)/shard_map/retention_forward/pallas_call | solution.py:45
  247.6 6.8 attn_odd.1
  261.3 7.5 %attn_even.1 = (f32[256,2048]{1,0:T(8,128)}, f32[256,2048]{1,0:T(8,128)}) custom-call(s32[17]{0:T(128)} %pad_add_fusion.at, bf16[1024,1024]{1,0:T(8,128)(2,1)} %get-tuple-element.105.refs_0_.refs_5_, bf16[128,2048]{1,0:T(8,128)(2,1)} %tie.27.refs_15_.refs_16_.refs_1_.refs_4_, bf16[128,2048]{1,0:T(8,128)(2,1)} %tie.30.refs_2_.refs_5_, ...), custom_call_target="tpu_custom_call" | custom-call | flops 2147483648 | bytes 10485760 | tf_op jit(solution)/shard_map/attn_even/pallas_call | solution.py:45
  274.1 8.5 %collective-permute-done.43.refs_6_.refs_15_.refs_7_ = bf16[256,2048]{1,0:T(8,128)(2,1)S(1)} collective-permute-done((bf16[256,2048]{1,0:T(8,128)(2,1)S(1)}, bf16[256,2048]{1,0:T(8,128)(2,1)S(1)}, u32[]{:S(2)}, u32[]{:S(2)}) %collective-permute-start.43) | collective-permute-done | bytes 1048608 | tf_op jit(solution)/shard_map/ppermute | solution.py:341
  286.6 9.7 %collective-permute-done.41.refs_5_ = bf16[256,2048]{1,0:T(8,128)(2,1)S(1)} collective-permute-done((bf16[256,2048]{1,0:T(8,128)(2,1)}, bf16[256,2048]{1,0:T(8,128)(2,1)S(1)}, u32[]{:S(2)}, u32[]{:S(2)}) %collective-permute-start.41) | collective-permute-done | bytes 1048608 | tf_op jit(solution)/shard_map/ppermute | solution.py:78
  297.2 4.1 norm_forward.3
  312.2 12.2 %collective-permute-done.46.refs_0_ = bf16[256,2048]{1,0:T(8,128)(2,1)S(1)} collective-permute-done((bf16[256,2048]{1,0:T(8,128)(2,1)}, bf16[256,2048]{1,0:T(8,128)(2,1)S(1)}, u32[]{:S(2)}, u32[]{:S(2)}) %collective-permute-start.46) | collective-permute-done | bytes 1048608 | tf_op jit(solution)/shard_map/ppermute | solution.py:78
  327.3 12.9 %feed_forward.2 = (bf16[256,1024]{1,0:T(8,128)(2,1)}, bf16[256,1024]{1,0:T(8,128)(2,1)}, bf16[256,1024]{1,0:T(8,128)(2,1)}, bf16[256,1024]{1,0:T(8,128)(2,1)}, b...) custom-call(s32[17]{0:T(128)} %pad_add_fusion.at, bf16[256,2048]{1,0:T(8,128)(2,1)} %copy-done.12, ...), custom_call_target="tpu_custom_call" | custom-call | flops 6442450944 | bytes 28311552 | tf_op jit(solution)/shard_map/feed_forward/pallas_call | solution.py:45
  341.2 12.9 %feed_forward.3 = (bf16[256,1024]{1,0:T(8,128)(2,1)}, bf16[256,1024]{1,0:T(8,128)(2,1)}, bf16[256,1024]{1,0:T(8,128)(2,1)}, bf16[256,1024]{1,0:T(8,128)(2,1)}, b...) custom-call(s32[17]{0:T(128)} %pad_add_fusion.at, bf16[256,2048]{1,0:T(8,128)(2,1)} %copy-done.8, ...), custom_call_target="tpu_custom_call" | custom-call | flops 6442450944 | bytes 28311552 | tf_op jit(solution)/shard_map/feed_forward/pallas_call | solution.py:45
  361.2 5.5 ffn_hop.5
  368.8 12.1 %collective-permute-done.56.refs_13_ = bf16[128,2048]{1,0:T(8,128)(2,1)S(1)} collective-permute-done((bf16[128,2048]{1,0:T(8,128)(2,1)}, bf16[128,2048]{1,0:T(8,128)(2,1)S(1)}, u32[]{:S(2)}, u32[]{:S(2)}) %collective-permute-start.56) | collective-permute-done | bytes 524320 | tf_op jit(solution)/shard_map/ppermute | solution.py:702
  383.0 8.4 %ffn_hop.6 = (bf16[256,2048]{1,0:T(8,128)(2,1)}, bf16[256,2048]{1,0:T(8,128)(2,1)}) custom-call(s32[17]{0:T(128)} %pad_add_fusion.at, bf16[256,2048]{1,0:T(8,128)(2,1)} %get-tuple-element.110.refs_1_.refs_0_, bf16[256,2048]{1,0:T(8,128)(2,1)} %copy-done.12, bf16[256,2048]{1,0:T(8,128)(2,1)} %tie.34.refs_1_.refs_2_, bf16[256,2048]{1,0:T(8,128)(2,1)} %copy-done.8, ...), custom_call_target="tpu_custom_call" | custom-call | flops 2147483648 | bytes 15728640 | tf_op jit(solution)/shard_map/ffn_hop/pallas_call | solution.py:45
  394.8 5.2 norm_backward.2
  401.8 10.0 %down.1.refs_1_.refs_0_ = bf16[1024,2048]{1,0:T(8,128)(2,1)} custom-call(s32[17]{0:T(128)} %pad_add_fusion.at, bf16[256,1024]{1,0:T(8,128)(2,1)} %get-tuple-element.112.refs_11_.refs_0_, bf16[256,1024]{1,0:T(8,128)(2,1)} %get-tuple-element.113.refs_9_.refs_1_, bf16[256,1024]{1,0:T(8,128)(2,1)} %get-tuple-element.114.refs_10_.refs_2_, ...), custom_call_target="tpu_custom_call" | custom-call | flops 4294967296 | bytes 14680064 | tf_op jit(solution)/shard_map/down/pallas_call | solution.py:45
  411.8 4.1 collective-permute-done.58.refs_2_.refs_13_
  417.1 6.9 collective-permute-done.60.refs_0_
  425.0 8.8 %ffn_hop.7 = (bf16[256,2048]{1,0:T(8,128)(2,1)}, bf16[256,2048]{1,0:T(8,128)(2,1)}) custom-call(s32[17]{0:T(128)} %pad_add_fusion.at, bf16[256,2048]{1,0:T(8,128)(2,1)} %get-tuple-element.110.refs_1_.refs_0_, bf16[256,2048]{1,0:T(8,128)(2,1)} %copy-done.12, bf16[256,2048]{1,0:T(8,128)(2,1)} %tie.34.refs_1_.refs_2_, bf16[256,2048]{1,0:T(8,128)(2,1)} %copy-done.8, ...), custom_call_target="tpu_custom_call" | custom-call | flops 2147483648 | bytes 16777216 | tf_op jit(solution)/shard_map/ffn_hop/pallas_call | solution.py:45
  440.2 10.2 %grad_mixed.1.refs_2_ = f32[1024,1024]{1,0:T(8,128)} custom-call(s32[17]{0:T(128)} %pad_add_fusion.at, bf16[256,2048]{1,0:T(8,128)(2,1)} %get-tuple-element.128.refs_13_.refs_0_.refs_6_, bf16[256,2048]{1,0:T(8,128)(2,1)} %tie.36.refs_15_.refs_1_.refs_7_, bf16[256,2048]{1,0:T(8,128)(2,1)} %copy-done.10, bf16[256,2048]{1,0:T(8,128)(2,1)} %copy-done.11, ...), custom_call_target="tpu_custom_call" | custom-call | flops 4294967296 | bytes 12582912 | tf_op jit(solution)/shard_map/grad_mixed/pallas_call | solution.py:45
  450.4 16.2 %retention_backward.1 = (bf16[1024,1024]{1,0:T(8,128)(2,1)}, bf16[1024,1024]{1,0:T(8,128)(2,1)}, bf16[1024,1024]{1,0:T(8,128)(2,1)}) custom-call(s32[17]{0:T(128)} %pad_add_fusion.at, f32[2]{0:T(128)} %dynamic_slice.8.refs_0_, f32[4]{0:T(128)} %subtract_bitcast_fusion.refs_1_, f32[1024,1024]{1,0:T(8,128)} %grad_mixed.1.refs_2_, ...), custom_call_target="tpu_custom_call" | custom-call | flops 3758096384 | bytes 27263000 | tf_op jit(solution)/shard_map/retention_backward/pallas_call | solution.py:45
  466.6 5.5 gate_hop.5
  474.3 8.7 %ffn_hop.8 = (bf16[256,2048]{1,0:T(8,128)(2,1)}, bf16[256,2048]{1,0:T(8,128)(2,1)}) custom-call(s32[17]{0:T(128)} %pad_add_fusion.at, bf16[256,2048]{1,0:T(8,128)(2,1)} %get-tuple-element.110.refs_1_.refs_0_, bf16[256,2048]{1,0:T(8,128)(2,1)} %copy-done.12, bf16[256,2048]{1,0:T(8,128)(2,1)} %tie.34.refs_1_.refs_2_, bf16[256,2048]{1,0:T(8,128)(2,1)} %copy-done.8, ...), custom_call_target="tpu_custom_call" | custom-call | flops 2147483648 | bytes 16777216 | tf_op jit(solution)/shard_map/ffn_hop/pallas_call | solution.py:45
  483.0 5.1 qkv_hop.5
  490.4 14.4 %grad_one_odd.1 = (bf16[256,2048]{1,0:T(8,128)(2,1)}, bf16[256,2048]{1,0:T(8,128)(2,1)}) custom-call(s32[17]{0:T(128)} %pad_add_fusion.at, bf16[1024,1024]{1,0:T(8,128)(2,1)} %get-tuple-element.135.refs_4_.refs_10_.refs_0_, bf16[256,1024]{1,0:T(8,128)(2,1)} %join_pieces.4.refs_4_.refs_1_, bf16[256,1024]{1,0:T(8,128)(2,1)} %tie.24.refs_1_.refs_13_.refs_5_.refs_2_, ...), custom_call_target="tpu_custom_call" | custom-call | flops 6442450944 | bytes 29360128 | tf_op jit(solution)/shard_map/grad_one_odd/pallas_call | solution.py:45
  507.1 8.4 %gate_hop.6 = (bf16[256,2048]{1,0:T(8,128)(2,1)}, bf16[256,2048]{1,0:T(8,128)(2,1)}) custom-call(s32[17]{0:T(128)} %pad_add_fusion.at, bf16[256,2048]{1,0:T(8,128)(2,1)} %norm_forward.2.refs_0_.refs_5_, bf16[256,2048]{1,0:T(8,128)(2,1)} %copy-done.1, bf16[256,2048]{1,0:T(8,128)(2,1)} %copy-done, bf16[256,2048]{1,0:T(8,128)(2,1)} %copy-done.2, ...), custom_call_target="tpu_custom_call" | custom-call | flops 2147483648 | bytes 15728640 | tf_op jit(solution)/shard_map/gate_hop/pallas_call | solution.py:45
  518.6 15.0 %grad_one_even.1 = (f32[256,2048]{1,0:T(8,128)}, f32[256,2048]{1,0:T(8,128)}) custom-call(s32[17]{0:T(128)} %pad_add_fusion.at, bf16[1024,1024]{1,0:T(8,128)(2,1)} %get-tuple-element.135.refs_4_.refs_10_.refs_0_, bf16[256,1024]{1,0:T(8,128)(2,1)} %join_pieces.4.refs_4_.refs_1_, bf16[256,1024]{1,0:T(8,128)(2,1)} %tie.24.refs_1_.refs_13_.refs_5_.refs_2_, ...), custom_call_target="tpu_custom_call" | custom-call | flops 6442450944 | bytes 31457280 | tf_op jit(solution)/shard_map/grad_one_even/pallas_call | solution.py:45
  538.3 7.9 %qkv_hop.6 = (bf16[256,2048]{1,0:T(8,128)(2,1)}, bf16[256,2048]{1,0:T(8,128)(2,1)}) custom-call(s32[17]{0:T(128)} %pad_add_fusion.at, bf16[256,2048]{1,0:T(8,128)(2,1)} %norm_forward.2.refs_0_.refs_5_, bf16[256,2048]{1,0:T(8,128)(2,1)} %copy-done.1, bf16[256,2048]{1,0:T(8,128)(2,1)} %copy-done, bf16[256,2048]{1,0:T(8,128)(2,1)} %copy-done.2, ...), custom_call_target="tpu_custom_call" | custom-call | flops 2147483648 | bytes 15728640 | tf_op jit(solution)/shard_map/qkv_hop/pallas_call | solution.py:45
  548.0 5.5 collective-permute-done.74.refs_10_
  555.8 7.2 ffn_hop.9
  568.2 8.7 %gate_hop.7 = (bf16[256,2048]{1,0:T(8,128)(2,1)}, bf16[256,2048]{1,0:T(8,128)(2,1)}) custom-call(s32[17]{0:T(128)} %pad_add_fusion.at, bf16[256,2048]{1,0:T(8,128)(2,1)} %norm_forward.2.refs_0_.refs_5_, bf16[256,2048]{1,0:T(8,128)(2,1)} %copy-done.1, bf16[256,2048]{1,0:T(8,128)(2,1)} %copy-done, bf16[256,2048]{1,0:T(8,128)(2,1)} %copy-done.2, ...), custom_call_target="tpu_custom_call" | custom-call | flops 2147483648 | bytes 16777216 | tf_op jit(solution)/shard_map/gate_hop/pallas_call | solution.py:45
  579.2 5.2 norm_backward.3
  585.5 8.4 %qkv_hop.7 = (bf16[256,2048]{1,0:T(8,128)(2,1)}, bf16[256,2048]{1,0:T(8,128)(2,1)}) custom-call(s32[17]{0:T(128)} %pad_add_fusion.at, bf16[256,2048]{1,0:T(8,128)(2,1)} %norm_forward.2.refs_0_.refs_5_, bf16[256,2048]{1,0:T(8,128)(2,1)} %copy-done.1, bf16[256,2048]{1,0:T(8,128)(2,1)} %copy-done, bf16[256,2048]{1,0:T(8,128)(2,1)} %copy-done.2, ...), custom_call_target="tpu_custom_call" | custom-call | flops 2147483648 | bytes 16777216 | tf_op jit(solution)/shard_map/qkv_hop/pallas_call | solution.py:45
  605.7 8.7 %gate_hop.8 = (bf16[256,2048]{1,0:T(8,128)(2,1)}, bf16[256,2048]{1,0:T(8,128)(2,1)}) custom-call(s32[17]{0:T(128)} %pad_add_fusion.at, bf16[256,2048]{1,0:T(8,128)(2,1)} %norm_forward.2.refs_0_.refs_5_, bf16[256,2048]{1,0:T(8,128)(2,1)} %copy-done.1, bf16[256,2048]{1,0:T(8,128)(2,1)} %copy-done, bf16[256,2048]{1,0:T(8,128)(2,1)} %copy-done.2, ...), custom_call_target="tpu_custom_call" | custom-call | flops 2147483648 | bytes 16777216 | tf_op jit(solution)/shard_map/gate_hop/pallas_call | solution.py:45
  626.7 8.2 %qkv_hop.8 = (bf16[256,2048]{1,0:T(8,128)(2,1)}, bf16[256,2048]{1,0:T(8,128)(2,1)}) custom-call(s32[17]{0:T(128)} %pad_add_fusion.at, bf16[256,2048]{1,0:T(8,128)(2,1)} %norm_forward.2.refs_0_.refs_5_, bf16[256,2048]{1,0:T(8,128)(2,1)} %copy-done.1, bf16[256,2048]{1,0:T(8,128)(2,1)} %copy-done, bf16[256,2048]{1,0:T(8,128)(2,1)} %copy-done.2, ...), custom_call_target="tpu_custom_call" | custom-call | flops 2147483648 | bytes 16777216 | tf_op jit(solution)/shard_map/qkv_hop/pallas_call | solution.py:45
  637.0 11.2 %collective-permute-done.89.refs_10_ = bf16[256,2048]{1,0:T(8,128)(2,1)S(1)} collective-permute-done((bf16[256,2048]{1,0:T(8,128)(2,1)}, bf16[256,2048]{1,0:T(8,128)(2,1)S(1)}, u32[]{:S(2)}, u32[]{:S(2)}) %collective-permute-start.89) | collective-permute-done | bytes 1048608 | tf_op jit(solution)/shard_map/ppermute | solution.py:702
  650.2 6.9 gate_hop.9
  661.6 7.3 %collective-permute-done.87.refs_10_ = bf16[256,2048]{1,0:T(8,128)(2,1)S(1)} collective-permute-done((bf16[256,2048]{1,0:T(8,128)(2,1)}, bf16[256,2048]{1,0:T(8,128)(2,1)S(1)}, u32[]{:S(2)}, u32[]{:S(2)}) %collective-permute-start.87) | collective-permute-done | bytes 1048608 | tf_op jit(solution)/shard_map/ppermute | solution.py:702
  670.3 6.7 qkv_hop.9.refs_0_
  682.9 11.3 %collective-permute-done.91.refs_1_.refs_2_ = bf16[64,2048]{1,0:T(8,128)(2,1)S(1)} collective-permute-done((bf16[64,2048]{1,0:T(8,128)(2,1)}, bf16[64,2048]{1,0:T(8,128)(2,1)S(1)}, u32[]{:S(2)}, u32[]{:S(2)}) %collective-permute-start.91) | collective-permute-done | bytes 262176 | tf_op jit(solution)/shard_map/ppermute | solution.py:78
  698.1 8.9 %collective-permute-start.93 = (f32[4,1,4,64]{3,2,1,0:T(4,128)S(1)}, f32[4,1,4,64]{3,2,1,0:T(4,128)S(1)}, u32[]{:S(2)}, u32[]{:S(2)}) collective-permute-start(f32[4,1,4,64]{3,2,1,0:T(4,128)S(1)} %slice_select_fusion.2), channel_id=1, source_target_pairs={{0,16},{1,17},{2,18},{3,19},{4,20},{5,21},{6,22},{7,23},{8,24},{9,... | collective-permute-start | bytes 12296 | tf_op jit(solution)/shard_map/ppermute | solution.py:253
  (467 shorter events, 264.6 us)
Async XLA Ops:
  7.2 318.1 %all-gather.2.cloned.1.call-start = ((), (), s32[]{:S(2)}) async-start(), calls=%async_computation.1 | async-start | bytes 5242880 | tf_op jit(solution)/shard_map/all_gather | solution.py:1073
  38.9 24.5 %collective-permute-start.11 = (bf16[256,2048]{1,0:T(8,128)(2,1)}, bf16[256,2048]{1,0:T(8,128)(2,1)S(1)}, u32[]{:S(2)}, u32[]{:S(2)}) collective-permute-start(bf16[256,2048]{1,0:T(8,128)(2,1)} %join_pieces.3.refs_3_.refs_4_.refs_11_.refs_21_), channel_id=1, source_target_pairs={{0,4},{4,12},{12,20},{20,28},{28,24},{24,16},{16,8},{8,0},{1,5},{5... | collective-permute-start | bytes 3145736 | tf_op jit(solution)/shard_map/ppermute | solution.py:341
  40.7 24.3 %collective-permute-start.12 = (bf16[256,2048]{1,0:T(8,128)(2,1)}, bf16[256,2048]{1,0:T(8,128)(2,1)S(1)}, u32[]{:S(2)}, u32[]{:S(2)}) collective-permute-start(bf16[256,2048]{1,0:T(8,128)(2,1)} %join_pieces.3.refs_3_.refs_4_.refs_11_.refs_21_), channel_id=1, source_target_pairs={{4,0},{12,4},{20,12},{28,20},{24,28},{16,24},{8,16},{0,8},{5,1},{1... | collective-permute-start | bytes 3145736 | tf_op jit(solution)/shard_map/ppermute | solution.py:341
  88.8 25.8 %collective-permute-start.9 = (bf16[256,2048]{1,0:T(8,128)(2,1)}, bf16[256,2048]{1,0:T(8,128)(2,1)S(1)}, u32[]{:S(2)}, u32[]{:S(2)}) collective-permute-start(bf16[256,2048]{1,0:T(8,128)(2,1)} %norm_forward.2.refs_0_.refs_5_), channel_id=1, source_target_pairs={{0,1},{1,0},{2,3},{3,2},{4,5},{5,4},{6,7},{7,6},{8,9},{9,8},{10,11... | collective-permute-start | bytes 3145736 | tf_op jit(solution)/shard_map/ppermute | solution.py:78
  92.5 28.2 %collective-permute-start.10 = (bf16[256,2048]{1,0:T(8,128)(2,1)S(1)}, bf16[256,2048]{1,0:T(8,128)(2,1)S(1)}, u32[]{:S(2)}, u32[]{:S(2)}) collective-permute-start(bf16[256,2048]{1,0:T(8,128)(2,1)S(1)} %collective-permute-done.8.refs_3_.refs_1_.refs_2_.refs_7_), channel_id=1, source_target_pairs={{0,1},{1,0},{2,3},{3,2},{4,5},{5,4},{6,7},{7,6},{8,9},{9,8},{10,11... | collective-permute-start | bytes 3145736 | tf_op jit(solution)/shard_map/ppermute | solution.py:78
  130.5 435.0 %reduce-scatter.2.cloned.1.call-start = ((), (), s32[]{:S(2)}) async-start(), calls=%async_computation.2 | async-start | bytes 5242880 | tf_op jit(solution)/shard_map/reduce_scatter | solution.py:1157
  141.4 30.6 %collective-permute-start.25 = (bf16[256,1024]{1,0:T(8,128)(2,1)}, bf16[256,1024]{1,0:T(8,128)(2,1)S(1)}, u32[]{:S(2)}, u32[]{:S(2)}) collective-permute-start(bf16[256,1024]{1,0:T(8,128)(2,1)} %tie.24.refs_1_.refs_13_.refs_5_.refs_2_), channel_id=1, source_target_pairs={{0,4},{4,12},{12,20},{20,28},{28,24},{24,16},{16,8},{8,0},{1,5},{5... | collective-permute-start | bytes 1572872 | tf_op jit(solution)/shard_map/ppermute | solution.py:341
  143.6 31.8 %collective-permute-start.26 = (bf16[256,1024]{1,0:T(8,128)(2,1)}, bf16[256,1024]{1,0:T(8,128)(2,1)S(1)}, u32[]{:S(2)}, u32[]{:S(2)}) collective-permute-start(bf16[256,1024]{1,0:T(8,128)(2,1)} %tie.25.refs_2_.refs_14_.refs_6_.refs_3_), channel_id=1, source_target_pairs={{4,0},{12,4},{20,12},{28,20},{24,28},{16,24},{8,16},{0,8},{5,1},{1... | collective-permute-start | bytes 1572872 | tf_op jit(solution)/shard_map/ppermute | solution.py:341
  145.0 36.7 %collective-permute-start.31 = (bf16[128,2048]{1,0:T(8,128)(2,1)}, bf16[128,2048]{1,0:T(8,128)(2,1)S(1)}, u32[]{:S(2)}, u32[]{:S(2)}) collective-permute-start(bf16[128,2048]{1,0:T(8,128)(2,1)} %tie.27.refs_15_.refs_16_.refs_1_.refs_4_), channel_id=1, source_target_pairs={{0,4},{4,12},{12,20},{20,28},{28,24},{24,16},{16,8},{8,0},{1,5},{5... | collective-permute-start | bytes 1572872 | tf_op jit(solution)/shard_map/ppermute | solution.py:341
  146.4 39.1 %collective-permute-start.33 = (bf16[128,2048]{1,0:T(8,128)(2,1)}, bf16[128,2048]{1,0:T(8,128)(2,1)S(1)}, u32[]{:S(2)}, u32[]{:S(2)}) collective-permute-start(bf16[128,2048]{1,0:T(8,128)(2,1)} %tie.27.refs_15_.refs_16_.refs_1_.refs_4_), channel_id=1, source_target_pairs={{4,0},{12,4},{20,12},{28,20},{24,28},{16,24},{8,16},{0,8},{5,1},{1... | collective-permute-start | bytes 1572872 | tf_op jit(solution)/shard_map/ppermute | solution.py:341
  234.3 24.7 %collective-permute-start.42 = (bf16[256,2048]{1,0:T(8,128)(2,1)}, bf16[256,2048]{1,0:T(8,128)(2,1)S(1)}, u32[]{:S(2)}, u32[]{:S(2)}) collective-permute-start(bf16[256,2048]{1,0:T(8,128)(2,1)} %join_pieces.5.refs_9_.refs_10_.refs_3_.refs_12_.refs_4_), channel_id=1, source_target_pairs={{0,4},{4,12},{12,20},{20,28},{28,24},{24,16},{16,8},{8,0},{1,5},{5... | collective-permute-start | bytes 3145736 | tf_op jit(solution)/shard_map/ppermute | solution.py:341
  236.4 24.8 %collective-permute-start.44 = (bf16[256,2048]{1,0:T(8,128)(2,1)}, bf16[256,2048]{1,0:T(8,128)(2,1)S(1)}, u32[]{:S(2)}, u32[]{:S(2)}) collective-permute-start(bf16[256,2048]{1,0:T(8,128)(2,1)} %join_pieces.5.refs_9_.refs_10_.refs_3_.refs_12_.refs_4_), channel_id=1, source_target_pairs={{4,0},{12,4},{20,12},{28,20},{24,28},{16,24},{8,16},{0,8},{5,1},{1... | collective-permute-start | bytes 3145736 | tf_op jit(solution)/shard_map/ppermute | solution.py:341
  254.5 32.1 %collective-permute-start.39 = (bf16[256,2048]{1,0:T(8,128)(2,1)}, bf16[256,2048]{1,0:T(8,128)(2,1)S(1)}, u32[]{:S(2)}, u32[]{:S(2)}) collective-permute-start(bf16[256,2048]{1,0:T(8,128)(2,1)} %get-tuple-element.106.refs_10_), channel_id=1, source_target_pairs={{0,1},{1,0},{2,3},{3,2},{4,5},{5,4},{6,7},{7,6},{8,9},{9,8},{10,11... | collective-permute-start | bytes 3145736 | tf_op jit(solution)/shard_map/ppermute | solution.py:78
  261.3 23.7 %collective-permute-start.45 = (bf16[256,2048]{1,0:T(8,128)(2,1)S(1)}, bf16[256,2048]{1,0:T(8,128)(2,1)}, u32[]{:S(2)}, u32[]{:S(2)}) collective-permute-start(bf16[256,2048]{1,0:T(8,128)(2,1)S(1)} %collective-permute-done.44.refs_5_.refs_14_.refs_6_), channel_id=1, source_target_pairs={{4,0},{12,4},{20,12},{28,20},{24,28},{16,24},{8,16},{0,8},{5,1},{1... | collective-permute-start | bytes 3145736 | tf_op jit(solution)/shard_map/ppermute | solution.py:341
  272.5 23.8 %collective-permute-start.41 = (bf16[256,2048]{1,0:T(8,128)(2,1)}, bf16[256,2048]{1,0:T(8,128)(2,1)S(1)}, u32[]{:S(2)}, u32[]{:S(2)}) collective-permute-start(bf16[256,2048]{1,0:T(8,128)(2,1)} %add_up.4), channel_id=1, source_target_pairs={{0,2},{1,3},{2,0},{3,1},{4,6},{5,7},{6,4},{7,5},{8,10},{9,11},{10,... | collective-permute-start | bytes 3145736 | tf_op jit(solution)/shard_map/ppermute | solution.py:78
  285.0 24.8 %collective-permute-start.49 = (bf16[256,2048]{1,0:T(8,128)(2,1)}, bf16[256,2048]{1,0:T(8,128)(2,1)}, u32[]{:S(2)}, u32[]{:S(2)}) collective-permute-start(bf16[256,2048]{1,0:T(8,128)(2,1)} %collective-permute-done.45.refs_7_.refs_16_.refs_8_), channel_id=1, source_target_pairs={{4,0},{12,4},{20,12},{28,20},{24,28},{16,24},{8,16},{0,8},{5,1},{1... | collective-permute-start | bytes 3145736 | tf_op jit(solution)/shard_map/ppermute | solution.py:341
  301.7 23.6 %collective-permute-start.52 = (bf16[256,2048]{1,0:T(8,128)(2,1)}, bf16[256,2048]{1,0:T(8,128)(2,1)S(1)}, u32[]{:S(2)}, u32[]{:S(2)}) collective-permute-start(bf16[256,2048]{1,0:T(8,128)(2,1)} %get-tuple-element.110.refs_1_.refs_0_), channel_id=1, source_target_pairs={{0,1},{1,0},{2,3},{3,2},{4,5},{5,4},{6,7},{7,6},{8,9},{9,8},{10,11... | collective-permute-start | bytes 3145736 | tf_op jit(solution)/shard_map/ppermute | solution.py:78
  354.7 38.8 %collective-permute-start.53 = (bf16[256,2048]{1,0:T(8,128)(2,1)}, bf16[256,2048]{1,0:T(8,128)(2,1)S(1)}, u32[]{:S(2)}, u32[]{:S(2)}) collective-permute-start(bf16[256,2048]{1,0:T(8,128)(2,1)} %get-tuple-element.117), channel_id=1, source_target_pairs={{0,1},{1,0},{2,3},{3,2},{4,5},{5,4},{6,7},{7,6},{8,9},{9,8},{10,11... | collective-permute-start | bytes 3145736 | tf_op jit(solution)/shard_map/ppermute | solution.py:78
  360.9 32.6 %collective-permute-start.55 = (bf16[256,2048]{1,0:T(8,128)(2,1)}, bf16[256,2048]{1,0:T(8,128)(2,1)S(1)}, u32[]{:S(2)}, u32[]{:S(2)}) collective-permute-start(bf16[256,2048]{1,0:T(8,128)(2,1)} %add_up.5.refs_13_), channel_id=1, source_target_pairs={{0,2},{1,3},{2,0},{3,1},{4,6},{5,7},{6,4},{7,5},{8,10},{9,11},{10,... | collective-permute-start | bytes 3145736 | tf_op jit(solution)/shard_map/ppermute | solution.py:78
  391.4 24.6 %collective-permute-start.58 = (bf16[256,2048]{1,0:T(8,128)(2,1)}, bf16[256,2048]{1,0:T(8,128)(2,1)S(1)}, u32[]{:S(2)}, u32[]{:S(2)}) collective-permute-start(bf16[256,2048]{1,0:T(8,128)(2,1)} %get-tuple-element.126.refs_6_), channel_id=1, source_target_pairs={{4,0},{12,4},{20,12},{28,20},{24,28},{16,24},{8,16},{0,8},{5,1},{1... | collective-permute-start | bytes 3145736 | tf_op jit(solution)/shard_map/ppermute | solution.py:702
  393.2 23.9 %collective-permute-start.59 = (bf16[256,2048]{1,0:T(8,128)(2,1)}, bf16[256,2048]{1,0:T(8,128)(2,1)S(1)}, u32[]{:S(2)}, u32[]{:S(2)}) collective-permute-start(bf16[256,2048]{1,0:T(8,128)(2,1)} %get-tuple-element.127.refs_7_), channel_id=1, source_target_pairs={{0,4},{4,12},{12,20},{20,28},{28,24},{24,16},{16,8},{8,0},{1,5},{5... | collective-permute-start | bytes 3145736 | tf_op jit(solution)/shard_map/ppermute | solution.py:702
  400.0 24.0 %collective-permute-start.60 = (bf16[256,2048]{1,0:T(8,128)(2,1)}, bf16[256,2048]{1,0:T(8,128)(2,1)S(1)}, u32[]{:S(2)}, u32[]{:S(2)}) collective-permute-start(bf16[256,2048]{1,0:T(8,128)(2,1)} %get-tuple-element.128.refs_13_.refs_0_.refs_6_), channel_id=1, source_target_pairs={{0,2},{1,3},{2,0},{3,1},{4,6},{5,7},{6,4},{7,5},{8,10},{9,11},{10,... | collective-permute-start | bytes 3145736 | tf_op jit(solution)/shard_map/ppermute | solution.py:78
  435.5 38.7 %collective-permute-start.61 = (bf16[256,2048]{1,0:T(8,128)(2,1)}, bf16[256,2048]{1,0:T(8,128)(2,1)}, u32[]{:S(2)}, u32[]{:S(2)}) collective-permute-start(bf16[256,2048]{1,0:T(8,128)(2,1)} %get-tuple-element.129.refs_1_.refs_13_.refs_11_), channel_id=1, source_target_pairs={{4,0},{12,4},{20,12},{28,20},{24,28},{16,24},{8,16},{0,8},{5,1},{1... | collective-permute-start | bytes 3145736 | tf_op jit(solution)/shard_map/ppermute | solution.py:702
  437.0 37.3 %collective-permute-start.62 = (bf16[256,2048]{1,0:T(8,128)(2,1)S(1)}, bf16[256,2048]{1,0:T(8,128)(2,1)}, u32[]{:S(2)}, u32[]{:S(2)}) collective-permute-start(bf16[256,2048]{1,0:T(8,128)(2,1)S(1)} %copy-done.20), channel_id=1, source_target_pairs={{0,4},{4,12},{12,20},{20,28},{28,24},{24,16},{16,8},{8,0},{1,5},{5... | collective-permute-start | bytes 3145736 | tf_op jit(solution)/shard_map/ppermute | solution.py:702
  472.2 32.6 %collective-permute-start.69 = (bf16[128,2048]{1,0:T(8,128)(2,1)}, bf16[128,2048]{1,0:T(8,128)(2,1)S(1)}, u32[]{:S(2)}, u32[]{:S(2)}) collective-permute-start(bf16[128,2048]{1,0:T(8,128)(2,1)} %get-tuple-element.136.refs_15_), channel_id=1, source_target_pairs={{4,0},{12,4},{20,12},{28,20},{24,28},{16,24},{8,16},{0,8},{5,1},{1... | collective-permute-start | bytes 1572872 | tf_op jit(solution)/shard_map/ppermute | solution.py:702
  473.6 32.7 %collective-permute-start.70 = (bf16[128,2048]{1,0:T(8,128)(2,1)}, bf16[128,2048]{1,0:T(8,128)(2,1)S(1)}, u32[]{:S(2)}, u32[]{:S(2)}) collective-permute-start(bf16[128,2048]{1,0:T(8,128)(2,1)} %get-tuple-element.137.refs_16_), channel_id=1, source_target_pairs={{0,4},{4,12},{12,20},{20,28},{28,24},{24,16},{16,8},{8,0},{1,5},{5... | collective-permute-start | bytes 1572872 | tf_op jit(solution)/shard_map/ppermute | solution.py:702
  488.1 27.4 %collective-permute-start.67 = (bf16[128,2048]{1,0:T(8,128)(2,1)}, bf16[128,2048]{1,0:T(8,128)(2,1)S(1)}, u32[]{:S(2)}, u32[]{:S(2)}) collective-permute-start(bf16[128,2048]{1,0:T(8,128)(2,1)} %get-tuple-element.142.refs_30_), channel_id=1, source_target_pairs={{4,0},{12,4},{20,12},{28,20},{24,28},{16,24},{8,16},{0,8},{5,1},{1... | collective-permute-start | bytes 1572872 | tf_op jit(solution)/shard_map/ppermute | solution.py:702
  489.5 27.6 %collective-permute-start.68 = (bf16[128,2048]{1,0:T(8,128)(2,1)}, bf16[128,2048]{1,0:T(8,128)(2,1)S(1)}, u32[]{:S(2)}, u32[]{:S(2)}) collective-permute-start(bf16[128,2048]{1,0:T(8,128)(2,1)} %get-tuple-element.143.refs_31_), channel_id=1, source_target_pairs={{0,4},{4,12},{12,20},{20,28},{28,24},{24,16},{16,8},{8,0},{1,5},{5... | collective-permute-start | bytes 1572872 | tf_op jit(solution)/shard_map/ppermute | solution.py:702
  504.7 28.8 %collective-permute-start.71 = (bf16[256,2048]{1,0:T(8,128)(2,1)}, bf16[256,2048]{1,0:T(8,128)(2,1)}, u32[]{:S(2)}, u32[]{:S(2)}) collective-permute-start(bf16[256,2048]{1,0:T(8,128)(2,1)} %get-tuple-element.148), channel_id=1, source_target_pairs={{0,1},{1,0},{2,3},{3,2},{4,5},{5,4},{6,7},{7,6},{8,9},{9,8},{10,11... | collective-permute-start | bytes 3145736 | tf_op jit(solution)/shard_map/ppermute | solution.py:78
  504.8 31.6 %collective-permute-start.65 = (bf16[256,2048]{1,0:T(8,128)(2,1)}, bf16[256,2048]{1,0:T(8,128)(2,1)S(1)}, u32[]{:S(2)}, u32[]{:S(2)}) collective-permute-start(bf16[256,2048]{1,0:T(8,128)(2,1)} %get-tuple-element.138.refs_10_), channel_id=1, source_target_pairs={{4,0},{12,4},{20,12},{28,20},{24,28},{16,24},{8,16},{0,8},{5,1},{1... | collective-permute-start | bytes 3145736 | tf_op jit(solution)/shard_map/ppermute | solution.py:702
  506.3 39.9 %collective-permute-start.66 = (bf16[256,2048]{1,0:T(8,128)(2,1)S(1)}, bf16[256,2048]{1,0:T(8,128)(2,1)S(1)}, u32[]{:S(2)}, u32[]{:S(2)}) collective-permute-start(bf16[256,2048]{1,0:T(8,128)(2,1)S(1)} %copy-done.37), channel_id=1, source_target_pairs={{0,4},{4,12},{12,20},{20,28},{28,24},{24,16},{16,8},{8,0},{1,5},{5... | collective-permute-start | bytes 3145736 | tf_op jit(solution)/shard_map/ppermute | solution.py:702
  515.5 38.1 %collective-permute-start.74 = (bf16[256,2048]{1,0:T(8,128)(2,1)}, bf16[256,2048]{1,0:T(8,128)(2,1)S(1)}, u32[]{:S(2)}, u32[]{:S(2)}) collective-permute-start(bf16[256,2048]{1,0:T(8,128)(2,1)} %get-tuple-element.145.refs_30_), channel_id=1, source_target_pairs={{4,0},{12,4},{20,12},{28,20},{24,28},{16,24},{8,16},{0,8},{5,1},{1... | collective-permute-start | bytes 3145736 | tf_op jit(solution)/shard_map/ppermute | solution.py:702
  518.0 50.2 %collective-permute-start.75 = (bf16[256,2048]{1,0:T(8,128)(2,1)}, bf16[256,2048]{1,0:T(8,128)(2,1)}, u32[]{:S(2)}, u32[]{:S(2)}) collective-permute-start(bf16[256,2048]{1,0:T(8,128)(2,1)} %get-tuple-element.146.refs_31_), channel_id=1, source_target_pairs={{0,4},{4,12},{12,20},{20,28},{28,24},{24,16},{16,8},{8,0},{1,5},{5... | collective-permute-start | bytes 3145736 | tf_op jit(solution)/shard_map/ppermute | solution.py:702
  533.6 44.0 %collective-permute-start.72 = (bf16[256,2048]{1,0:T(8,128)(2,1)S(1)}, bf16[256,2048]{1,0:T(8,128)(2,1)}, u32[]{:S(2)}, u32[]{:S(2)}) collective-permute-start(bf16[256,2048]{1,0:T(8,128)(2,1)S(1)} %copy-done.34), channel_id=1, source_target_pairs={{0,1},{1,0},{2,3},{3,2},{4,5},{5,4},{6,7},{7,6},{8,9},{9,8},{10,11... | collective-permute-start | bytes 3145736 | tf_op jit(solution)/shard_map/ppermute | solution.py:78
  536.4 42.8 %collective-permute-start.73 = (bf16[256,2048]{1,0:T(8,128)(2,1)}, bf16[256,2048]{1,0:T(8,128)(2,1)}, u32[]{:S(2)}, u32[]{:S(2)}) collective-permute-start(bf16[256,2048]{1,0:T(8,128)(2,1)} %add_up.6.refs_12_), channel_id=1, source_target_pairs={{0,2},{1,3},{2,0},{3,1},{4,6},{5,7},{6,4},{7,5},{8,10},{9,11},{10,... | collective-permute-start | bytes 3145736 | tf_op jit(solution)/shard_map/ppermute | solution.py:78
  546.2 39.3 %collective-permute-start.78 = (bf16[256,2048]{1,0:T(8,128)(2,1)}, bf16[256,2048]{1,0:T(8,128)(2,1)}, u32[]{:S(2)}, u32[]{:S(2)}) collective-permute-start(bf16[256,2048]{1,0:T(8,128)(2,1)} %get-tuple-element.149.refs_15_), channel_id=1, source_target_pairs={{4,0},{12,4},{20,12},{28,20},{24,28},{16,24},{8,16},{0,8},{5,1},{1... | collective-permute-start | bytes 3145736 | tf_op jit(solution)/shard_map/ppermute | solution.py:702
  553.5 32.0 %collective-permute-start.79 = (bf16[256,2048]{1,0:T(8,128)(2,1)}, bf16[256,2048]{1,0:T(8,128)(2,1)}, u32[]{:S(2)}, u32[]{:S(2)}) collective-permute-start(bf16[256,2048]{1,0:T(8,128)(2,1)} %get-tuple-element.150.refs_16_), channel_id=1, source_target_pairs={{0,4},{4,12},{12,20},{20,28},{28,24},{24,16},{16,8},{8,0},{1,5},{5... | collective-permute-start | bytes 3145736 | tf_op jit(solution)/shard_map/ppermute | solution.py:702
  576.9 26.4 %collective-permute-start.85 = (bf16[256,2048]{1,0:T(8,128)(2,1)}, bf16[256,2048]{1,0:T(8,128)(2,1)S(1)}, u32[]{:S(2)}, u32[]{:S(2)}) collective-permute-start(bf16[256,2048]{1,0:T(8,128)(2,1)} %get-tuple-element.155.refs_6_), channel_id=1, source_target_pairs={{4,0},{12,4},{20,12},{28,20},{24,28},{16,24},{8,16},{0,8},{5,1},{1... | collective-permute-start | bytes 3145736 | tf_op jit(solution)/shard_map/ppermute | solution.py:702
  577.6 27.1 %collective-permute-start.86 = (bf16[256,2048]{1,0:T(8,128)(2,1)}, bf16[256,2048]{1,0:T(8,128)(2,1)S(1)}, u32[]{:S(2)}, u32[]{:S(2)}) collective-permute-start(bf16[256,2048]{1,0:T(8,128)(2,1)} %get-tuple-element.156.refs_7_), channel_id=1, source_target_pairs={{0,4},{4,12},{12,20},{20,28},{28,24},{24,16},{16,8},{8,0},{1,5},{5... | collective-permute-start | bytes 3145736 | tf_op jit(solution)/shard_map/ppermute | solution.py:702
  593.9 31.8 %collective-permute-start.80 = (bf16[256,2048]{1,0:T(8,128)(2,1)}, bf16[256,2048]{1,0:T(8,128)(2,1)S(1)}, u32[]{:S(2)}, u32[]{:S(2)}) collective-permute-start(bf16[256,2048]{1,0:T(8,128)(2,1)} %get-tuple-element.160.refs_12_), channel_id=1, source_target_pairs={{4,0},{12,4},{20,12},{28,20},{24,28},{16,24},{8,16},{0,8},{5,1},{1... | collective-permute-start | bytes 3145736 | tf_op jit(solution)/shard_map/ppermute | solution.py:702
  594.6 32.1 %collective-permute-start.81 = (bf16[256,2048]{1,0:T(8,128)(2,1)}, bf16[256,2048]{1,0:T(8,128)(2,1)}, u32[]{:S(2)}, u32[]{:S(2)}) collective-permute-start(bf16[256,2048]{1,0:T(8,128)(2,1)} %get-tuple-element.161.refs_13_), channel_id=1, source_target_pairs={{0,4},{4,12},{12,20},{20,28},{28,24},{24,16},{16,8},{8,0},{1,5},{5... | collective-permute-start | bytes 3145736 | tf_op jit(solution)/shard_map/ppermute | solution.py:702
  614.9 33.3 %collective-permute-start.89 = (bf16[256,2048]{1,0:T(8,128)(2,1)}, bf16[256,2048]{1,0:T(8,128)(2,1)S(1)}, u32[]{:S(2)}, u32[]{:S(2)}) collective-permute-start(bf16[256,2048]{1,0:T(8,128)(2,1)} %get-tuple-element.165.refs_4_), channel_id=1, source_target_pairs={{4,0},{12,4},{20,12},{28,20},{24,28},{16,24},{8,16},{0,8},{5,1},{1... | collective-permute-start | bytes 3145736 | tf_op jit(solution)/shard_map/ppermute | solution.py:702
  616.4 32.7 %collective-permute-start.90 = (bf16[256,2048]{1,0:T(8,128)(2,1)}, bf16[256,2048]{1,0:T(8,128)(2,1)S(1)}, u32[]{:S(2)}, u32[]{:S(2)}) collective-permute-start(bf16[256,2048]{1,0:T(8,128)(2,1)} %get-tuple-element.166.refs_5_), channel_id=1, source_target_pairs={{0,4},{4,12},{12,20},{20,28},{28,24},{24,16},{16,8},{8,0},{1,5},{5... | collective-permute-start | bytes 3145736 | tf_op jit(solution)/shard_map/ppermute | solution.py:702
  634.9 34.0 %collective-permute-start.87 = (bf16[256,2048]{1,0:T(8,128)(2,1)}, bf16[256,2048]{1,0:T(8,128)(2,1)S(1)}, u32[]{:S(2)}, u32[]{:S(2)}) collective-permute-start(bf16[256,2048]{1,0:T(8,128)(2,1)} %get-tuple-element.167.refs_12_), channel_id=1, source_target_pairs={{4,0},{12,4},{20,12},{28,20},{24,28},{16,24},{8,16},{0,8},{5,1},{1... | collective-permute-start | bytes 3145736 | tf_op jit(solution)/shard_map/ppermute | solution.py:702
  636.4 32.9 %collective-permute-start.88 = (bf16[256,2048]{1,0:T(8,128)(2,1)}, bf16[256,2048]{1,0:T(8,128)(2,1)S(1)}, u32[]{:S(2)}, u32[]{:S(2)}) collective-permute-start(bf16[256,2048]{1,0:T(8,128)(2,1)} %get-tuple-element.168.refs_13_), channel_id=1, source_target_pairs={{0,4},{4,12},{12,20},{20,28},{28,24},{24,16},{16,8},{8,0},{1,5},{5... | collective-permute-start | bytes 3145736 | tf_op jit(solution)/shard_map/ppermute | solution.py:702
  657.1 39.6 %collective-permute-start.92 = (bf16[256,1024]{1,0:T(8,128)(2,1)}, bf16[256,1024]{1,0:T(8,128)(2,1)S(1)}, u32[]{:S(2)}, u32[]{:S(2)}) collective-permute-start(bf16[256,1024]{1,0:T(8,128)(2,1)} %get-tuple-element.172), channel_id=1, source_target_pairs={{0,0},{8,1},{16,2},{24,3},{4,4},{12,5},{20,6},{28,7},{1,8},{9,9},{... | collective-permute-start | bytes 1572872 | tf_op jit(solution)/shard_map/ppermute | solution.py:1193
  681.9 26.3 %collective-permute-start.96 = (bf16[64,2048]{1,0:T(8,128)(2,1)S(1)}, bf16[64,2048]{1,0:T(8,128)(2,1)S(1)}, u32[]{:S(2)}, u32[]{:S(2)}) collective-permute-start(bf16[64,2048]{1,0:T(8,128)(2,1)S(1)} %copy-done.86), channel_id=1, source_target_pairs={{0,1},{1,0},{2,3},{3,2},{4,5},{5,4},{6,7},{7,6},{8,9},{9,8},{10,11... | collective-permute-start | bytes 786440 | tf_op jit(solution)/shard_map/ppermute | solution.py:78
  682.0 26.2 %collective-permute-start.97 = (bf16[64,2048]{1,0:T(8,128)(2,1)S(1)}, bf16[64,2048]{1,0:T(8,128)(2,1)S(1)}, u32[]{:S(2)}, u32[]{:S(2)}) collective-permute-start(bf16[64,2048]{1,0:T(8,128)(2,1)S(1)} %copy-done.85), channel_id=1, source_target_pairs={{0,3},{1,2},{2,1},{3,0},{4,7},{5,6},{6,5},{7,4},{8,11},{9,10},{10,... | collective-permute-start | bytes 786440 | tf_op jit(solution)/shard_map/ppermute | solution.py:78
  (148 other events, 1279.6 us)
Sparse Core Ops, SparseCore 0:
  130.6 44.0 all-gather.1
  434.0 45.9 reduce-scatter.1

commit v5 on v4

--- a/solution.py
+++ b/solution.py
@@ -639,7 +639,6 @@
                     loads.add(i, source, target)
             for source, target in zip(recvs, held):
                 loads.add("got", source, target)
-            loads.wait("got")
             column = 0
             for i, term in enumerate(terms):
                 y_buf, x_buf = buffers[2 * i : 2 * i + 2]
@@ -650,6 +649,7 @@
                         values = x_buf[:, cols].astype(f32)
                     else:
                         values = dot(x_buf[...], y_buf[:, cols], ((0,), (0,)))
+                    loads.wait("got")
                     for n in range(n_w):
                         piece = values[n * term.columns : (n + 1) * term.columns]
                         write(n, c * term.columns, term.columns, column, piece, held, results)

time: 739 us -> 735 us (level)
  Pallas kernels: 309 us -> 299 us
    pallas_call x36, Pallas kernels: 281 us -> 271 us  [call(): pl.pallas_call(inner, out_shape=outs, grid_spec=spec, name=name, cost_est...]
  transfers between devices with their start and end apart: 103 -> 103, of which waited for: 42 -> 42; matrix products, arithmetic and copies ran while one was open for 4% -> 4% of each run, Pallas kernels for 39% -> 38%
where the time goes in v5:
time: 735 us; the launch traced here: 725 us
  Pallas kernels  299 us (41%)
  waiting for transfers between devices  212 us (29%)
  starting transfers between devices  135 us (18%)
  local copies, waits for them, and re-layouts  52 us (7%)
  between operations  15.6 us (2%)
  other arithmetic  10.5 us (1%)
    pallas_call x36, Pallas kernels, call(): pl.pallas_call(inner, out_shape=outs, grid_spec=spec, name=name, cost_est...  271 us
    ppermute x32, waiting for transfers between devices, step(): a, b = (lax.ppermute(a, 'dp', self.ahead), lax.ppermute(b, 'dp', self.back))  93.4 us
    ppermute x32, starting transfers between devices, step(): a, b = (lax.ppermute(a, 'dp', self.ahead), lax.ppermute(b, 'dp', self.back))  59.3 us
    ppermute x33, waiting for transfers between devices, swap_seq(): return lax.ppermute(x, 'seq', [(i, i ^ gap) for i in range(size)])  53.8 us
    ppermute x12, waiting for transfers between devices, step(): lax.ppermute(a, 'dp', self.back)  51.2 us
    unnamed x188, local copies, waits for them, and re-layouts  35.2 us
    pallas_call x8, Pallas kernels, plain(): pl.pallas_call(inner, out_shape=outs, grid=grid, in_specs=[*in_specs, *[A...  28.1 us
    ppermute x10, starting transfers between devices, swap_all(): return lax.ppermute(x, BOTH, [(i, i ^ gap) for i in range(size)])  25.6 us
  transfers between devices with their start and end apart: 103, of which 42 were waited for; matrix products, arithmetic and copies ran while one was open for 4% of the time, Pallas kernels for 38%

profile of v5, /device:TPU:0, one launch (start us, length us, event | category | flops | bytes accessed | tf_op | source)
XLA Modules:
  0.0 725.1 jit_solution(17015444126795642106)
XLA Ops:
  40.9 22.4 %collective-permute-done.11.refs_1_.refs_5_.refs_12_.refs_22_ = bf16[256,2048]{1,0:T(8,128)(2,1)S(1)} collective-permute-done((bf16[256,2048]{1,0:T(8,128)(2,1)}, bf16[256,2048]{1,0:T(8,128)(2,1)S(1)}, u32[]{:S(2)}, u32[]{:S(2)}) %collective-permute-start.11) | collective-permute-done | bytes 1048608 | tf_op jit(solution)/shard_map/ppermute | solution.py:341
  71.2 15.6 %collective-permute-done.13.refs_7_.refs_14_.refs_24_ = bf16[256,2048]{1,0:T(8,128)(2,1)} collective-permute-done((bf16[256,2048]{1,0:T(8,128)(2,1)S(1)}, bf16[256,2048]{1,0:T(8,128)(2,1)}, u32[]{:S(2)}, u32[]{:S(2)}) %collective-permute-start.13) | collective-permute-done | bytes 1048608 | tf_op jit(solution)/shard_map/ppermute | solution.py:341
  93.5 16.0 %collective-permute-done.15.refs_9_.refs_16_.refs_26_ = bf16[256,2048]{1,0:T(8,128)(2,1)} collective-permute-done((bf16[256,2048]{1,0:T(8,128)(2,1)}, bf16[256,2048]{1,0:T(8,128)(2,1)}, u32[]{:S(2)}, u32[]{:S(2)}) %collective-permute-start.15) | collective-permute-done | bytes 1048608 | tf_op jit(solution)/shard_map/ppermute | solution.py:341
  133.5 7.1 collective-permute-done.22.refs_0_
  146.4 10.6 %collective-permute-start.33 = (bf16[128,2048]{1,0:T(8,128)(2,1)}, bf16[128,2048]{1,0:T(8,128)(2,1)S(1)}, u32[]{:S(2)}, u32[]{:S(2)}) collective-permute-start(bf16[128,2048]{1,0:T(8,128)(2,1)} %tie.27.refs_15_.refs_16_.refs_1_.refs_4_), channel_id=1, source_target_pairs={{4,0},{12,4},{20,12},{28,20},{24,28},{16,24},{8,16},{0,8},{5,1},{1... | collective-permute-start | bytes 1572872 | tf_op jit(solution)/shard_map/ppermute | solution.py:341
  157.1 14.9 %project_qkv.1 = (f32[1024,1024]{1,0:T(8,128)}, bf16[1024,1024]{1,0:T(8,128)(2,1)}) custom-call(s32[17]{0:T(128)} %pad_add_fusion.at, bf16[256,2048]{1,0:T(8,128)(2,1)} %norm_forward.2.refs_0_.refs_5_, bf16[256,2048]{1,0:T(8,128)(2,1)} %copy-done, bf16[256,2048]{1,0:T(8,128)(2,1)} %copy-done.1, bf16[256,2048]{1,0:T(8,128)(2,1)} %copy-done.2, ...), custom_call_target="tpu_custom_call" | custom-call | flops 8589934592 | bytes 18874368 | tf_op jit(solution)/shard_map/project_qkv/pallas_call | solution.py:45
  176.2 5.6 collective-permute-start.28
  198.7 5.6 collective-permute-done.32.refs_13_.refs_4_.refs_7_
  215.3 9.6 %project_gate.1.refs_1_.refs_4_.refs_3_ = f32[1024,1024]{1,0:T(8,128)} custom-call(s32[17]{0:T(128)} %pad_add_fusion.at, bf16[256,2048]{1,0:T(8,128)(2,1)} %norm_forward.2.refs_0_.refs_5_, bf16[256,2048]{1,0:T(8,128)(2,1)} %copy-done, bf16[256,2048]{1,0:T(8,128)(2,1)} %copy-done.1, bf16[256,2048]{1,0:T(8,128)(2,1)} %copy-done.2, ...), custom_call_target="tpu_custom_call" | custom-call | flops 4294967296 | bytes 12582912 | tf_op jit(solution)/shard_map/project_gate/pallas_call | solution.py:45
  236.5 10.3 %retention_forward.1 = (bf16[1024,1024]{1,0:T(8,128)(2,1)}, bf16[1024,1024]{1,0:T(8,128)(2,1)}, f32[1024,1024]{1,0:T(8,128)}, bf16[2,4,256,512]{3,2,1,0:T(8,128)(2,1)}, bf16[2,4,256,256]{3,2,1,0:T(8,128)(2,1)}) custom-call(s32[17]{0:T(128)} %pad_add_fusion.at, f32[2]{0:T(128)} %dynamic_slice.8.refs_0_, f32[4]{0:T(128)} %subtract_bitcast_fusion.refs_1_, ...), custom_call_target="tpu_custom_call" | custom-call | flops 1879048192 | bytes 23068696 | tf_op jit(solution)/shard_map/retention_forward/pallas_call | solution.py:45
  247.6 6.8 attn_odd.1
  261.3 7.5 %attn_even.1 = (f32[256,2048]{1,0:T(8,128)}, f32[256,2048]{1,0:T(8,128)}) custom-call(s32[17]{0:T(128)} %pad_add_fusion.at, bf16[1024,1024]{1,0:T(8,128)(2,1)} %get-tuple-element.105.refs_0_.refs_5_, bf16[128,2048]{1,0:T(8,128)(2,1)} %tie.27.refs_15_.refs_16_.refs_1_.refs_4_, bf16[128,2048]{1,0:T(8,128)(2,1)} %tie.30.refs_2_.refs_5_, ...), custom_call_target="tpu_custom_call" | custom-call | flops 2147483648 | bytes 10485760 | tf_op jit(solution)/shard_map/attn_even/pallas_call | solution.py:45
  274.1 8.5 %collective-permute-done.43.refs_6_.refs_15_.refs_7_ = bf16[256,2048]{1,0:T(8,128)(2,1)S(1)} collective-permute-done((bf16[256,2048]{1,0:T(8,128)(2,1)S(1)}, bf16[256,2048]{1,0:T(8,128)(2,1)S(1)}, u32[]{:S(2)}, u32[]{:S(2)}) %collective-permute-start.43) | collective-permute-done | bytes 1048608 | tf_op jit(solution)/shard_map/ppermute | solution.py:341
  286.6 9.7 %collective-permute-done.41.refs_5_ = bf16[256,2048]{1,0:T(8,128)(2,1)S(1)} collective-permute-done((bf16[256,2048]{1,0:T(8,128)(2,1)}, bf16[256,2048]{1,0:T(8,128)(2,1)S(1)}, u32[]{:S(2)}, u32[]{:S(2)}) %collective-permute-start.41) | collective-permute-done | bytes 1048608 | tf_op jit(solution)/shard_map/ppermute | solution.py:78
  312.4 11.9 %collective-permute-done.46.refs_0_ = bf16[256,2048]{1,0:T(8,128)(2,1)S(1)} collective-permute-done((bf16[256,2048]{1,0:T(8,128)(2,1)}, bf16[256,2048]{1,0:T(8,128)(2,1)S(1)}, u32[]{:S(2)}, u32[]{:S(2)}) %collective-permute-start.46) | collective-permute-done | bytes 1048608 | tf_op jit(solution)/shard_map/ppermute | solution.py:78
  327.3 12.9 %feed_forward.2 = (bf16[256,1024]{1,0:T(8,128)(2,1)}, bf16[256,1024]{1,0:T(8,128)(2,1)}, bf16[256,1024]{1,0:T(8,128)(2,1)}, bf16[256,1024]{1,0:T(8,128)(2,1)}, b...) custom-call(s32[17]{0:T(128)} %pad_add_fusion.at, bf16[256,2048]{1,0:T(8,128)(2,1)} %copy-done.12, ...), custom_call_target="tpu_custom_call" | custom-call | flops 6442450944 | bytes 28311552 | tf_op jit(solution)/shard_map/feed_forward/pallas_call | solution.py:45
  341.1 12.9 %feed_forward.3 = (bf16[256,1024]{1,0:T(8,128)(2,1)}, bf16[256,1024]{1,0:T(8,128)(2,1)}, bf16[256,1024]{1,0:T(8,128)(2,1)}, bf16[256,1024]{1,0:T(8,128)(2,1)}, b...) custom-call(s32[17]{0:T(128)} %pad_add_fusion.at, bf16[256,2048]{1,0:T(8,128)(2,1)} %copy-done.8, ...), custom_call_target="tpu_custom_call" | custom-call | flops 6442450944 | bytes 28311552 | tf_op jit(solution)/shard_map/feed_forward/pallas_call | solution.py:45
  361.2 5.5 ffn_hop.5
  368.8 12.1 %collective-permute-done.56.refs_13_ = bf16[128,2048]{1,0:T(8,128)(2,1)S(1)} collective-permute-done((bf16[128,2048]{1,0:T(8,128)(2,1)}, bf16[128,2048]{1,0:T(8,128)(2,1)S(1)}, u32[]{:S(2)}, u32[]{:S(2)}) %collective-permute-start.56) | collective-permute-done | bytes 524320 | tf_op jit(solution)/shard_map/ppermute | solution.py:702
  383.0 7.2 ffn_hop.6
  393.6 5.2 norm_backward.2
  400.6 10.0 %down.1.refs_1_.refs_0_ = bf16[1024,2048]{1,0:T(8,128)(2,1)} custom-call(s32[17]{0:T(128)} %pad_add_fusion.at, bf16[256,1024]{1,0:T(8,128)(2,1)} %get-tuple-element.112.refs_11_.refs_0_, bf16[256,1024]{1,0:T(8,128)(2,1)} %get-tuple-element.113.refs_9_.refs_1_, bf16[256,1024]{1,0:T(8,128)(2,1)} %get-tuple-element.114.refs_10_.refs_2_, ...), custom_call_target="tpu_custom_call" | custom-call | flops 4294967296 | bytes 14680064 | tf_op jit(solution)/shard_map/down/pallas_call | solution.py:45
  410.6 4.1 collective-permute-done.58.refs_2_.refs_13_
  415.9 6.9 collective-permute-done.60.refs_0_
  423.8 7.7 %ffn_hop.7 = (bf16[256,2048]{1,0:T(8,128)(2,1)}, bf16[256,2048]{1,0:T(8,128)(2,1)}) custom-call(s32[17]{0:T(128)} %pad_add_fusion.at, bf16[256,2048]{1,0:T(8,128)(2,1)} %get-tuple-element.110.refs_1_.refs_0_, bf16[256,2048]{1,0:T(8,128)(2,1)} %copy-done.12, bf16[256,2048]{1,0:T(8,128)(2,1)} %tie.34.refs_1_.refs_2_, bf16[256,2048]{1,0:T(8,128)(2,1)} %copy-done.8, ...), custom_call_target="tpu_custom_call" | custom-call | flops 2147483648 | bytes 16777216 | tf_op jit(solution)/shard_map/ffn_hop/pallas_call | solution.py:45
  437.9 10.2 %grad_mixed.1.refs_2_ = f32[1024,1024]{1,0:T(8,128)} custom-call(s32[17]{0:T(128)} %pad_add_fusion.at, bf16[256,2048]{1,0:T(8,128)(2,1)} %get-tuple-element.128.refs_13_.refs_0_.refs_6_, bf16[256,2048]{1,0:T(8,128)(2,1)} %tie.36.refs_15_.refs_1_.refs_7_, bf16[256,2048]{1,0:T(8,128)(2,1)} %copy-done.10, bf16[256,2048]{1,0:T(8,128)(2,1)} %copy-done.11, ...), custom_call_target="tpu_custom_call" | custom-call | flops 4294967296 | bytes 12582912 | tf_op jit(solution)/shard_map/grad_mixed/pallas_call | solution.py:45
  448.1 16.2 %retention_backward.1 = (bf16[1024,1024]{1,0:T(8,128)(2,1)}, bf16[1024,1024]{1,0:T(8,128)(2,1)}, bf16[1024,1024]{1,0:T(8,128)(2,1)}) custom-call(s32[17]{0:T(128)} %pad_add_fusion.at, f32[2]{0:T(128)} %dynamic_slice.8.refs_0_, f32[4]{0:T(128)} %subtract_bitcast_fusion.refs_1_, f32[1024,1024]{1,0:T(8,128)} %grad_mixed.1.refs_2_, ...), custom_call_target="tpu_custom_call" | custom-call | flops 3758096384 | bytes 27263000 | tf_op jit(solution)/shard_map/retention_backward/pallas_call | solution.py:45
  464.4 5.5 gate_hop.5
  472.4 7.6 %ffn_hop.8 = (bf16[256,2048]{1,0:T(8,128)(2,1)}, bf16[256,2048]{1,0:T(8,128)(2,1)}) custom-call(s32[17]{0:T(128)} %pad_add_fusion.at, bf16[256,2048]{1,0:T(8,128)(2,1)} %get-tuple-element.110.refs_1_.refs_0_, bf16[256,2048]{1,0:T(8,128)(2,1)} %copy-done.12, bf16[256,2048]{1,0:T(8,128)(2,1)} %tie.34.refs_1_.refs_2_, bf16[256,2048]{1,0:T(8,128)(2,1)} %copy-done.8, ...), custom_call_target="tpu_custom_call" | custom-call | flops 2147483648 | bytes 16777216 | tf_op jit(solution)/shard_map/ffn_hop/pallas_call | solution.py:45
  480.0 5.1 qkv_hop.5
  487.2 14.4 %grad_one_odd.1 = (bf16[256,2048]{1,0:T(8,128)(2,1)}, bf16[256,2048]{1,0:T(8,128)(2,1)}) custom-call(s32[17]{0:T(128)} %pad_add_fusion.at, bf16[1024,1024]{1,0:T(8,128)(2,1)} %get-tuple-element.135.refs_4_.refs_10_.refs_0_, bf16[256,1024]{1,0:T(8,128)(2,1)} %join_pieces.4.refs_4_.refs_1_, bf16[256,1024]{1,0:T(8,128)(2,1)} %tie.24.refs_1_.refs_13_.refs_5_.refs_2_, ...), custom_call_target="tpu_custom_call" | custom-call | flops 6442450944 | bytes 29360128 | tf_op jit(solution)/shard_map/grad_one_odd/pallas_call | solution.py:45
  503.9 7.2 gate_hop.6
  514.1 15.0 %grad_one_even.1 = (f32[256,2048]{1,0:T(8,128)}, f32[256,2048]{1,0:T(8,128)}) custom-call(s32[17]{0:T(128)} %pad_add_fusion.at, bf16[1024,1024]{1,0:T(8,128)(2,1)} %get-tuple-element.135.refs_4_.refs_10_.refs_0_, bf16[256,1024]{1,0:T(8,128)(2,1)} %join_pieces.4.refs_4_.refs_1_, bf16[256,1024]{1,0:T(8,128)(2,1)} %tie.24.refs_1_.refs_13_.refs_5_.refs_2_, ...), custom_call_target="tpu_custom_call" | custom-call | flops 6442450944 | bytes 31457280 | tf_op jit(solution)/shard_map/grad_one_even/pallas_call | solution.py:45
  534.0 6.9 qkv_hop.6
  542.7 7.6 %collective-permute-done.74.refs_10_ = bf16[256,2048]{1,0:T(8,128)(2,1)S(1)} collective-permute-done((bf16[256,2048]{1,0:T(8,128)(2,1)}, bf16[256,2048]{1,0:T(8,128)(2,1)S(1)}, u32[]{:S(2)}, u32[]{:S(2)}) %collective-permute-start.74) | collective-permute-done | bytes 1048608 | tf_op jit(solution)/shard_map/ppermute | solution.py:702
  552.5 7.1 ffn_hop.9
  564.9 7.6 %gate_hop.7 = (bf16[256,2048]{1,0:T(8,128)(2,1)}, bf16[256,2048]{1,0:T(8,128)(2,1)}) custom-call(s32[17]{0:T(128)} %pad_add_fusion.at, bf16[256,2048]{1,0:T(8,128)(2,1)} %norm_forward.2.refs_0_.refs_5_, bf16[256,2048]{1,0:T(8,128)(2,1)} %copy-done.1, bf16[256,2048]{1,0:T(8,128)(2,1)} %copy-done, bf16[256,2048]{1,0:T(8,128)(2,1)} %copy-done.2, ...), custom_call_target="tpu_custom_call" | custom-call | flops 2147483648 | bytes 16777216 | tf_op jit(solution)/shard_map/gate_hop/pallas_call | solution.py:45
  574.8 5.2 norm_backward.3
  581.1 7.3 %qkv_hop.7 = (bf16[256,2048]{1,0:T(8,128)(2,1)}, bf16[256,2048]{1,0:T(8,128)(2,1)}) custom-call(s32[17]{0:T(128)} %pad_add_fusion.at, bf16[256,2048]{1,0:T(8,128)(2,1)} %norm_forward.2.refs_0_.refs_5_, bf16[256,2048]{1,0:T(8,128)(2,1)} %copy-done.1, bf16[256,2048]{1,0:T(8,128)(2,1)} %copy-done, bf16[256,2048]{1,0:T(8,128)(2,1)} %copy-done.2, ...), custom_call_target="tpu_custom_call" | custom-call | flops 2147483648 | bytes 16777216 | tf_op jit(solution)/shard_map/qkv_hop/pallas_call | solution.py:45
  594.5 4.4 collective-permute-done.85.refs_10_
  601.4 7.6 %gate_hop.8 = (bf16[256,2048]{1,0:T(8,128)(2,1)}, bf16[256,2048]{1,0:T(8,128)(2,1)}) custom-call(s32[17]{0:T(128)} %pad_add_fusion.at, bf16[256,2048]{1,0:T(8,128)(2,1)} %norm_forward.2.refs_0_.refs_5_, bf16[256,2048]{1,0:T(8,128)(2,1)} %copy-done.1, bf16[256,2048]{1,0:T(8,128)(2,1)} %copy-done, bf16[256,2048]{1,0:T(8,128)(2,1)} %copy-done.2, ...), custom_call_target="tpu_custom_call" | custom-call | flops 2147483648 | bytes 16777216 | tf_op jit(solution)/shard_map/gate_hop/pallas_call | solution.py:45
  622.4 7.1 qkv_hop.8
  631.5 12.3 %collective-permute-done.89.refs_10_ = bf16[256,2048]{1,0:T(8,128)(2,1)S(1)} collective-permute-done((bf16[256,2048]{1,0:T(8,128)(2,1)}, bf16[256,2048]{1,0:T(8,128)(2,1)S(1)}, u32[]{:S(2)}, u32[]{:S(2)}) %collective-permute-start.89) | collective-permute-done | bytes 1048608 | tf_op jit(solution)/shard_map/ppermute | solution.py:702
  645.8 6.8 gate_hop.9
  657.2 7.4 %collective-permute-done.87.refs_10_ = bf16[256,2048]{1,0:T(8,128)(2,1)S(1)} collective-permute-done((bf16[256,2048]{1,0:T(8,128)(2,1)}, bf16[256,2048]{1,0:T(8,128)(2,1)S(1)}, u32[]{:S(2)}, u32[]{:S(2)}) %collective-permute-start.87) | collective-permute-done | bytes 1048608 | tf_op jit(solution)/shard_map/ppermute | solution.py:702
  665.9 6.6 qkv_hop.9.refs_0_
  678.6 11.3 %collective-permute-done.91.refs_1_.refs_2_ = bf16[64,2048]{1,0:T(8,128)(2,1)S(1)} collective-permute-done((bf16[64,2048]{1,0:T(8,128)(2,1)}, bf16[64,2048]{1,0:T(8,128)(2,1)S(1)}, u32[]{:S(2)}, u32[]{:S(2)}) %collective-permute-start.91) | collective-permute-done | bytes 262176 | tf_op jit(solution)/shard_map/ppermute | solution.py:78
  693.8 9.0 %collective-permute-start.93 = (f32[4,1,4,64]{3,2,1,0:T(4,128)S(1)}, f32[4,1,4,64]{3,2,1,0:T(4,128)S(1)}, u32[]{:S(2)}, u32[]{:S(2)}) collective-permute-start(f32[4,1,4,64]{3,2,1,0:T(4,128)S(1)} %slice_select_fusion.2), channel_id=1, source_target_pairs={{0,16},{1,17},{2,18},{3,19},{4,20},{5,21},{6,22},{7,23},{8,24},{9,... | collective-permute-start | bytes 12296 | tf_op jit(solution)/shard_map/ppermute | solution.py:253
  (467 shorter events, 267.0 us)
Async XLA Ops:
  7.2 318.1 %all-gather.2.cloned.1.call-start = ((), (), s32[]{:S(2)}) async-start(), calls=%async_computation.1 | async-start | bytes 5242880 | tf_op jit(solution)/shard_map/all_gather | solution.py:1073
  38.9 24.5 %collective-permute-start.11 = (bf16[256,2048]{1,0:T(8,128)(2,1)}, bf16[256,2048]{1,0:T(8,128)(2,1)S(1)}, u32[]{:S(2)}, u32[]{:S(2)}) collective-permute-start(bf16[256,2048]{1,0:T(8,128)(2,1)} %join_pieces.3.refs_3_.refs_4_.refs_11_.refs_21_), channel_id=1, source_target_pairs={{0,4},{4,12},{12,20},{20,28},{28,24},{24,16},{16,8},{8,0},{1,5},{5... | collective-permute-start | bytes 3145736 | tf_op jit(solution)/shard_map/ppermute | solution.py:341
  40.7 24.3 %collective-permute-start.12 = (bf16[256,2048]{1,0:T(8,128)(2,1)}, bf16[256,2048]{1,0:T(8,128)(2,1)S(1)}, u32[]{:S(2)}, u32[]{:S(2)}) collective-permute-start(bf16[256,2048]{1,0:T(8,128)(2,1)} %join_pieces.3.refs_3_.refs_4_.refs_11_.refs_21_), channel_id=1, source_target_pairs={{4,0},{12,4},{20,12},{28,20},{24,28},{16,24},{8,16},{0,8},{5,1},{1... | collective-permute-start | bytes 3145736 | tf_op jit(solution)/shard_map/ppermute | solution.py:341
  88.8 25.8 %collective-permute-start.9 = (bf16[256,2048]{1,0:T(8,128)(2,1)}, bf16[256,2048]{1,0:T(8,128)(2,1)S(1)}, u32[]{:S(2)}, u32[]{:S(2)}) collective-permute-start(bf16[256,2048]{1,0:T(8,128)(2,1)} %norm_forward.2.refs_0_.refs_5_), channel_id=1, source_target_pairs={{0,1},{1,0},{2,3},{3,2},{4,5},{5,4},{6,7},{7,6},{8,9},{9,8},{10,11... | collective-permute-start | bytes 3145736 | tf_op jit(solution)/shard_map/ppermute | solution.py:78
  92.5 28.2 %collective-permute-start.10 = (bf16[256,2048]{1,0:T(8,128)(2,1)S(1)}, bf16[256,2048]{1,0:T(8,128)(2,1)S(1)}, u32[]{:S(2)}, u32[]{:S(2)}) collective-permute-start(bf16[256,2048]{1,0:T(8,128)(2,1)S(1)} %collective-permute-done.8.refs_3_.refs_1_.refs_2_.refs_7_), channel_id=1, source_target_pairs={{0,1},{1,0},{2,3},{3,2},{4,5},{5,4},{6,7},{7,6},{8,9},{9,8},{10,11... | collective-permute-start | bytes 3145736 | tf_op jit(solution)/shard_map/ppermute | solution.py:78
  130.5 431.7 %reduce-scatter.2.cloned.1.call-start = ((), (), s32[]{:S(2)}) async-start(), calls=%async_computation.2 | async-start | bytes 5242880 | tf_op jit(solution)/shard_map/reduce_scatter | solution.py:1157
  141.4 30.6 %collective-permute-start.25 = (bf16[256,1024]{1,0:T(8,128)(2,1)}, bf16[256,1024]{1,0:T(8,128)(2,1)S(1)}, u32[]{:S(2)}, u32[]{:S(2)}) collective-permute-start(bf16[256,1024]{1,0:T(8,128)(2,1)} %tie.24.refs_1_.refs_13_.refs_5_.refs_2_), channel_id=1, source_target_pairs={{0,4},{4,12},{12,20},{20,28},{28,24},{24,16},{16,8},{8,0},{1,5},{5... | collective-permute-start | bytes 1572872 | tf_op jit(solution)/shard_map/ppermute | solution.py:341
  143.6 31.8 %collective-permute-start.26 = (bf16[256,1024]{1,0:T(8,128)(2,1)}, bf16[256,1024]{1,0:T(8,128)(2,1)S(1)}, u32[]{:S(2)}, u32[]{:S(2)}) collective-permute-start(bf16[256,1024]{1,0:T(8,128)(2,1)} %tie.25.refs_2_.refs_14_.refs_6_.refs_3_), channel_id=1, source_target_pairs={{4,0},{12,4},{20,12},{28,20},{24,28},{16,24},{8,16},{0,8},{5,1},{1... | collective-permute-start | bytes 1572872 | tf_op jit(solution)/shard_map/ppermute | solution.py:341
  145.0 36.7 %collective-permute-start.31 = (bf16[128,2048]{1,0:T(8,128)(2,1)}, bf16[128,2048]{1,0:T(8,128)(2,1)S(1)}, u32[]{:S(2)}, u32[]{:S(2)}) collective-permute-start(bf16[128,2048]{1,0:T(8,128)(2,1)} %tie.27.refs_15_.refs_16_.refs_1_.refs_4_), channel_id=1, source_target_pairs={{0,4},{4,12},{12,20},{20,28},{28,24},{24,16},{16,8},{8,0},{1,5},{5... | collective-permute-start | bytes 1572872 | tf_op jit(solution)/shard_map/ppermute | solution.py:341
  146.4 39.1 %collective-permute-start.33 = (bf16[128,2048]{1,0:T(8,128)(2,1)}, bf16[128,2048]{1,0:T(8,128)(2,1)S(1)}, u32[]{:S(2)}, u32[]{:S(2)}) collective-permute-start(bf16[128,2048]{1,0:T(8,128)(2,1)} %tie.27.refs_15_.refs_16_.refs_1_.refs_4_), channel_id=1, source_target_pairs={{4,0},{12,4},{20,12},{28,20},{24,28},{16,24},{8,16},{0,8},{5,1},{1... | collective-permute-start | bytes 1572872 | tf_op jit(solution)/shard_map/ppermute | solution.py:341
  234.3 24.7 %collective-permute-start.42 = (bf16[256,2048]{1,0:T(8,128)(2,1)}, bf16[256,2048]{1,0:T(8,128)(2,1)S(1)}, u32[]{:S(2)}, u32[]{:S(2)}) collective-permute-start(bf16[256,2048]{1,0:T(8,128)(2,1)} %join_pieces.5.refs_9_.refs_10_.refs_3_.refs_12_.refs_4_), channel_id=1, source_target_pairs={{0,4},{4,12},{12,20},{20,28},{28,24},{24,16},{16,8},{8,0},{1,5},{5... | collective-permute-start | bytes 3145736 | tf_op jit(solution)/shard_map/ppermute | solution.py:341
  236.4 24.8 %collective-permute-start.44 = (bf16[256,2048]{1,0:T(8,128)(2,1)}, bf16[256,2048]{1,0:T(8,128)(2,1)S(1)}, u32[]{:S(2)}, u32[]{:S(2)}) collective-permute-start(bf16[256,2048]{1,0:T(8,128)(2,1)} %join_pieces.5.refs_9_.refs_10_.refs_3_.refs_12_.refs_4_), channel_id=1, source_target_pairs={{4,0},{12,4},{20,12},{28,20},{24,28},{16,24},{8,16},{0,8},{5,1},{1... | collective-permute-start | bytes 3145736 | tf_op jit(solution)/shard_map/ppermute | solution.py:341
  254.5 32.1 %collective-permute-start.39 = (bf16[256,2048]{1,0:T(8,128)(2,1)}, bf16[256,2048]{1,0:T(8,128)(2,1)S(1)}, u32[]{:S(2)}, u32[]{:S(2)}) collective-permute-start(bf16[256,2048]{1,0:T(8,128)(2,1)} %get-tuple-element.106.refs_10_), channel_id=1, source_target_pairs={{0,1},{1,0},{2,3},{3,2},{4,5},{5,4},{6,7},{7,6},{8,9},{9,8},{10,11... | collective-permute-start | bytes 3145736 | tf_op jit(solution)/shard_map/ppermute | solution.py:78
  261.3 23.7 %collective-permute-start.45 = (bf16[256,2048]{1,0:T(8,128)(2,1)S(1)}, bf16[256,2048]{1,0:T(8,128)(2,1)}, u32[]{:S(2)}, u32[]{:S(2)}) collective-permute-start(bf16[256,2048]{1,0:T(8,128)(2,1)S(1)} %collective-permute-done.44.refs_5_.refs_14_.refs_6_), channel_id=1, source_target_pairs={{4,0},{12,4},{20,12},{28,20},{24,28},{16,24},{8,16},{0,8},{5,1},{1... | collective-permute-start | bytes 3145736 | tf_op jit(solution)/shard_map/ppermute | solution.py:341
  272.5 23.8 %collective-permute-start.41 = (bf16[256,2048]{1,0:T(8,128)(2,1)}, bf16[256,2048]{1,0:T(8,128)(2,1)S(1)}, u32[]{:S(2)}, u32[]{:S(2)}) collective-permute-start(bf16[256,2048]{1,0:T(8,128)(2,1)} %add_up.4), channel_id=1, source_target_pairs={{0,2},{1,3},{2,0},{3,1},{4,6},{5,7},{6,4},{7,5},{8,10},{9,11},{10,... | collective-permute-start | bytes 3145736 | tf_op jit(solution)/shard_map/ppermute | solution.py:78
  285.0 24.8 %collective-permute-start.49 = (bf16[256,2048]{1,0:T(8,128)(2,1)}, bf16[256,2048]{1,0:T(8,128)(2,1)}, u32[]{:S(2)}, u32[]{:S(2)}) collective-permute-start(bf16[256,2048]{1,0:T(8,128)(2,1)} %collective-permute-done.45.refs_7_.refs_16_.refs_8_), channel_id=1, source_target_pairs={{4,0},{12,4},{20,12},{28,20},{24,28},{16,24},{8,16},{0,8},{5,1},{1... | collective-permute-start | bytes 3145736 | tf_op jit(solution)/shard_map/ppermute | solution.py:341
  301.7 23.6 %collective-permute-start.52 = (bf16[256,2048]{1,0:T(8,128)(2,1)}, bf16[256,2048]{1,0:T(8,128)(2,1)S(1)}, u32[]{:S(2)}, u32[]{:S(2)}) collective-permute-start(bf16[256,2048]{1,0:T(8,128)(2,1)} %get-tuple-element.110.refs_1_.refs_0_), channel_id=1, source_target_pairs={{0,1},{1,0},{2,3},{3,2},{4,5},{5,4},{6,7},{7,6},{8,9},{9,8},{10,11... | collective-permute-start | bytes 3145736 | tf_op jit(solution)/shard_map/ppermute | solution.py:78
  354.6 37.6 %collective-permute-start.53 = (bf16[256,2048]{1,0:T(8,128)(2,1)}, bf16[256,2048]{1,0:T(8,128)(2,1)S(1)}, u32[]{:S(2)}, u32[]{:S(2)}) collective-permute-start(bf16[256,2048]{1,0:T(8,128)(2,1)} %get-tuple-element.117), channel_id=1, source_target_pairs={{0,1},{1,0},{2,3},{3,2},{4,5},{5,4},{6,7},{7,6},{8,9},{9,8},{10,11... | collective-permute-start | bytes 3145736 | tf_op jit(solution)/shard_map/ppermute | solution.py:78
  360.9 31.4 %collective-permute-start.55 = (bf16[256,2048]{1,0:T(8,128)(2,1)}, bf16[256,2048]{1,0:T(8,128)(2,1)S(1)}, u32[]{:S(2)}, u32[]{:S(2)}) collective-permute-start(bf16[256,2048]{1,0:T(8,128)(2,1)} %add_up.5.refs_13_), channel_id=1, source_target_pairs={{0,2},{1,3},{2,0},{3,1},{4,6},{5,7},{6,4},{7,5},{8,10},{9,11},{10,... | collective-permute-start | bytes 3145736 | tf_op jit(solution)/shard_map/ppermute | solution.py:78
  390.2 24.6 %collective-permute-start.58 = (bf16[256,2048]{1,0:T(8,128)(2,1)}, bf16[256,2048]{1,0:T(8,128)(2,1)S(1)}, u32[]{:S(2)}, u32[]{:S(2)}) collective-permute-start(bf16[256,2048]{1,0:T(8,128)(2,1)} %get-tuple-element.126.refs_6_), channel_id=1, source_target_pairs={{4,0},{12,4},{20,12},{28,20},{24,28},{16,24},{8,16},{0,8},{5,1},{1... | collective-permute-start | bytes 3145736 | tf_op jit(solution)/shard_map/ppermute | solution.py:702
  392.0 23.9 %collective-permute-start.59 = (bf16[256,2048]{1,0:T(8,128)(2,1)}, bf16[256,2048]{1,0:T(8,128)(2,1)S(1)}, u32[]{:S(2)}, u32[]{:S(2)}) collective-permute-start(bf16[256,2048]{1,0:T(8,128)(2,1)} %get-tuple-element.127.refs_7_), channel_id=1, source_target_pairs={{0,4},{4,12},{12,20},{20,28},{28,24},{24,16},{16,8},{8,0},{1,5},{5... | collective-permute-start | bytes 3145736 | tf_op jit(solution)/shard_map/ppermute | solution.py:702
  398.8 24.0 %collective-permute-start.60 = (bf16[256,2048]{1,0:T(8,128)(2,1)}, bf16[256,2048]{1,0:T(8,128)(2,1)S(1)}, u32[]{:S(2)}, u32[]{:S(2)}) collective-permute-start(bf16[256,2048]{1,0:T(8,128)(2,1)} %get-tuple-element.128.refs_13_.refs_0_.refs_6_), channel_id=1, source_target_pairs={{0,2},{1,3},{2,0},{3,1},{4,6},{5,7},{6,4},{7,5},{8,10},{9,11},{10,... | collective-permute-start | bytes 3145736 | tf_op jit(solution)/shard_map/ppermute | solution.py:78
  433.2 39.1 %collective-permute-start.61 = (bf16[256,2048]{1,0:T(8,128)(2,1)}, bf16[256,2048]{1,0:T(8,128)(2,1)}, u32[]{:S(2)}, u32[]{:S(2)}) collective-permute-start(bf16[256,2048]{1,0:T(8,128)(2,1)} %get-tuple-element.129.refs_1_.refs_13_.refs_11_), channel_id=1, source_target_pairs={{4,0},{12,4},{20,12},{28,20},{24,28},{16,24},{8,16},{0,8},{5,1},{1... | collective-permute-start | bytes 3145736 | tf_op jit(solution)/shard_map/ppermute | solution.py:702
  434.7 37.7 %collective-permute-start.62 = (bf16[256,2048]{1,0:T(8,128)(2,1)S(1)}, bf16[256,2048]{1,0:T(8,128)(2,1)}, u32[]{:S(2)}, u32[]{:S(2)}) collective-permute-start(bf16[256,2048]{1,0:T(8,128)(2,1)S(1)} %copy-done.20), channel_id=1, source_target_pairs={{0,4},{4,12},{12,20},{20,28},{28,24},{24,16},{16,8},{8,0},{1,5},{5... | collective-permute-start | bytes 3145736 | tf_op jit(solution)/shard_map/ppermute | solution.py:702
  469.9 31.7 %collective-permute-start.69 = (bf16[128,2048]{1,0:T(8,128)(2,1)}, bf16[128,2048]{1,0:T(8,128)(2,1)S(1)}, u32[]{:S(2)}, u32[]{:S(2)}) collective-permute-start(bf16[128,2048]{1,0:T(8,128)(2,1)} %get-tuple-element.136.refs_15_), channel_id=1, source_target_pairs={{4,0},{12,4},{20,12},{28,20},{24,28},{16,24},{8,16},{0,8},{5,1},{1... | collective-permute-start | bytes 1572872 | tf_op jit(solution)/shard_map/ppermute | solution.py:702
  471.3 31.7 %collective-permute-start.70 = (bf16[128,2048]{1,0:T(8,128)(2,1)}, bf16[128,2048]{1,0:T(8,128)(2,1)S(1)}, u32[]{:S(2)}, u32[]{:S(2)}) collective-permute-start(bf16[128,2048]{1,0:T(8,128)(2,1)} %get-tuple-element.137.refs_16_), channel_id=1, source_target_pairs={{0,4},{4,12},{12,20},{20,28},{28,24},{24,16},{16,8},{8,0},{1,5},{5... | collective-permute-start | bytes 1572872 | tf_op jit(solution)/shard_map/ppermute | solution.py:702
  485.1 26.0 %collective-permute-start.67 = (bf16[128,2048]{1,0:T(8,128)(2,1)}, bf16[128,2048]{1,0:T(8,128)(2,1)S(1)}, u32[]{:S(2)}, u32[]{:S(2)}) collective-permute-start(bf16[128,2048]{1,0:T(8,128)(2,1)} %get-tuple-element.142.refs_30_), channel_id=1, source_target_pairs={{4,0},{12,4},{20,12},{28,20},{24,28},{16,24},{8,16},{0,8},{5,1},{1... | collective-permute-start | bytes 1572872 | tf_op jit(solution)/shard_map/ppermute | solution.py:702
  486.5 26.4 %collective-permute-start.68 = (bf16[128,2048]{1,0:T(8,128)(2,1)}, bf16[128,2048]{1,0:T(8,128)(2,1)S(1)}, u32[]{:S(2)}, u32[]{:S(2)}) collective-permute-start(bf16[128,2048]{1,0:T(8,128)(2,1)} %get-tuple-element.143.refs_31_), channel_id=1, source_target_pairs={{0,4},{4,12},{12,20},{20,28},{28,24},{24,16},{16,8},{8,0},{1,5},{5... | collective-permute-start | bytes 1572872 | tf_op jit(solution)/shard_map/ppermute | solution.py:702
  501.5 27.6 %collective-permute-start.71 = (bf16[256,2048]{1,0:T(8,128)(2,1)}, bf16[256,2048]{1,0:T(8,128)(2,1)}, u32[]{:S(2)}, u32[]{:S(2)}) collective-permute-start(bf16[256,2048]{1,0:T(8,128)(2,1)} %get-tuple-element.148), channel_id=1, source_target_pairs={{0,1},{1,0},{2,3},{3,2},{4,5},{5,4},{6,7},{7,6},{8,9},{9,8},{10,11... | collective-permute-start | bytes 3145736 | tf_op jit(solution)/shard_map/ppermute | solution.py:78
  501.6 30.3 %collective-permute-start.65 = (bf16[256,2048]{1,0:T(8,128)(2,1)}, bf16[256,2048]{1,0:T(8,128)(2,1)S(1)}, u32[]{:S(2)}, u32[]{:S(2)}) collective-permute-start(bf16[256,2048]{1,0:T(8,128)(2,1)} %get-tuple-element.138.refs_10_), channel_id=1, source_target_pairs={{4,0},{12,4},{20,12},{28,20},{24,28},{16,24},{8,16},{0,8},{5,1},{1... | collective-permute-start | bytes 3145736 | tf_op jit(solution)/shard_map/ppermute | solution.py:702
  503.1 37.8 %collective-permute-start.66 = (bf16[256,2048]{1,0:T(8,128)(2,1)S(1)}, bf16[256,2048]{1,0:T(8,128)(2,1)S(1)}, u32[]{:S(2)}, u32[]{:S(2)}) collective-permute-start(bf16[256,2048]{1,0:T(8,128)(2,1)S(1)} %copy-done.37), channel_id=1, source_target_pairs={{0,4},{4,12},{12,20},{20,28},{28,24},{24,16},{16,8},{8,0},{1,5},{5... | collective-permute-start | bytes 3145736 | tf_op jit(solution)/shard_map/ppermute | solution.py:702
  511.1 39.3 %collective-permute-start.74 = (bf16[256,2048]{1,0:T(8,128)(2,1)}, bf16[256,2048]{1,0:T(8,128)(2,1)S(1)}, u32[]{:S(2)}, u32[]{:S(2)}) collective-permute-start(bf16[256,2048]{1,0:T(8,128)(2,1)} %get-tuple-element.145.refs_30_), channel_id=1, source_target_pairs={{4,0},{12,4},{20,12},{28,20},{24,28},{16,24},{8,16},{0,8},{5,1},{1... | collective-permute-start | bytes 3145736 | tf_op jit(solution)/shard_map/ppermute | solution.py:702
  513.7 51.3 %collective-permute-start.75 = (bf16[256,2048]{1,0:T(8,128)(2,1)}, bf16[256,2048]{1,0:T(8,128)(2,1)}, u32[]{:S(2)}, u32[]{:S(2)}) collective-permute-start(bf16[256,2048]{1,0:T(8,128)(2,1)} %get-tuple-element.146.refs_31_), channel_id=1, source_target_pairs={{0,4},{4,12},{12,20},{20,28},{28,24},{24,16},{16,8},{8,0},{1,5},{5... | collective-permute-start | bytes 3145736 | tf_op jit(solution)/shard_map/ppermute | solution.py:702
  529.2 44.1 %collective-permute-start.72 = (bf16[256,2048]{1,0:T(8,128)(2,1)S(1)}, bf16[256,2048]{1,0:T(8,128)(2,1)}, u32[]{:S(2)}, u32[]{:S(2)}) collective-permute-start(bf16[256,2048]{1,0:T(8,128)(2,1)S(1)} %copy-done.34), channel_id=1, source_target_pairs={{0,1},{1,0},{2,3},{3,2},{4,5},{5,4},{6,7},{7,6},{8,9},{9,8},{10,11... | collective-permute-start | bytes 3145736 | tf_op jit(solution)/shard_map/ppermute | solution.py:78
  532.0 42.8 %collective-permute-start.73 = (bf16[256,2048]{1,0:T(8,128)(2,1)}, bf16[256,2048]{1,0:T(8,128)(2,1)}, u32[]{:S(2)}, u32[]{:S(2)}) collective-permute-start(bf16[256,2048]{1,0:T(8,128)(2,1)} %add_up.6.refs_12_), channel_id=1, source_target_pairs={{0,2},{1,3},{2,0},{3,1},{4,6},{5,7},{6,4},{7,5},{8,10},{9,11},{10,... | collective-permute-start | bytes 3145736 | tf_op jit(solution)/shard_map/ppermute | solution.py:78
  540.9 40.2 %collective-permute-start.78 = (bf16[256,2048]{1,0:T(8,128)(2,1)}, bf16[256,2048]{1,0:T(8,128)(2,1)}, u32[]{:S(2)}, u32[]{:S(2)}) collective-permute-start(bf16[256,2048]{1,0:T(8,128)(2,1)} %get-tuple-element.149.refs_15_), channel_id=1, source_target_pairs={{4,0},{12,4},{20,12},{28,20},{24,28},{16,24},{8,16},{0,8},{5,1},{1... | collective-permute-start | bytes 3145736 | tf_op jit(solution)/shard_map/ppermute | solution.py:702
  550.3 30.7 %collective-permute-start.79 = (bf16[256,2048]{1,0:T(8,128)(2,1)}, bf16[256,2048]{1,0:T(8,128)(2,1)}, u32[]{:S(2)}, u32[]{:S(2)}) collective-permute-start(bf16[256,2048]{1,0:T(8,128)(2,1)} %get-tuple-element.150.refs_16_), channel_id=1, source_target_pairs={{0,4},{4,12},{12,20},{20,28},{28,24},{24,16},{16,8},{8,0},{1,5},{5... | collective-permute-start | bytes 3145736 | tf_op jit(solution)/shard_map/ppermute | solution.py:702
  572.5 26.4 %collective-permute-start.85 = (bf16[256,2048]{1,0:T(8,128)(2,1)}, bf16[256,2048]{1,0:T(8,128)(2,1)S(1)}, u32[]{:S(2)}, u32[]{:S(2)}) collective-permute-start(bf16[256,2048]{1,0:T(8,128)(2,1)} %get-tuple-element.155.refs_6_), channel_id=1, source_target_pairs={{4,0},{12,4},{20,12},{28,20},{24,28},{16,24},{8,16},{0,8},{5,1},{1... | collective-permute-start | bytes 3145736 | tf_op jit(solution)/shard_map/ppermute | solution.py:702
  573.3 27.1 %collective-permute-start.86 = (bf16[256,2048]{1,0:T(8,128)(2,1)}, bf16[256,2048]{1,0:T(8,128)(2,1)S(1)}, u32[]{:S(2)}, u32[]{:S(2)}) collective-permute-start(bf16[256,2048]{1,0:T(8,128)(2,1)} %get-tuple-element.156.refs_7_), channel_id=1, source_target_pairs={{0,4},{4,12},{12,20},{20,28},{28,24},{24,16},{16,8},{8,0},{1,5},{5... | collective-permute-start | bytes 3145736 | tf_op jit(solution)/shard_map/ppermute | solution.py:702
  588.4 33.0 %collective-permute-start.80 = (bf16[256,2048]{1,0:T(8,128)(2,1)}, bf16[256,2048]{1,0:T(8,128)(2,1)S(1)}, u32[]{:S(2)}, u32[]{:S(2)}) collective-permute-start(bf16[256,2048]{1,0:T(8,128)(2,1)} %get-tuple-element.160.refs_12_), channel_id=1, source_target_pairs={{4,0},{12,4},{20,12},{28,20},{24,28},{16,24},{8,16},{0,8},{5,1},{1... | collective-permute-start | bytes 3145736 | tf_op jit(solution)/shard_map/ppermute | solution.py:702
  589.1 33.2 %collective-permute-start.81 = (bf16[256,2048]{1,0:T(8,128)(2,1)}, bf16[256,2048]{1,0:T(8,128)(2,1)}, u32[]{:S(2)}, u32[]{:S(2)}) collective-permute-start(bf16[256,2048]{1,0:T(8,128)(2,1)} %get-tuple-element.161.refs_13_), channel_id=1, source_target_pairs={{0,4},{4,12},{12,20},{20,28},{28,24},{24,16},{16,8},{8,0},{1,5},{5... | collective-permute-start | bytes 3145736 | tf_op jit(solution)/shard_map/ppermute | solution.py:702
  609.4 34.4 %collective-permute-start.89 = (bf16[256,2048]{1,0:T(8,128)(2,1)}, bf16[256,2048]{1,0:T(8,128)(2,1)S(1)}, u32[]{:S(2)}, u32[]{:S(2)}) collective-permute-start(bf16[256,2048]{1,0:T(8,128)(2,1)} %get-tuple-element.165.refs_4_), channel_id=1, source_target_pairs={{4,0},{12,4},{20,12},{28,20},{24,28},{16,24},{8,16},{0,8},{5,1},{1... | collective-permute-start | bytes 3145736 | tf_op jit(solution)/shard_map/ppermute | solution.py:702
  611.0 33.8 %collective-permute-start.90 = (bf16[256,2048]{1,0:T(8,128)(2,1)}, bf16[256,2048]{1,0:T(8,128)(2,1)S(1)}, u32[]{:S(2)}, u32[]{:S(2)}) collective-permute-start(bf16[256,2048]{1,0:T(8,128)(2,1)} %get-tuple-element.166.refs_5_), channel_id=1, source_target_pairs={{0,4},{4,12},{12,20},{20,28},{28,24},{24,16},{16,8},{8,0},{1,5},{5... | collective-permute-start | bytes 3145736 | tf_op jit(solution)/shard_map/ppermute | solution.py:702
  629.5 35.2 %collective-permute-start.87 = (bf16[256,2048]{1,0:T(8,128)(2,1)}, bf16[256,2048]{1,0:T(8,128)(2,1)S(1)}, u32[]{:S(2)}, u32[]{:S(2)}) collective-permute-start(bf16[256,2048]{1,0:T(8,128)(2,1)} %get-tuple-element.167.refs_12_), channel_id=1, source_target_pairs={{4,0},{12,4},{20,12},{28,20},{24,28},{16,24},{8,16},{0,8},{5,1},{1... | collective-permute-start | bytes 3145736 | tf_op jit(solution)/shard_map/ppermute | solution.py:702
  631.0 33.9 %collective-permute-start.88 = (bf16[256,2048]{1,0:T(8,128)(2,1)}, bf16[256,2048]{1,0:T(8,128)(2,1)S(1)}, u32[]{:S(2)}, u32[]{:S(2)}) collective-permute-start(bf16[256,2048]{1,0:T(8,128)(2,1)} %get-tuple-element.168.refs_13_), channel_id=1, source_target_pairs={{0,4},{4,12},{12,20},{20,28},{28,24},{24,16},{16,8},{8,0},{1,5},{5... | collective-permute-start | bytes 3145736 | tf_op jit(solution)/shard_map/ppermute | solution.py:702
  652.7 39.7 %collective-permute-start.92 = (bf16[256,1024]{1,0:T(8,128)(2,1)}, bf16[256,1024]{1,0:T(8,128)(2,1)S(1)}, u32[]{:S(2)}, u32[]{:S(2)}) collective-permute-start(bf16[256,1024]{1,0:T(8,128)(2,1)} %get-tuple-element.172), channel_id=1, source_target_pairs={{0,0},{8,1},{16,2},{24,3},{4,4},{12,5},{20,6},{28,7},{1,8},{9,9},{... | collective-permute-start | bytes 1572872 | tf_op jit(solution)/shard_map/ppermute | solution.py:1193
  677.6 26.3 %collective-permute-start.96 = (bf16[64,2048]{1,0:T(8,128)(2,1)S(1)}, bf16[64,2048]{1,0:T(8,128)(2,1)S(1)}, u32[]{:S(2)}, u32[]{:S(2)}) collective-permute-start(bf16[64,2048]{1,0:T(8,128)(2,1)S(1)} %copy-done.86), channel_id=1, source_target_pairs={{0,1},{1,0},{2,3},{3,2},{4,5},{5,4},{6,7},{7,6},{8,9},{9,8},{10,11... | collective-permute-start | bytes 786440 | tf_op jit(solution)/shard_map/ppermute | solution.py:78
  677.7 26.2 %collective-permute-start.97 = (bf16[64,2048]{1,0:T(8,128)(2,1)S(1)}, bf16[64,2048]{1,0:T(8,128)(2,1)S(1)}, u32[]{:S(2)}, u32[]{:S(2)}) collective-permute-start(bf16[64,2048]{1,0:T(8,128)(2,1)S(1)} %copy-done.85), channel_id=1, source_target_pairs={{0,3},{1,2},{2,1},{3,0},{4,7},{5,6},{6,5},{7,4},{8,11},{9,10},{10,... | collective-permute-start | bytes 786440 | tf_op jit(solution)/shard_map/ppermute | solution.py:78
  (148 other events, 1276.2 us)
Sparse Core Ops, SparseCore 0:
  130.6 44.0 all-gather.1
  431.7 45.9 reduce-scatter.1
